TPU v7x, 32 devices: a whole 2x2x4 slice. The times are simulated.
32 devices in a mesh: rows: 8 (over z, x), grp: 4 (over y, core).
Axes of the slice: x: 2, y: 2, z: 4, core: 2. Of those that a mesh axis runs over, the one named last changes fastest.
Arguments:
- vectors: bfloat16 [64, 131072], P(None, 'rows'), may hold values from -6 to 6
- wear_freq: bfloat16 [131072], P('rows'), may hold values from 0 to 400
- param_scale: bfloat16 [131072], P('rows'), may hold values from 0.29882812 to 3
- row_angle: bfloat16 [32768], P(('rows', 'grp')), may hold values from -3.140625 to 3.140625
- row_weight: bfloat16 [32768], P(('rows', 'grp')), may hold values from 0.29882812 to 3
- entry_block: int32 [4096], P(('rows', 'grp')), may hold values from 0 to 255, as said below
- entry_row: int32 [4096], P(('rows', 'grp')), may hold values from 0 to 3
- entry_count: int32 [32], P(('rows', 'grp')), may hold values from 16 to 128, as said below
- block_home: int32 [256], replicated, may hold values from 0 to 255, as said below
Outputs:
- product: float32 [64, 131072], P(None, 'rows')
Inputs may be any that keep to these rules, and one draw needn't show every extreme that they name: block_home is a permutation of the 256 parameter blocks. Among the live entries of one group at most 16 have block_home[entry_block] // 32 equal to any one value; a group with 128 live entries reaches 16 for every value. `entry_count`: in every draw some group has 128 live entries.
All inputs are finite; a program needn't handle non-finite values.
Results may differ from a plain program's by a relative error of at most 0.0036.
Values may be sent and summed in bfloat16 or wider, within the bound.
No kernel may reach another device: no remote copies, remote signals or barrier semaphores. Data moves between devices by JAX's collectives and lax.ppermute only.
A program may use at most 128 MiB of HBM per device.

v0:
```python
import functools
import math

import jax
import jax.numpy as jnp
from jax import lax
from jax.experimental import pallas as pl
from jax.experimental.pallas import tpu as pltpu
from jax.sharding import PartitionSpec as P

BLK_R = 256
BLK_P = 512
PIECES = 8
RING = 8
VMEM_LIMIT = 40 << 20

f32 = jnp.float32
bf16 = jnp.bfloat16

COS_POLY = (
    1.4142134965678816,
    -6.978850988354285,
    5.7394611717976565,
    -1.8835629903409246,
    0.3106981920279389,
)
ROUNDER = 12582912.0


def turn_constants():
    constants = []
    rest = 1.0 / (2.0 * math.pi)
    for _ in range(3):
        mantissa, exponent = math.frexp(rest)
        constant = math.ldexp(round(mantissa * 256.0) / 256.0, exponent)
        constants.append(constant)
        rest -= constant
    return constants


def angle_pieces(angles):
    out = []
    for constant in turn_constants():
        exact = angles * constant
        top = lax.reduce_precision(exact, 8, 7)
        out += [top, exact - top]
    return out


def collect(codes, todo, wanted=None):
    def visit(place, found):
        todo[found] = place
        code = codes[place]
        take = code >= 0
        if wanted is not None:
            take = take & wanted(code)
        return found + take.astype(jnp.int32)

    return lax.fori_loop(0, codes.shape[0], visit, 0)


def forward_kernel(
    blocks, capacity, codes, left, right, turned, part, jac, todo, even, odd, sems
):
    spare = codes.shape[0]
    part[...] = jnp.zeros_like(part)
    found = collect(codes, todo)
    steps = (found + 1) // 2

    def decode(place):
        code = codes[place]
        return lax.rem(code, blocks), lax.div(code, blocks), lax.div(place, capacity)

    def make(buffer, place):
        block, row, group = decode(place)
        angles = left[group, :, pl.ds(pl.multiple_of(row * BLK_R, BLK_R), BLK_R)]
        both = lax.dot_general(
            angles, right[block], (((0,), (0,)), ((), ())), preferred_element_type=f32
        )
        turns, weight = both[:, :BLK_P], both[:, BLK_P:]
        rest = turns - ((turns + ROUNDER) - ROUNDER)
        square = rest * rest
        root = COS_POLY[4] * square + COS_POLY[3]
        for k in (2, 1, 0):
            root = root * square + COS_POLY[k]
        buffer[...] = (weight * (root * root - 1.0)).astype(bf16)

    def apply(buffer, place, keep):
        block, row, group = decode(place)
        chosen = turned[pl.ds(pl.multiple_of(block * BLK_P, BLK_P), BLK_P), :]
        term = jnp.dot(buffer[...], chosen, preferred_element_type=f32)
        if keep is not None:
            term = jnp.where(keep, term, 0.0)
        part[group, :, pl.ds(pl.multiple_of(row * BLK_R, BLK_R), BLK_R)] += term.T

    def save(buffer, parity, which, place):
        return pltpu.make_async_copy(buffer.at[parity], jac.at[place], sems.at[parity, which])

    def step(turn, before):
        parity = lax.rem(turn, 2)
        first = todo[2 * turn]
        paired = 2 * turn + 1 < found
        second = todo[jnp.where(paired, 2 * turn + 1, 2 * turn)]

        @pl.when(turn >= 2)
        def _():
            save(even, parity, 0, 0).wait()
            save(odd, parity, 1, 0).wait()

        apply(odd.at[1 - parity], before, turn > 0)
        make(even.at[parity], first)
        save(even, parity, 0, first).start()
        apply(even.at[parity], first, None)
        make(odd.at[parity], second)
        save(odd, parity, 1, jnp.where(paired, second, spare)).start()
        return second

    last = lax.fori_loop(0, steps, step, 0)

    @pl.when((found > 0) & (lax.rem(found, 2) == 0))
    def _():
        apply(odd.at[lax.rem(steps + 1, 2)], last, None)

    for back in (1, 2):
        @pl.when(steps >= back)
        def _():
            parity = lax.rem(steps + back, 2)
            save(even, parity, 0, 0).wait()
            save(odd, parity, 1, 0).wait()


def forward(codes, left, right, turned, capacity):
    groups, _, width = left.shape
    blocks = right.shape[0]
    room = codes.shape[0]
    vector_count = turned.shape[1]
    vmem = pl.BlockSpec(memory_space=pltpu.VMEM)
    return pl.pallas_call(
        functools.partial(forward_kernel, blocks, capacity),
        out_shape=(
            jax.ShapeDtypeStruct((groups, vector_count, width), f32),
            jax.ShapeDtypeStruct((room + 1, BLK_R, BLK_P), bf16),
        ),
        in_specs=[pl.BlockSpec(memory_space=pltpu.SMEM), vmem, vmem, vmem],
        out_specs=(vmem, pl.BlockSpec(memory_space=pl.ANY)),
        scratch_shapes=[
            pltpu.SMEM((room + 1,), jnp.int32),
            pltpu.VMEM((2, BLK_R, BLK_P), bf16),
            pltpu.VMEM((2, BLK_R, BLK_P), bf16),
            pltpu.SemaphoreType.DMA((2, 2)),
        ],
        compiler_params=pltpu.CompilerParams(vmem_limit_bytes=VMEM_LIMIT),
        name="forward",
    )(codes, left, right, turned)


def backward_kernel(blocks, capacity, codes, half, gathered, jac, out, todo, ring, sems):
    per_half = blocks // 2
    depth = ring.shape[0]
    found = collect(codes, todo, lambda code: lax.div(lax.rem(code, blocks), per_half) == half[0])

    def load(turn):
        slot = lax.rem(turn, depth)
        return pltpu.make_async_copy(jac.at[todo[turn]], ring.at[slot], sems.at[slot])

    def prime(turn, carry):
        load(turn).start()
        return carry

    lax.fori_loop(0, jnp.minimum(found, depth - 1), prime, 0)
    out[...] = jnp.zeros_like(out)

    def step(turn, carry):
        @pl.when(turn + depth - 1 < found)
        def _():
            load(turn + depth - 1).start()

        place = todo[turn]
        code = codes[place]
        block, row = lax.rem(lax.rem(code, blocks), per_half), lax.div(code, blocks)
        group = lax.div(place, capacity)
        chosen = gathered[group, :, pl.ds(pl.multiple_of(row * BLK_R, BLK_R), BLK_R)]
        at = pl.ds(pl.multiple_of(block * BLK_P, BLK_P), BLK_P)
        load(turn).wait()
        out[:, at] += jnp.dot(chosen, ring[lax.rem(turn, depth)], preferred_element_type=f32)
        return carry

    lax.fori_loop(0, found, step, 0)


def backward(codes, half, gathered, jac, blocks, capacity):
    smem = pl.BlockSpec(memory_space=pltpu.SMEM)
    vmem = pl.BlockSpec(memory_space=pltpu.VMEM)
    return pl.pallas_call(
        functools.partial(backward_kernel, blocks, capacity),
        out_shape=jax.ShapeDtypeStruct((gathered.shape[1], blocks // 2 * BLK_P), f32),
        in_specs=[smem, smem, vmem, pl.BlockSpec(memory_space=pl.ANY)],
        out_specs=vmem,
        scratch_shapes=[
            pltpu.SMEM((codes.shape[0] + 1,), jnp.int32),
            pltpu.VMEM((RING, BLK_R, BLK_P), bf16),
            pltpu.SemaphoreType.DMA((RING,)),
        ],
        compiler_params=pltpu.CompilerParams(vmem_limit_bytes=VMEM_LIMIT),
        name="backward",
    )(codes, half, gathered, jac)


def swap(array, axis, bit):
    return lax.ppermute(array, axis, [(i, i ^ bit) for i in range(lax.axis_size(axis))])


def body(
    vectors,
    wear_freq,
    param_scale,
    row_angle,
    row_weight,
    entry_block,
    entry_row,
    entry_count,
    block_home,
):
    holders = lax.axis_size("rows")
    members = lax.axis_size("grp")
    vector_count = vectors.shape[0]
    blocks_here = vectors.shape[1] // BLK_P
    slots = entry_block.shape[0]
    capacity = slots // holders
    width = row_angle.shape[0]

    names = jnp.arange(block_home.shape[0], dtype=jnp.int32)
    stored = jnp.sum(
        jnp.where(entry_block[:, None] == names[None, :], block_home[None, :], 0), axis=1
    )
    slot_ids = jnp.arange(slots, dtype=jnp.int32)
    live = slot_ids < entry_count[0]
    holder = jnp.where(live, stored // blocks_here, -1)
    earlier = (holder[:, None] == holder[None, :]) & (slot_ids[None, :] < slot_ids[:, None])
    places = jnp.sum(earlier.astype(jnp.int32), axis=1)
    code = entry_row * blocks_here + stored % blocks_here
    target = jnp.where(live, holder * capacity + places, -1)
    room_ids = jnp.arange(holders * capacity, dtype=jnp.int32)
    wanted = (
        jnp.sum(jnp.where(target[None, :] == room_ids[:, None], code[None, :] + 1, 0), axis=1) - 1
    )
    wanted = wanted.reshape(holders, 1, capacity).astype(f32)

    angle_rows = jnp.stack(
        angle_pieces(row_angle.astype(f32)) + [row_weight.astype(f32)], axis=0
    )
    send = jnp.concatenate(
        [
            jnp.broadcast_to(angle_rows[None], (holders, PIECES - 1, width)),
            jnp.pad(wanted, ((0, 0), (0, 0), (0, width - capacity))),
        ],
        axis=1,
    ).astype(bf16)
    left = lax.all_to_all(send, "rows", split_axis=0, concat_axis=0, tiled=True)
    codes = left[:, PIECES - 1, :capacity].astype(jnp.int32).reshape(holders * capacity)

    freq = wear_freq.reshape(blocks_here, 1, BLK_P)
    scale = (param_scale.astype(f32) * (1.0 / math.sqrt(8.0 * BLK_P))).astype(bf16)
    scale = scale.reshape(blocks_here, 1, BLK_P)
    kind = lax.broadcasted_iota(jnp.int32, (1, PIECES, 1), 1)
    right = jnp.concatenate(
        [
            jnp.where(kind < PIECES - 2, freq, jnp.zeros_like(freq)),
            jnp.where(kind == PIECES - 2, scale, jnp.zeros_like(scale)),
        ],
        axis=2,
    )
    part, jac = forward(codes, left, right, vectors.T, capacity)

    pieces = lax.all_to_all(part, "rows", split_axis=0, concat_axis=0, tiled=True)
    outputs = jnp.sum(pieces, axis=0).astype(bf16)
    gathered = lax.all_gather(outputs, "rows")

    core = lax.axis_index("grp") % 2
    give = backward(codes, (1 - core).reshape(1), gathered, jac, blocks_here, capacity)
    got = swap(give, "grp", 1)
    keep = backward(codes, core.reshape(1), gathered, jac, blocks_here, capacity)
    half_sum = keep + got
    bit = 2
    while bit < members:
        rounded = lax.reduce_precision(half_sum, 8, 7)
        half_sum = rounded + swap(rounded.astype(bf16), "grp", bit).astype(f32)
        bit *= 2
    other = swap(half_sum, "grp", 1)
    first = core == 0
    return jnp.concatenate(
        [jnp.where(first, half_sum, other), jnp.where(first, other, half_sum)], axis=1
    )


def solution(mesh):
    return jax.shard_map(
        body,
        mesh=mesh,
        in_specs=(
            P(None, "rows"),
            P("rows"),
            P("rows"),
            P(("rows", "grp")),
            P(("rows", "grp")),
            P(("rows", "grp")),
            P(("rows", "grp")),
            P(("rows", "grp")),
            P(),
        ),
        out_specs=P(None, "rows"),
        check_vma=False,
    )
```

profile of v0, /device:TPU:0, one launch (start us, length us, event | category | flops | bytes accessed | tf_op | source)
XLA Modules:
  0.0 211.1 jit_solution(6973683317154458477)
XLA Ops:
  7.2 0.9 select_reduce_fusion
  8.0 0.7 compare_select_fusion.4
  8.7 0.2 convert_reduce_fusion
  8.9 0.1 select_reduce_fusion.1
  9.0 0.1 convert_element_type.69
  9.1 0.7 fusion.8
  9.8 0.7 stack.36
  10.5 0.1 stack.35
  10.6 0.7 fusion.2
  11.3 7.3 %all-to-all-start = ((bf16[8,8,1024]{2,1,0:T(8,128)(2,1)}), bf16[8,8,1024]{2,1,0:T(8,128)(2,1)S(1)}, u32[]{:S(2)}, u32[]{:S(2)}) async-start(bf16[8,8,1024]{2,1,0:T(8,128)(2,1)} %fusion.2), calls=%async_computation | async-start | bytes 262144 | tf_op jit(solution)/shard_map/all_to_all | solution.py:259
  18.5 0.0 all-gather.3.cloned.1.call-start
  18.6 0.8 multiply_convert_fusion
  19.4 0.8 broadcast_in_dim.90
  20.2 0.1 broadcast_select_fusion.2
  20.3 4.8 %copy.13 = bf16[64,16384]{0,1:T(8,128)(2,1)} copy(bf16[64,16384]{1,0:T(8,128)(2,1)} %param.9) | data formatting | bytes 4194304 | tf_op args[0]
  25.0 0.1 pad_maximum_fusion.1.right
  25.1 0.7 all-to-all-done.left
  25.9 0.1 reshape.114.codes
  26.0 0.0 copy-start
  26.0 2.2 %copy-done = bf16[64,16384]{0,1:T(8,128)(2,1)S(1)} copy-done((bf16[64,16384]{0,1:T(8,128)(2,1)S(1)}, bf16[64,16384]{0,1:T(8,128)(2,1)}, u32[]{:S(2)}) %copy-start) | copy-done | bytes 2097176
  28.1 33.9 %forward.1 = (f32[8,64,1024]{2,1,0:T(8,128)S(1)}, bf16[129,256,512]{2,1,0:T(8,128)(2,1)}) custom-call(s32[128]{0:T(128)S(1)} %reshape.114.codes, bf16[8,8,1024]{2,1,0:T(8,128)(2,1)S(1)} %all-to-all-done.left, bf16[32,8,1024]{2,1,0:T(8,128)(2,1)S(1)} %pad_maximum_fusion.1.right, bf16[16384,64]{1,0:T(8,128)(2,1)S(1)} %bitcast.14), custom_call_target="tpu_custom_call" | custom-call | tf_op jit(solution)/shard_map/forward/pallas_call | solution.py:138
  62.0 47.2 %all_to_all.10 = f32[8,64,1024]{2,1,0:T(8,128)S(1)} all-to-all(f32[8,64,1024]{2,1,0:T(8,128)S(1)} %get-tuple-element.7), channel_id=1, replica_groups=mesh['rows'=8,'grp'=4] {'rows'}, dimensions={0} | all-to-all | bytes 4194304 | tf_op jit(solution)/shard_map/all_to_all | solution.py:275
  109.2 0.8 reduce_sum.39
  110.0 0.0 all-gather.3.cloned.1.call-update
  110.0 40.2 %all-gather.3.cloned.1.call-done = bf16[512,1024]{1,0:T(8,128)(2,1)} async-done(((bf16[64,1024]{1,0:T(8,128)(2,1)}), bf16[512,1024]{1,0:T(8,128)(2,1)}) %all-gather.3.cloned.1.call-update) | async-done | bytes 1048592 | tf_op jit(solution)/shard_map/all_gather | solution.py:277
  150.2 0.0 copy-start.1
  150.2 1.2 copy-done.1
  151.5 0.0 copy-start.2
  151.5 10.2 %backward.3 = f32[64,8192]{1,0:T(8,128)S(1)} custom-call(s32[128]{0:T(128)S(1)} %reshape.114.codes, s32[1]{0:T(128)} %bitcast.11.half, bf16[8,64,1024]{2,1,0:T(8,128)(2,1)S(1)} %bitcast.15, bf16[129,256,512]{2,1,0:T(8,128)(2,1)} %get-tuple-element.8.jac), custom_call_target="tpu_custom_call" | custom-call | tf_op jit(solution)/shard_map/backward/pallas_call | solution.py:194
  161.6 0.1 collective-permute-start
  161.7 0.0 copy-done.2
  161.7 8.2 %backward.2 = f32[64,8192]{1,0:T(8,128)S(1)} custom-call(s32[128]{0:T(128)S(1)} %reshape.114.codes, s32[1]{0:T(128)} %bitcast.8.half, bf16[8,64,1024]{2,1,0:T(8,128)(2,1)S(1)} %bitcast.16, bf16[129,256,512]{2,1,0:T(8,128)(2,1)} %get-tuple-element.8.jac), custom_call_target="tpu_custom_call" | custom-call | tf_op jit(solution)/shard_map/backward/pallas_call | solution.py:194
  169.9 0.0 collective-permute-done
  169.9 0.2 fusion
  170.1 1.9 collective-permute-start.1
  172.0 23.4 %collective-permute-done.1 = bf16[64,8192]{1,0:T(8,128)(2,1)S(1)} collective-permute-done((bf16[64,8192]{1,0:T(8,128)(2,1)S(1)}, bf16[64,8192]{1,0:T(8,128)(2,1)S(1)}, u32[]{:S(2)}, u32[]{:S(2)}) %collective-permute-start.1) | collective-permute-done | bytes 1048608 | tf_op jit(solution)/shard_map/ppermute | solution.py:210
  195.4 0.3 convert_add_fusion
  195.7 0.1 collective-permute-start.2
  195.7 4.3 %collective-permute-done.2 = f32[64,8192]{1,0:T(8,128)} collective-permute-done((f32[64,8192]{1,0:T(8,128)S(1)}, f32[64,8192]{1,0:T(8,128)}, u32[]{:S(2)}, u32[]{:S(2)}) %collective-permute-start.2) | collective-permute-done | bytes 2097184 | tf_op jit(solution)/shard_map/ppermute | solution.py:210
  200.0 1.9 broadcast_select_fusion.1
  202.0 2.3 %pad_maximum_fusion = f32[64,16384]{1,0:T(8,128)} fusion(f32[64,8192]{1,0:T(8,128)S(1)} %get-tuple-element.10, f32[64,8192]{1,0:T(8,128)S(1)} %get-tuple-element.9), kind=kLoop, calls=%fused_computation | loop fusion | flops 1048576 | bytes 8388608 | tf_op jit(solution)/shard_map/concatenate | solution.py:291
  (7 shorter events, 0.1 us)
Async XLA Ops:
  11.3 14.6 %all-to-all-start = ((bf16[8,8,1024]{2,1,0:T(8,128)(2,1)}), bf16[8,8,1024]{2,1,0:T(8,128)(2,1)S(1)}, u32[]{:S(2)}, u32[]{:S(2)}) async-start(bf16[8,8,1024]{2,1,0:T(8,128)(2,1)} %fusion.2), calls=%async_computation | async-start | bytes 262144 | tf_op jit(solution)/shard_map/all_to_all | solution.py:259
  18.5 131.7 %all-gather.3.cloned.1.call-start = ((), (), s32[]{:S(2)}) async-start(), calls=%async_computation.2 | async-start | bytes 1179648 | tf_op jit(solution)/shard_map/all_gather | solution.py:277
  26.0 2.2 %copy-start = (bf16[64,16384]{0,1:T(8,128)(2,1)S(1)}, bf16[64,16384]{0,1:T(8,128)(2,1)}, u32[]{:S(2)}) copy-start(bf16[64,16384]{0,1:T(8,128)(2,1)} %copy.13) | copy-start | bytes 6291460
  150.2 1.2 copy-start.1
  151.5 10.2 %copy-start.2 = (bf16[512,1024]{1,0:T(8,128)(2,1)S(1)}, bf16[512,1024]{1,0:T(8,128)(2,1)}, u32[]{:S(2)}) copy-start(bf16[512,1024]{1,0:T(8,128)(2,1)} %all-gather.3.cloned.1.call-done) | copy-start | bytes 3145732
  161.6 8.3 %collective-permute-start = (f32[64,8192]{1,0:T(8,128)S(1)}, f32[64,8192]{1,0:T(8,128)S(1)}, u32[]{:S(2)}, u32[]{:S(2)}) collective-permute-start(f32[64,8192]{1,0:T(8,128)S(1)} %backward.3), channel_id=1, source_target_pairs={{0,1},{1,0},{2,3},{3,2},{4,5},{5,4},{6,7},{7,6},{8,9},{9,8},{10,11... | collective-permute-start | bytes 6291464 | tf_op jit(solution)/shard_map/ppermute | solution.py:210
  170.1 25.3 %collective-permute-start.1 = (bf16[64,8192]{1,0:T(8,128)(2,1)S(1)}, bf16[64,8192]{1,0:T(8,128)(2,1)S(1)}, u32[]{:S(2)}, u32[]{:S(2)}) collective-permute-start(bf16[64,8192]{1,0:T(8,128)(2,1)S(1)} %fusion), channel_id=1, source_target_pairs={{0,2},{1,3},{2,0},{3,1},{4,6},{5,7},{6,4},{7,5},{8,10},{9,11},{10,... | collective-permute-start | bytes 3145736 | tf_op jit(solution)/shard_map/ppermute | solution.py:210
  195.7 4.4 %collective-permute-start.2 = (f32[64,8192]{1,0:T(8,128)S(1)}, f32[64,8192]{1,0:T(8,128)}, u32[]{:S(2)}, u32[]{:S(2)}) collective-permute-start(f32[64,8192]{1,0:T(8,128)S(1)} %convert_add_fusion), channel_id=1, source_target_pairs={{0,1},{1,0},{2,3},{3,2},{4,5},{5,4},{6,7},{7,6},{8,9},{9,8},{10,11... | collective-permute-start | bytes 6291464 | tf_op jit(solution)/shard_map/ppermute | solution.py:210
Sparse Core Ops, SparseCore 0:
  110.1 40.0 all-gather.2
where the time goes:
time: 212 us; the launch traced here: 211 us
  waiting for transfers between devices  68.6 us (32%)
  Pallas kernels  52.2 us (25%)
  blocking collectives  47.2 us (22%)
  between operations  14.2 us (7%)
  other arithmetic  10.4 us (5%)
  starting transfers between devices  9.33 us (4%)
  local copies, waits for them, and re-layouts  9.23 us (4%)
    all_to_all x1, blocking collectives, body(): lax.all_to_all(part, 'rows', split_axis=0, concat_axis=0, tiled=True)  47.2 us
    all_gather x1, waiting for transfers between devices, body(): gathered = lax.all_gather(outputs, 'rows')  40.2 us
    pallas_call x1, Pallas kernels, forward(): pl.pallas_call(functools.partial(forward_kernel, blocks, capacity), out_s...  33.9 us
    ppermute x3, waiting for transfers between devices, swap(): lax.ppermute(array, axis, [(i, i ^ bit) for i in range(lax.axis_size(axis...  27.6 us
    pallas_call x2, Pallas kernels, backward(): pl.pallas_call(functools.partial(backward_kernel, blocks, capacity), out_...  18.3 us
    unnamed x7, local copies, waits for them, and re-layouts  8.17 us
    all_to_all x1, starting transfers between devices, body(): left = lax.all_to_all(send, 'rows', split_axis=0, concat_axis=0, tiled=True)  7.25 us
  transfers between devices with their start and end apart: 5, of which 4 were waited for; matrix products, arithmetic and copies ran while one was open for 3% of the time, Pallas kernels for 4%

commit v1 on v0

--- a/solution.py
+++ b/solution.py
@@ -12,7 +12,7 @@
 BLK_P = 512
 PIECES = 8
 RING = 8
-VMEM_LIMIT = 40 << 20
+VMEM_BASE = 12 << 20
 
 f32 = jnp.float32
 bf16 = jnp.bfloat16
@@ -47,32 +47,49 @@
     return out
 
 
-def collect(codes, todo, wanted=None):
+def collect(codes, todo, wanted):
     def visit(place, found):
         todo[found] = place
         code = codes[place]
-        take = code >= 0
-        if wanted is not None:
-            take = take & wanted(code)
-        return found + take.astype(jnp.int32)
+        return found + ((code >= 0) & wanted(place, code)).astype(jnp.int32)
 
     return lax.fori_loop(0, codes.shape[0], visit, 0)
 
 
+def entry_cost(entries, vector_count):
+    return pl.CostEstimate(flops=entries, bytes_accessed=vector_count, transcendentals=0)
+
+
 def forward_kernel(
-    blocks, capacity, codes, left, right, turned, part, jac, todo, even, odd, sems
+    blocks,
+    capacity,
+    ring,
+    splits,
+    codes,
+    where,
+    left,
+    right,
+    vectors,
+    *refs,
 ):
+    *parts, jac, todo, part, even, odd, sems = refs
     spare = codes.shape[0]
     part[...] = jnp.zeros_like(part)
-    found = collect(codes, todo)
+
+    def wanted(place, code):
+        return lax.rem(lax.div(place, capacity), 2) == where[1]
+
+    found = collect(codes, todo, wanted)
     steps = (found + 1) // 2
 
     def decode(place):
         code = codes[place]
-        return lax.rem(code, blocks), lax.div(code, blocks), lax.div(place, capacity)
+        position = lax.div(place, 2 * capacity)
+        behind = lax.rem(where[0] - 1 - position + 2 * ring, ring)
+        return lax.rem(code, blocks), lax.div(code, blocks), lax.div(place, capacity), behind
 
     def make(buffer, place):
-        block, row, group = decode(place)
+        block, row, group, _ = decode(place)
         angles = left[group, :, pl.ds(pl.multiple_of(row * BLK_R, BLK_R), BLK_R)]
         both = lax.dot_general(
             angles, right[block], (((0,), (0,)), ((), ())), preferred_element_type=f32
@@ -86,12 +103,14 @@
         buffer[...] = (weight * (root * root - 1.0)).astype(bf16)
 
     def apply(buffer, place, keep):
-        block, row, group = decode(place)
-        chosen = turned[pl.ds(pl.multiple_of(block * BLK_P, BLK_P), BLK_P), :]
-        term = jnp.dot(buffer[...], chosen, preferred_element_type=f32)
+        block, row, _, behind = decode(place)
+        chosen = vectors[:, pl.ds(pl.multiple_of(block * BLK_P, BLK_P), BLK_P)]
+        term = lax.dot_general(
+            buffer[...], chosen, (((1,), (1,)), ((), ())), preferred_element_type=f32
+        )
         if keep is not None:
             term = jnp.where(keep, term, 0.0)
-        part[group, :, pl.ds(pl.multiple_of(row * BLK_R, BLK_R), BLK_R)] += term.T
+        part[behind, :, pl.ds(pl.multiple_of(row * BLK_R, BLK_R), BLK_R)] += term.T
 
     def save(buffer, parity, which, place):
         return pltpu.make_async_copy(buffer.at[parity], jac.at[place], sems.at[parity, which])
@@ -128,86 +147,167 @@
             save(even, parity, 0, 0).wait()
             save(odd, parity, 1, 0).wait()
 
-
-def forward(codes, left, right, turned, capacity):
+    each = ring // splits
+    for k in range(splits):
+        parts[k][...] = part[k * each : (k + 1) * each]
+
+
+def forward(codes, where, left, right, vectors, capacity, splits):
     groups, _, width = left.shape
+    ring = groups // 2
     blocks = right.shape[0]
     room = codes.shape[0]
-    vector_count = turned.shape[1]
+    count = vectors.shape[0]
     vmem = pl.BlockSpec(memory_space=pltpu.VMEM)
+    smem = pl.BlockSpec(memory_space=pltpu.SMEM)
     return pl.pallas_call(
-        functools.partial(forward_kernel, blocks, capacity),
-        out_shape=(
-            jax.ShapeDtypeStruct((groups, vector_count, width), f32),
-            jax.ShapeDtypeStruct((room + 1, BLK_R, BLK_P), bf16),
-        ),
-        in_specs=[pl.BlockSpec(memory_space=pltpu.SMEM), vmem, vmem, vmem],
-        out_specs=(vmem, pl.BlockSpec(memory_space=pl.ANY)),
+        functools.partial(forward_kernel, blocks, capacity, ring, splits),
+        out_shape=(jax.ShapeDtypeStruct((ring // splits, count, width), f32),) * splits
+        + (pltpu.HBM((room + 1, BLK_R, BLK_P), bf16),),
+        in_specs=[smem, smem, vmem, vmem, vmem],
+        out_specs=(vmem,) * splits + (pl.BlockSpec(memory_space=pltpu.HBM),),
         scratch_shapes=[
             pltpu.SMEM((room + 1,), jnp.int32),
+            pltpu.VMEM((ring, count, width), f32),
             pltpu.VMEM((2, BLK_R, BLK_P), bf16),
             pltpu.VMEM((2, BLK_R, BLK_P), bf16),
             pltpu.SemaphoreType.DMA((2, 2)),
         ],
-        compiler_params=pltpu.CompilerParams(vmem_limit_bytes=VMEM_LIMIT),
+        compiler_params=pltpu.CompilerParams(
+            vmem_limit_bytes=VMEM_BASE + 12 * ring * count * width
+        ),
+        cost_estimate=entry_cost(room // 4, count),
         name="forward",
-    )(codes, left, right, turned)
-
-
-def backward_kernel(blocks, capacity, codes, half, gathered, jac, out, todo, ring, sems):
-    per_half = blocks // 2
-    depth = ring.shape[0]
-    found = collect(codes, todo, lambda code: lax.div(lax.rem(code, blocks), per_half) == half[0])
-
-    def load(turn):
+    )(codes, where, left, right, vectors)
+
+
+def backward_kernel(blocks, capacity, ring, codes, where, near_jac, far_jac, *refs):
+    *pieces, out, gathered, todo, buffers, sems = refs
+    here = out.shape[1] // BLK_P
+    depth = buffers.shape[0]
+
+    def wanted(place, code):
+        block = lax.rem(code, blocks)
+        return (block >= where[2]) & (block < where[2] + here)
+
+    found = collect(codes, todo, wanted)
+
+    def is_near(place):
+        return lax.rem(lax.div(place, capacity), 2) == where[1]
+
+    def start(turn):
         slot = lax.rem(turn, depth)
-        return pltpu.make_async_copy(jac.at[todo[turn]], ring.at[slot], sems.at[slot])
+        place = todo[turn]
+
+        @pl.when(is_near(place))
+        def _():
+            pltpu.make_async_copy(near_jac.at[place], buffers.at[slot], sems.at[slot]).start()
+
+        @pl.when(~is_near(place))
+        def _():
+            pltpu.make_async_copy(far_jac.at[place], buffers.at[slot], sems.at[slot]).start()
 
     def prime(turn, carry):
-        load(turn).start()
+        start(turn)
         return carry
 
     lax.fori_loop(0, jnp.minimum(found, depth - 1), prime, 0)
+    for k in range(len(pieces)):
+        gathered[k] = pieces[k][...]
     out[...] = jnp.zeros_like(out)
 
     def step(turn, carry):
         @pl.when(turn + depth - 1 < found)
         def _():
-            load(turn + depth - 1).start()
+            start(turn + depth - 1)
 
         place = todo[turn]
         code = codes[place]
-        block, row = lax.rem(lax.rem(code, blocks), per_half), lax.div(code, blocks)
-        group = lax.div(place, capacity)
-        chosen = gathered[group, :, pl.ds(pl.multiple_of(row * BLK_R, BLK_R), BLK_R)]
+        block, row = lax.rem(code, blocks) - where[2], lax.div(code, blocks)
+        behind = lax.rem(where[0] - lax.div(place, 2 * capacity) + ring, ring)
+        piece = jnp.where(is_near(place), behind, ring + behind)
+        chosen = gathered[piece, :, pl.ds(pl.multiple_of(row * BLK_R, BLK_R), BLK_R)]
         at = pl.ds(pl.multiple_of(block * BLK_P, BLK_P), BLK_P)
-        load(turn).wait()
-        out[:, at] += jnp.dot(chosen, ring[lax.rem(turn, depth)], preferred_element_type=f32)
+        slot = lax.rem(turn, depth)
+        pltpu.make_async_copy(near_jac.at[0], buffers.at[slot], sems.at[slot]).wait()
+        out[:, at] += jnp.dot(chosen, buffers[slot], preferred_element_type=f32)
         return carry
 
     lax.fori_loop(0, found, step, 0)
 
 
-def backward(codes, half, gathered, jac, blocks, capacity):
+def joined_backward_kernel(blocks, capacity, ring, *refs):
+    *inputs, gathered, out, todo, buffers, sems = refs
+    backward_kernel(blocks, capacity, ring, *inputs, out, gathered, todo, buffers, sems)
+
+
+def backward(codes, where, near_jac, far_jac, pieces, blocks, here, capacity):
+    joined = not isinstance(pieces, list)
     smem = pl.BlockSpec(memory_space=pltpu.SMEM)
     vmem = pl.BlockSpec(memory_space=pltpu.VMEM)
-    return pl.pallas_call(
-        functools.partial(backward_kernel, blocks, capacity),
-        out_shape=jax.ShapeDtypeStruct((gathered.shape[1], blocks // 2 * BLK_P), f32),
-        in_specs=[smem, smem, vmem, pl.BlockSpec(memory_space=pl.ANY)],
-        out_specs=vmem,
+    hbm = pl.BlockSpec(memory_space=pl.ANY)
+    sources = [pieces] if joined else pieces
+    count, width = sources[0].shape[-2:]
+    total = pieces.shape[0] if joined else len(pieces)
+    terms = jax.ShapeDtypeStruct((count, here * BLK_P), f32)
+    gathered = jax.ShapeDtypeStruct((total, count, width), bf16)
+    kernel = joined_backward_kernel if joined else backward_kernel
+    result = pl.pallas_call(
+        functools.partial(kernel, blocks, capacity, total // 2),
+        out_shape=terms if joined else (terms, gathered),
+        in_specs=[smem, smem, hbm, hbm] + [vmem] * len(sources),
+        out_specs=vmem if joined else (vmem, vmem),
         scratch_shapes=[
             pltpu.SMEM((codes.shape[0] + 1,), jnp.int32),
             pltpu.VMEM((RING, BLK_R, BLK_P), bf16),
             pltpu.SemaphoreType.DMA((RING,)),
         ],
-        compiler_params=pltpu.CompilerParams(vmem_limit_bytes=VMEM_LIMIT),
+        compiler_params=pltpu.CompilerParams(vmem_limit_bytes=36 << 20),
+        cost_estimate=entry_cost(codes.shape[0] // 8, count),
         name="backward",
-    )(codes, half, gathered, jac)
+    )(codes, where, near_jac, far_jac, *sources)
+    return (result, pieces) if joined else result
+
+
+def place_kernel(quarters, where, *refs):
+    *sources, out, sems = refs
+    sources = sources[-len(quarters) :]
+    wide = sources[0].shape[1]
+    copies = []
+    for k, (mine, chunk) in enumerate(quarters):
+        half = where[0] if mine else 1 - where[0]
+        at = pl.ds(pl.multiple_of((2 * half + chunk) * wide, wide), wide)
+        copies.append(pltpu.make_async_copy(sources[k], out.at[:, at], sems.at[k]))
+    for copy in copies:
+        copy.start()
+    for copy in copies:
+        copy.wait()
+
+
+def place(where, into, quarters, sources):
+    hbm = pl.BlockSpec(memory_space=pl.ANY)
+    vmem = pl.BlockSpec(memory_space=pltpu.VMEM)
+    count, wide = sources[0].shape
+    held = [] if into is None else [into]
+    return pl.pallas_call(
+        functools.partial(place_kernel, quarters),
+        out_shape=jax.ShapeDtypeStruct((count, 4 * wide), f32),
+        in_specs=[pl.BlockSpec(memory_space=pltpu.SMEM)] + [hbm] * len(held) + [vmem] * len(sources),
+        out_specs=hbm,
+        scratch_shapes=[pltpu.SemaphoreType.DMA((len(quarters),))],
+        input_output_aliases={1: 0} if held else {},
+        compiler_params=pltpu.CompilerParams(vmem_limit_bytes=8 << 20),
+        name="place",
+    )(where, *held, *sources)
 
 
 def swap(array, axis, bit):
     return lax.ppermute(array, axis, [(i, i ^ bit) for i in range(lax.axis_size(axis))])
+
+
+def onward(array, axis):
+    size = lax.axis_size(axis)
+    return lax.ppermute(array, axis, [(i, (i + 2) % size) for i in range(size)])
 
 
 def body(
@@ -270,27 +370,55 @@
         ],
         axis=2,
     )
-    part, jac = forward(codes, left, right, vectors.T, capacity)
-
-    pieces = lax.all_to_all(part, "rows", split_axis=0, concat_axis=0, tiled=True)
-    outputs = jnp.sum(pieces, axis=0).astype(bf16)
-    gathered = lax.all_gather(outputs, "rows")
-
+    me = lax.axis_index("rows")
     core = lax.axis_index("grp") % 2
-    give = backward(codes, (1 - core).reshape(1), gathered, jac, blocks_here, capacity)
-    got = swap(give, "grp", 1)
-    keep = backward(codes, core.reshape(1), gathered, jac, blocks_here, capacity)
-    half_sum = keep + got
-    bit = 2
-    while bit < members:
-        rounded = lax.reduce_precision(half_sum, 8, 7)
-        half_sum = rounded + swap(rounded.astype(bf16), "grp", bit).astype(f32)
-        bit *= 2
-    other = swap(half_sum, "grp", 1)
-    first = core == 0
-    return jnp.concatenate(
-        [jnp.where(first, half_sum, other), jnp.where(first, other, half_sum)], axis=1
-    )
+    side, position = me % 2, me // 2
+    ring = holders // 2
+
+    splits = 2 if ring % 2 == 0 else 1
+    *far, far_jac = forward(
+        codes, jnp.stack([position, 1 - side]), left, right, vectors, capacity, splits
+    )
+    far = [swap(array, "rows", 1) for array in far]
+    near, near_jac = forward(codes, jnp.stack([position, side]), left, right, vectors, capacity, 1)
+    each = ring // splits
+    running = None
+    for k in range(ring):
+        own = near[k] + far[k // each][k % each]
+        running = own if running is None else own + onward(running, "rows")
+    outputs = running.astype(bf16)
+
+    same, across = [outputs], [swap(outputs, "rows", 1)]
+    for k in range(1, ring):
+        outputs = onward(outputs, "rows")
+        same.append(outputs)
+        across.append(swap(outputs, "rows", 1))
+    pieces = same + across
+
+    def terms(first, here, pieces):
+        where = jnp.stack([position, side, first])
+        return backward(codes, where, near_jac, far_jac, pieces, blocks_here, here, capacity)
+
+    half = blocks_here // 2
+    wide = half // 2 * BLK_P
+    given, pieces = terms((1 - core) * half, half, pieces)
+    given = swap(given, "grp", 1)
+    sums = []
+    for chunk in range(2):
+        kept, _ = terms(core * half + chunk * half // 2, half // 2, pieces)
+        chunk_sum = kept + given[:, chunk * wide : (chunk + 1) * wide]
+        bit = 2
+        while bit < members:
+            rounded = lax.reduce_precision(chunk_sum, 8, 7)
+            sent = rounded.astype(bf16)
+            codes, sent, sums = lax.optimization_barrier((codes, sent, sums))
+            chunk_sum = rounded + swap(sent, "grp", bit).astype(f32)
+            bit *= 2
+        sums.append(chunk_sum)
+    held = [(chunk_sum, swap(chunk_sum, "grp", 1)) for chunk_sum in sums]
+    where = core.reshape(1)
+    total = place(where, None, ((True, 0), (False, 0), (True, 1)), (*held[0], held[1][0]))
+    return place(where, total, ((False, 1),), (held[1][1],))
 
 
 def solution(mesh):

time: 212 us -> 159 us (0.75)
  blocking collectives: 47.2 us -> 0 us
  starting transfers between devices: 9.33 us -> 46.9 us
  Pallas kernels: 52.2 us -> 36.8 us
  between operations: 14.2 us -> 0.88 us
  local copies, waits for them, and re-layouts: 9.23 us -> 1.07 us
  waiting for transfers between devices: 68.6 us -> 63.2 us
    all_to_all x1 -> x0, blocking collectives: 47.2 us -> none  [body(): lax.all_to_all(part, 'rows', split_axis=0, concat_axis=0, tiled=True)]
    all_gather x1 -> x0, waiting for transfers between devices: 40.2 us -> none  [body(): gathered = lax.all_gather(outputs, 'rows')]
    ppermute x3 -> x11, starting transfers between devices: 2.04 us -> 33 us  [swap(): lax.ppermute(array, axis, [(i, i ^ bit) for i in range(lax.axis_size(axis...]
    ppermute x0 -> x6, waiting for transfers between devices: none -> 28.6 us  [onward(): return lax.ppermute(array, axis, [(i, (i + 2) % size) for i in range(size)])]
    pallas_call x3 -> x7, Pallas kernels: 52.2 us -> 36.8 us  [the longest x2 17.9 us: forward(): pl.pallas_call(functools.partial(forward_kernel, blocks, capacity, ring,...]
    unnamed x7 -> x2, local copies, waits for them, and re-layouts: 8.17 us -> 0.01 us
    ppermute x0 -> x6, starting transfers between devices: none -> 6.65 us  [onward(): return lax.ppermute(array, axis, [(i, (i + 2) % size) for i in range(size)])]
    all_to_all x1, waiting for transfers between devices: 0.75 us -> 5.44 us  [body(): left = lax.all_to_all(send, 'rows', split_axis=0, concat_axis=0, tiled=True)]
  transfers between devices with their start and end apart: 5 -> 18, of which waited for: 4 -> 13; matrix products, arithmetic and copies ran while one was open for 3% -> 2% of each run, Pallas kernels for 4% -> 12%
where the time goes in v1:
time: 159 us
  waiting for transfers between devices  63.2 us (40%)
  starting transfers between devices  46.9 us (29%)
  Pallas kernels  36.8 us (23%)
  other arithmetic  10.1 us (6%)
    ppermute x11, starting transfers between devices, swap(): lax.ppermute(array, axis, [(i, i ^ bit) for i in range(lax.axis_size(axis...  33 us
    ppermute x11, waiting for transfers between devices, swap(): lax.ppermute(array, axis, [(i, i ^ bit) for i in range(lax.axis_size(axis...  29.2 us
    ppermute x6, waiting for transfers between devices, onward(): return lax.ppermute(array, axis, [(i, (i + 2) % size) for i in range(size)])  28.6 us
    pallas_call x2, Pallas kernels, forward(): pl.pallas_call(functools.partial(forward_kernel, blocks, capacity, ring,...  17.9 us
    pallas_call x3, Pallas kernels, backward(): pl.pallas_call(functools.partial(kernel, blocks, capacity, total // 2), o...  16.3 us
    all_to_all x1, starting transfers between devices, body(): left = lax.all_to_all(send, 'rows', split_axis=0, concat_axis=0, tiled=True)  7.25 us
    ppermute x6, starting transfers between devices, onward(): return lax.ppermute(array, axis, [(i, (i + 2) % size) for i in range(size)])  6.65 us
    all_to_all x1, waiting for transfers between devices, body(): left = lax.all_to_all(send, 'rows', split_axis=0, concat_axis=0, tiled=True)  5.44 us
  transfers between devices with their start and end apart: 18, of which 13 were waited for; matrix products, arithmetic and copies ran while one was open for 2% of the time, Pallas kernels for 12%

profile of v1, /device:TPU:0, one launch (start us, length us, event | category | flops | bytes accessed | tf_op | source)
XLA Modules:
  0.0 159.0 jit_solution(11477611831839284093)
XLA Ops:
  0.0 0.8 fusion.19
  0.8 0.7 stack.87
  2.2 0.9 select_reduce_fusion
  3.0 0.7 compare_select_fusion.4
  3.7 0.2 convert_reduce_fusion
  3.9 0.1 select_reduce_fusion.1
  4.0 0.1 convert_element_type.66
  4.1 0.1 stack.75
  4.2 0.7 fusion.13
  4.9 7.3 %all-to-all-start = ((bf16[8,8,1024]{2,1,0:T(8,128)(2,1)}), bf16[8,8,1024]{2,1,0:T(8,128)(2,1)S(1)}, u32[]{:S(2)}, u32[]{:S(2)}) async-start(bf16[8,8,1024]{2,1,0:T(8,128)(2,1)} %fusion.13), calls=%async_computation | async-start | bytes 262144 | tf_op jit(solution)/shard_map/all_to_all | solution.py:359
  12.2 0.8 multiply_convert_fusion
  13.0 0.8 broadcast_in_dim.90
  13.8 0.1 broadcast_select_fusion
  13.9 0.1 pad_add_fusion.2
  14.0 0.1 pad_maximum_fusion.right
  14.1 5.4 %all-to-all-done.left = bf16[8,8,1024]{2,1,0:T(8,128)(2,1)S(1)} async-done(((bf16[8,8,1024]{2,1,0:T(8,128)(2,1)}), bf16[8,8,1024]{2,1,0:T(8,128)(2,1)S(1)}, u32[]{:S(2)}, u32[]{:S(2)}) %all-to-all-start) | async-done | bytes 131104 | tf_op jit(solution)/shard_map/all_to_all | solution.py:359
  19.5 0.1 reshape.106.codes.refs_0_
  19.6 8.9 %forward.3 = (f32[2,64,1024]{2,1,0:T(8,128)S(1)}, f32[2,64,1024]{2,1,0:T(8,128)S(1)}, bf16[129,256,512]{2,1,0:T(8,128)(2,1)}) custom-call(s32[128]{0:T(128)S(1)} %reshape.106.codes.refs_0_, s32[2]{0:T(128)S(1)} %get-tuple-element.38.where, bf16[8,8,1024]{2,1,0:T(8,128)(2,1)S(1)} %all-to-all-done.left, bf16[32,8,1024]{2,1,0:T(8,128)(2,1)S(1)} %pad_maximum_fusion.right, ...), custom_call_target="tpu_custom_call" | custom-call | flops 32 | bytes 64 | tf_op jit(solution)/shard_map/forward/pallas_call | solution.py:163
  28.5 0.1 collective-permute-start.1
  28.6 8.9 %forward.2 = (f32[4,64,1024]{2,1,0:T(8,128)S(1)}, bf16[129,256,512]{2,1,0:T(8,128)(2,1)}) custom-call(s32[128]{0:T(128)S(1)} %reshape.106.codes.refs_0_, s32[2]{0:T(128)S(1)} %get-tuple-element.37.where, bf16[8,8,1024]{2,1,0:T(8,128)(2,1)S(1)} %all-to-all-done.left, bf16[32,8,1024]{2,1,0:T(8,128)(2,1)S(1)} %pad_maximum_fusion.right, ...), custom_call_target="tpu_custom_call" | custom-call | flops 32 | bytes 64 | tf_op jit(solution)/shard_map/forward/pallas_call | solution.py:163
  37.6 1.3 collective-permute-done.1
  38.9 3.9 %collective-permute-start.2 = (f32[64,1024]{1,0:T(8,128)S(1)}, f32[64,1024]{1,0:T(8,128)S(1)}, u32[]{:S(2)}, u32[]{:S(2)}) collective-permute-start(f32[64,1024]{1,0:T(8,128)S(1)} %fusion.4), channel_id=1, source_target_pairs={{0,8},{4,12},{8,16},{12,20},{16,24},{20,28},{24,0},{28,4},{1,9},{5... | collective-permute-start | bytes 786440 | tf_op jit(solution)/shard_map/ppermute | solution.py:310
  42.9 0.5 collective-permute-start
  43.4 3.7 %collective-permute-done.2 = f32[64,1024]{1,0:T(8,128)S(1)} collective-permute-done((f32[64,1024]{1,0:T(8,128)S(1)}, f32[64,1024]{1,0:T(8,128)S(1)}, u32[]{:S(2)}, u32[]{:S(2)}) %collective-permute-start.2) | collective-permute-done | bytes 262176 | tf_op jit(solution)/shard_map/ppermute | solution.py:310
  47.2 2.1 %collective-permute-start.3 = (f32[64,1024]{1,0:T(8,128)S(1)}, f32[64,1024]{1,0:T(8,128)S(1)}, u32[]{:S(2)}, u32[]{:S(2)}) collective-permute-start(f32[64,1024]{1,0:T(8,128)S(1)} %fusion.6), channel_id=1, source_target_pairs={{0,8},{4,12},{8,16},{12,20},{16,24},{20,28},{24,0},{28,4},{1,9},{5... | collective-permute-start | bytes 786440 | tf_op jit(solution)/shard_map/ppermute | solution.py:310
  49.3 2.7 %collective-permute-done = f32[2,64,1024]{2,1,0:T(8,128)S(1)} collective-permute-done((f32[2,64,1024]{2,1,0:T(8,128)S(1)}, f32[2,64,1024]{2,1,0:T(8,128)S(1)}, u32[]{:S(2)}, u32[]{:S(2)}) %collective-permute-start) | collective-permute-done | bytes 524320 | tf_op jit(solution)/shard_map/ppermute | solution.py:305
  52.0 3.4 %collective-permute-done.3 = f32[64,1024]{1,0:T(8,128)S(1)} collective-permute-done((f32[64,1024]{1,0:T(8,128)S(1)}, f32[64,1024]{1,0:T(8,128)S(1)}, u32[]{:S(2)}, u32[]{:S(2)}) %collective-permute-start.3) | collective-permute-done | bytes 262176 | tf_op jit(solution)/shard_map/ppermute | solution.py:310
  55.4 0.1 fusion.8
  55.5 0.5 collective-permute-start.4
  56.0 7.7 %collective-permute-done.4 = f32[64,1024]{1,0:T(8,128)S(1)} collective-permute-done((f32[64,1024]{1,0:T(8,128)S(1)}, f32[64,1024]{1,0:T(8,128)S(1)}, u32[]{:S(2)}, u32[]{:S(2)}) %collective-permute-start.4) | collective-permute-done | bytes 262176 | tf_op jit(solution)/shard_map/ppermute | solution.py:310
  63.7 0.1 fusion.11.refs_0_
  63.8 0.1 collective-permute-start.5
  63.8 6.8 %collective-permute-done.5.refs_1_ = bf16[64,1024]{1,0:T(8,128)(2,1)S(1)} collective-permute-done((bf16[64,1024]{1,0:T(8,128)(2,1)S(1)}, bf16[64,1024]{1,0:T(8,128)(2,1)S(1)}, u32[]{:S(2)}, u32[]{:S(2)}) %collective-permute-start.5) | collective-permute-done | bytes 131104 | tf_op jit(solution)/shard_map/ppermute | solution.py:310
  70.6 0.0 collective-permute-start.6
  70.6 7.0 %collective-permute-done.6.refs_2_ = bf16[64,1024]{1,0:T(8,128)(2,1)S(1)} collective-permute-done((bf16[64,1024]{1,0:T(8,128)(2,1)S(1)}, bf16[64,1024]{1,0:T(8,128)(2,1)S(1)}, u32[]{:S(2)}, u32[]{:S(2)}) %collective-permute-start.6) | collective-permute-done | bytes 131104 | tf_op jit(solution)/shard_map/ppermute | solution.py:310
  77.6 9.1 %collective-permute-start.8 = (bf16[64,1024]{1,0:T(8,128)(2,1)S(1)}, bf16[64,1024]{1,0:T(8,128)(2,1)S(1)}, u32[]{:S(2)}, u32[]{:S(2)}) collective-permute-start(bf16[64,1024]{1,0:T(8,128)(2,1)S(1)} %fusion.11.refs_0_), channel_id=1, source_target_pairs={{0,4},{4,0},{8,12},{12,8},{16,20},{20,16},{24,28},{28,24},{1,5},{5... | collective-permute-start | bytes 393224 | tf_op jit(solution)/shard_map/ppermute | solution.py:305
  86.6 0.0 collective-permute-start.9
  86.7 2.0 %collective-permute-start.10 = (bf16[64,1024]{1,0:T(8,128)(2,1)S(1)}, bf16[64,1024]{1,0:T(8,128)(2,1)S(1)}, u32[]{:S(2)}, u32[]{:S(2)}) collective-permute-start(bf16[64,1024]{1,0:T(8,128)(2,1)S(1)} %collective-permute-done.6.refs_2_), channel_id=1, source_target_pairs={{0,4},{4,0},{8,12},{12,8},{16,20},{20,16},{24,28},{28,24},{1,5},{5... | collective-permute-start | bytes 393224 | tf_op jit(solution)/shard_map/ppermute | solution.py:305
  88.7 0.0 collective-permute-done.7.refs_3_
  88.7 4.7 %collective-permute-start.11 = (bf16[64,1024]{1,0:T(8,128)(2,1)S(1)}, bf16[64,1024]{1,0:T(8,128)(2,1)S(1)}, u32[]{:S(2)}, u32[]{:S(2)}) collective-permute-start(bf16[64,1024]{1,0:T(8,128)(2,1)S(1)} %collective-permute-done.7.refs_3_), channel_id=1, source_target_pairs={{0,4},{4,0},{8,12},{12,8},{16,20},{20,16},{24,28},{28,24},{1,5},{5... | collective-permute-start | bytes 393224 | tf_op jit(solution)/shard_map/ppermute | solution.py:305
  93.4 0.1 pad_add_fusion.4.where
  93.5 0.0 collective-permute-done.8.refs_4_
  93.5 0.0 collective-permute-done.9.refs_5_
  93.5 0.1 collective-permute-done.10.refs_6_
  93.6 4.2 %collective-permute-done.11.refs_7_ = bf16[64,1024]{1,0:T(8,128)(2,1)S(1)} collective-permute-done((bf16[64,1024]{1,0:T(8,128)(2,1)S(1)}, bf16[64,1024]{1,0:T(8,128)(2,1)S(1)}, u32[]{:S(2)}, u32[]{:S(2)}) %collective-permute-start.11) | collective-permute-done | bytes 131104 | tf_op jit(solution)/shard_map/ppermute | solution.py:305
  97.8 7.5 %backward.3 = (f32[64,8192]{1,0:T(8,128)}, bf16[8,64,1024]{2,1,0:T(8,128)(2,1)S(1)}) custom-call(s32[128]{0:T(128)S(1)} %reshape.106.codes.refs_0_, s32[3]{0:T(128)S(1)} %pad_add_fusion.4.where, bf16[129,256,512]{2,1,0:T(8,128)(2,1)} %get-tuple-element.16.near_jac.refs_2_, bf16[129,256,512]{2,1,0:T(8,128)(2,1)} %get-tuple-element.17.far_jac.refs_3_, ...), custom_call_target="tpu_custom_call" | custom-call | flops 16 | bytes 64 | tf_op jit(solution)/shard_map/backward/pallas_call | solution.py:255
  105.3 3.6 %collective-permute-start.12 = (f32[64,8192]{1,0:T(8,128)}, f32[64,8192]{1,0:T(8,128)}, u32[]{:S(2)}, u32[]{:S(2)}) collective-permute-start(f32[64,8192]{1,0:T(8,128)} %get-tuple-element.22), channel_id=1, source_target_pairs={{0,1},{1,0},{2,3},{3,2},{4,5},{5,4},{6,7},{7,6},{8,9},{9,8},{10,11... | collective-permute-start | bytes 6291464 | tf_op jit(solution)/shard_map/ppermute | solution.py:305
  109.0 0.1 pad_add_fusion.refs_1_
  109.0 4.5 %backward.4 = f32[64,4096]{1,0:T(8,128)S(1)} custom-call(s32[128]{0:T(128)S(1)} %reshape.106.codes.refs_0_, s32[3]{0:T(128)S(1)} %pad_add_fusion.refs_1_, bf16[129,256,512]{2,1,0:T(8,128)(2,1)} %get-tuple-element.16.near_jac.refs_2_, bf16[129,256,512]{2,1,0:T(8,128)(2,1)} %get-tuple-element.17.far_jac.refs_3_, bf16[8,64,1024]{2,1,0:T(8,128)(2,1)S(1)} %get-tuple-element.21.refs_4_), custom_call_target="tpu_custom_call" | custom-call | flops 16 | bytes 64 | tf_op jit(solution)/shard_map/backward/pallas_call | solution.py:255
  113.5 1.3 fusion.2
  114.9 11.1 %collective-permute-start.13 = (bf16[64,4096]{1,0:T(8,128)(2,1)S(1)}, bf16[64,4096]{1,0:T(8,128)(2,1)S(1)}, u32[]{:S(2)}, u32[]{:S(2)}) collective-permute-start(bf16[64,4096]{1,0:T(8,128)(2,1)S(1)} %fusion.2), channel_id=1, source_target_pairs={{0,2},{1,3},{2,0},{3,1},{4,6},{5,7},{6,4},{7,5},{8,10},{9,11},{10,... | collective-permute-start | bytes 1572872 | tf_op jit(solution)/shard_map/ppermute | solution.py:305
  126.0 0.1 pad_add_fusion.5.refs_1_
  126.0 4.3 %backward.5 = f32[64,4096]{1,0:T(8,128)S(1)} custom-call(s32[128]{0:T(128)S(1)} %reshape.106.codes.refs_0_, s32[3]{0:T(128)S(1)} %pad_add_fusion.5.refs_1_, bf16[129,256,512]{2,1,0:T(8,128)(2,1)} %get-tuple-element.16.near_jac.refs_2_, bf16[129,256,512]{2,1,0:T(8,128)(2,1)} %get-tuple-element.17.far_jac.refs_3_, ...), custom_call_target="tpu_custom_call" | custom-call | flops 16 | bytes 64 | tf_op jit(solution)/shard_map/backward/pallas_call | solution.py:255
  130.3 8.0 %collective-permute-done.13 = bf16[64,4096]{1,0:T(8,128)(2,1)S(1)} collective-permute-done((bf16[64,4096]{1,0:T(8,128)(2,1)S(1)}, bf16[64,4096]{1,0:T(8,128)(2,1)S(1)}, u32[]{:S(2)}, u32[]{:S(2)}) %collective-permute-start.13) | collective-permute-done | bytes 524320 | tf_op jit(solution)/shard_map/ppermute | solution.py:305
  138.3 1.9 %convert_add_fusion.1 = (f32[64,4096]{1,0:T(8,128)S(1)}, bf16[64,4096]{1,0:T(8,128)(2,1)S(1)}) fusion(bf16[64,4096]{1,0:T(8,128)(2,1)S(1)} %collective-permute-done.13, f32[64,4096]{1,0:T(8,128)S(1)} %backward.4, f32[64,8192]{1,0:T(8,128)} %collective-permute-done.12, f32[64,4096]{1,0:T(8,128)S(1)} %backward.5), kind=kLoop, calls=%fused_computation.5 | loop fusion | flops 1835008 | bytes 6291456 | tf_op jit(solution)/shard_map/add | solution.py:415
  140.2 1.8 %collective-permute-start.15 = (bf16[64,4096]{1,0:T(8,128)(2,1)S(1)}, bf16[64,4096]{1,0:T(8,128)(2,1)S(1)}, u32[]{:S(2)}, u32[]{:S(2)}) collective-permute-start(bf16[64,4096]{1,0:T(8,128)(2,1)S(1)} %get-tuple-element.26), channel_id=1, source_target_pairs={{0,2},{1,3},{2,0},{3,1},{4,6},{5,7},{6,4},{7,5},{8,10},{9,11},{10,... | collective-permute-start | bytes 1572872 | tf_op jit(solution)/shard_map/ppermute | solution.py:305
  142.0 0.0 collective-permute-start.14
  142.0 11.9 %collective-permute-done.15 = bf16[64,4096]{1,0:T(8,128)(2,1)S(1)} collective-permute-done((bf16[64,4096]{1,0:T(8,128)(2,1)S(1)}, bf16[64,4096]{1,0:T(8,128)(2,1)S(1)}, u32[]{:S(2)}, u32[]{:S(2)}) %collective-permute-start.15) | collective-permute-done | bytes 524320 | tf_op jit(solution)/shard_map/ppermute | solution.py:305
  153.9 1.4 convert_add_fusion.refs_2_
  155.3 0.1 collective-permute-start.16
  155.4 0.0 collective-permute-done.14.refs_1_
  155.4 1.7 %place.2.refs_0_ = f32[64,16384]{1,0:T(8,128)} custom-call(s32[1]{0:T(128)} %bitcast.where, f32[64,4096]{1,0:T(8,128)S(1)} %get-tuple-element.25.refs_0_, f32[64,4096]{1,0:T(8,128)S(1)} %collective-permute-done.14.refs_1_, f32[64,4096]{1,0:T(8,128)S(1)} %convert_add_fusion.refs_2_), custom_call_target="tpu_custom_call" | custom-call | tf_op jit(solution)/shard_map/place/pallas_call | solution.py:292
  157.1 0.9 collective-permute-done.16.refs_1_
  158.1 1.0 place.3
  (13 shorter events, 0.2 us)
Async XLA Ops:
  0.0 19.6 %copy-start = (bf16[64,16384]{1,0:T(8,128)(2,1)S(1)}, bf16[64,16384]{1,0:T(8,128)(2,1)}, u32[]{:S(2)}) copy-start(bf16[64,16384]{1,0:T(8,128)(2,1)} %vectors.3) | copy-start | bytes 6291460
  4.9 14.6 %all-to-all-start = ((bf16[8,8,1024]{2,1,0:T(8,128)(2,1)}), bf16[8,8,1024]{2,1,0:T(8,128)(2,1)S(1)}, u32[]{:S(2)}, u32[]{:S(2)}) async-start(bf16[8,8,1024]{2,1,0:T(8,128)(2,1)} %fusion.13), calls=%async_computation | async-start | bytes 262144 | tf_op jit(solution)/shard_map/all_to_all | solution.py:359
  28.5 10.3 %collective-permute-start.1 = (f32[2,64,1024]{2,1,0:T(8,128)S(1)}, f32[2,64,1024]{2,1,0:T(8,128)S(1)}, u32[]{:S(2)}, u32[]{:S(2)}) collective-permute-start(f32[2,64,1024]{2,1,0:T(8,128)S(1)} %get-tuple-element.20), channel_id=1, source_target_pairs={{0,4},{4,0},{8,12},{12,8},{16,20},{20,16},{24,28},{28,24},{1,5},{5... | collective-permute-start | bytes 1572872 | tf_op jit(solution)/shard_map/ppermute | solution.py:305
  38.9 8.2 %collective-permute-start.2 = (f32[64,1024]{1,0:T(8,128)S(1)}, f32[64,1024]{1,0:T(8,128)S(1)}, u32[]{:S(2)}, u32[]{:S(2)}) collective-permute-start(f32[64,1024]{1,0:T(8,128)S(1)} %fusion.4), channel_id=1, source_target_pairs={{0,8},{4,12},{8,16},{12,20},{16,24},{20,28},{24,0},{28,4},{1,9},{5... | collective-permute-start | bytes 786440 | tf_op jit(solution)/shard_map/ppermute | solution.py:310
  42.9 9.2 %collective-permute-start = (f32[2,64,1024]{2,1,0:T(8,128)S(1)}, f32[2,64,1024]{2,1,0:T(8,128)S(1)}, u32[]{:S(2)}, u32[]{:S(2)}) collective-permute-start(f32[2,64,1024]{2,1,0:T(8,128)S(1)} %get-tuple-element.19), channel_id=1, source_target_pairs={{0,4},{4,0},{8,12},{12,8},{16,20},{20,16},{24,28},{28,24},{1,5},{5... | collective-permute-start | bytes 1572872 | tf_op jit(solution)/shard_map/ppermute | solution.py:305
  47.2 8.2 %collective-permute-start.3 = (f32[64,1024]{1,0:T(8,128)S(1)}, f32[64,1024]{1,0:T(8,128)S(1)}, u32[]{:S(2)}, u32[]{:S(2)}) collective-permute-start(f32[64,1024]{1,0:T(8,128)S(1)} %fusion.6), channel_id=1, source_target_pairs={{0,8},{4,12},{8,16},{12,20},{16,24},{20,28},{24,0},{28,4},{1,9},{5... | collective-permute-start | bytes 786440 | tf_op jit(solution)/shard_map/ppermute | solution.py:310
  55.5 8.2 %collective-permute-start.4 = (f32[64,1024]{1,0:T(8,128)S(1)}, f32[64,1024]{1,0:T(8,128)S(1)}, u32[]{:S(2)}, u32[]{:S(2)}) collective-permute-start(f32[64,1024]{1,0:T(8,128)S(1)} %fusion.8), channel_id=1, source_target_pairs={{0,8},{4,12},{8,16},{12,20},{16,24},{20,28},{24,0},{28,4},{1,9},{5... | collective-permute-start | bytes 786440 | tf_op jit(solution)/shard_map/ppermute | solution.py:310
  63.8 6.8 %collective-permute-start.5 = (bf16[64,1024]{1,0:T(8,128)(2,1)S(1)}, bf16[64,1024]{1,0:T(8,128)(2,1)S(1)}, u32[]{:S(2)}, u32[]{:S(2)}) collective-permute-start(bf16[64,1024]{1,0:T(8,128)(2,1)S(1)} %fusion.11.refs_0_), channel_id=1, source_target_pairs={{0,8},{4,12},{8,16},{12,20},{16,24},{20,28},{24,0},{28,4},{1,9},{5... | collective-permute-start | bytes 393224 | tf_op jit(solution)/shard_map/ppermute | solution.py:310
  70.6 7.0 %collective-permute-start.6 = (bf16[64,1024]{1,0:T(8,128)(2,1)S(1)}, bf16[64,1024]{1,0:T(8,128)(2,1)S(1)}, u32[]{:S(2)}, u32[]{:S(2)}) collective-permute-start(bf16[64,1024]{1,0:T(8,128)(2,1)S(1)} %collective-permute-done.5.refs_1_), channel_id=1, source_target_pairs={{0,8},{4,12},{8,16},{12,20},{16,24},{20,28},{24,0},{28,4},{1,9},{5... | collective-permute-start | bytes 393224 | tf_op jit(solution)/shard_map/ppermute | solution.py:310
  77.6 11.1 %collective-permute-start.7 = (bf16[64,1024]{1,0:T(8,128)(2,1)S(1)}, bf16[64,1024]{1,0:T(8,128)(2,1)S(1)}, u32[]{:S(2)}, u32[]{:S(2)}) collective-permute-start(bf16[64,1024]{1,0:T(8,128)(2,1)S(1)} %collective-permute-done.6.refs_2_), channel_id=1, source_target_pairs={{0,8},{4,12},{8,16},{12,20},{16,24},{20,28},{24,0},{28,4},{1,9},{5... | collective-permute-start | bytes 393224 | tf_op jit(solution)/shard_map/ppermute | solution.py:310
  77.6 15.9 %collective-permute-start.8 = (bf16[64,1024]{1,0:T(8,128)(2,1)S(1)}, bf16[64,1024]{1,0:T(8,128)(2,1)S(1)}, u32[]{:S(2)}, u32[]{:S(2)}) collective-permute-start(bf16[64,1024]{1,0:T(8,128)(2,1)S(1)} %fusion.11.refs_0_), channel_id=1, source_target_pairs={{0,4},{4,0},{8,12},{12,8},{16,20},{20,16},{24,28},{28,24},{1,5},{5... | collective-permute-start | bytes 393224 | tf_op jit(solution)/shard_map/ppermute | solution.py:305
  86.6 6.8 %collective-permute-start.9 = (bf16[64,1024]{1,0:T(8,128)(2,1)S(1)}, bf16[64,1024]{1,0:T(8,128)(2,1)S(1)}, u32[]{:S(2)}, u32[]{:S(2)}) collective-permute-start(bf16[64,1024]{1,0:T(8,128)(2,1)S(1)} %collective-permute-done.5.refs_1_), channel_id=1, source_target_pairs={{0,4},{4,0},{8,12},{12,8},{16,20},{20,16},{24,28},{28,24},{1,5},{5... | collective-permute-start | bytes 393224 | tf_op jit(solution)/shard_map/ppermute | solution.py:305
  86.7 6.9 %collective-permute-start.10 = (bf16[64,1024]{1,0:T(8,128)(2,1)S(1)}, bf16[64,1024]{1,0:T(8,128)(2,1)S(1)}, u32[]{:S(2)}, u32[]{:S(2)}) collective-permute-start(bf16[64,1024]{1,0:T(8,128)(2,1)S(1)} %collective-permute-done.6.refs_2_), channel_id=1, source_target_pairs={{0,4},{4,0},{8,12},{12,8},{16,20},{20,16},{24,28},{28,24},{1,5},{5... | collective-permute-start | bytes 393224 | tf_op jit(solution)/shard_map/ppermute | solution.py:305
  88.7 9.1 %collective-permute-start.11 = (bf16[64,1024]{1,0:T(8,128)(2,1)S(1)}, bf16[64,1024]{1,0:T(8,128)(2,1)S(1)}, u32[]{:S(2)}, u32[]{:S(2)}) collective-permute-start(bf16[64,1024]{1,0:T(8,128)(2,1)S(1)} %collective-permute-done.7.refs_3_), channel_id=1, source_target_pairs={{0,4},{4,0},{8,12},{12,8},{16,20},{20,16},{24,28},{28,24},{1,5},{5... | collective-permute-start | bytes 393224 | tf_op jit(solution)/shard_map/ppermute | solution.py:305
  105.3 8.2 %collective-permute-start.12 = (f32[64,8192]{1,0:T(8,128)}, f32[64,8192]{1,0:T(8,128)}, u32[]{:S(2)}, u32[]{:S(2)}) collective-permute-start(f32[64,8192]{1,0:T(8,128)} %get-tuple-element.22), channel_id=1, source_target_pairs={{0,1},{1,0},{2,3},{3,2},{4,5},{5,4},{6,7},{7,6},{8,9},{9,8},{10,11... | collective-permute-start | bytes 6291464 | tf_op jit(solution)/shard_map/ppermute | solution.py:305
  114.9 23.5 %collective-permute-start.13 = (bf16[64,4096]{1,0:T(8,128)(2,1)S(1)}, bf16[64,4096]{1,0:T(8,128)(2,1)S(1)}, u32[]{:S(2)}, u32[]{:S(2)}) collective-permute-start(bf16[64,4096]{1,0:T(8,128)(2,1)S(1)} %fusion.2), channel_id=1, source_target_pairs={{0,2},{1,3},{2,0},{3,1},{4,6},{5,7},{6,4},{7,5},{8,10},{9,11},{10,... | collective-permute-start | bytes 1572872 | tf_op jit(solution)/shard_map/ppermute | solution.py:305
  140.2 13.7 %collective-permute-start.15 = (bf16[64,4096]{1,0:T(8,128)(2,1)S(1)}, bf16[64,4096]{1,0:T(8,128)(2,1)S(1)}, u32[]{:S(2)}, u32[]{:S(2)}) collective-permute-start(bf16[64,4096]{1,0:T(8,128)(2,1)S(1)} %get-tuple-element.26), channel_id=1, source_target_pairs={{0,2},{1,3},{2,0},{3,1},{4,6},{5,7},{6,4},{7,5},{8,10},{9,11},{10,... | collective-permute-start | bytes 1572872 | tf_op jit(solution)/shard_map/ppermute | solution.py:305
  142.0 13.4 %collective-permute-start.14 = (f32[64,4096]{1,0:T(8,128)S(1)}, f32[64,4096]{1,0:T(8,128)S(1)}, u32[]{:S(2)}, u32[]{:S(2)}) collective-permute-start(f32[64,4096]{1,0:T(8,128)S(1)} %get-tuple-element.25.refs_0_), channel_id=1, source_target_pairs={{0,1},{1,0},{2,3},{3,2},{4,5},{5,4},{6,7},{7,6},{8,9},{9,8},{10,11... | collective-permute-start | bytes 3145736 | tf_op jit(solution)/shard_map/ppermute | solution.py:305
  155.3 2.7 %collective-permute-start.16 = (f32[64,4096]{1,0:T(8,128)S(1)}, f32[64,4096]{1,0:T(8,128)S(1)}, u32[]{:S(2)}, u32[]{:S(2)}) collective-permute-start(f32[64,4096]{1,0:T(8,128)S(1)} %convert_add_fusion.refs_2_), channel_id=1, source_target_pairs={{0,1},{1,0},{2,3},{3,2},{4,5},{5,4},{6,7},{7,6},{8,9},{9,8},{10,11... | collective-permute-start | bytes 3145736 | tf_op jit(solution)/shard_map/ppermute | solution.py:305

commit v2 on v1

--- a/solution.py
+++ b/solution.py
@@ -12,7 +12,6 @@
 BLK_P = 512
 PIECES = 8
 RING = 8
-VMEM_BASE = 12 << 20
 
 f32 = jnp.float32
 bf16 = jnp.bfloat16
@@ -47,46 +46,32 @@
     return out
 
 
-def collect(codes, todo, wanted):
-    def visit(place, found):
-        todo[found] = place
-        code = codes[place]
-        return found + ((code >= 0) & wanted(place, code)).astype(jnp.int32)
-
-    return lax.fori_loop(0, codes.shape[0], visit, 0)
+def collect(codes, todo, start, places, wanted):
+    def visit(step, found):
+        todo[found] = start + step
+        code = codes[start + step]
+        return found + ((code >= 0) & wanted(code)).astype(jnp.int32)
+
+    return lax.fori_loop(0, places, visit, 0)
 
 
 def entry_cost(entries, vector_count):
     return pl.CostEstimate(flops=entries, bytes_accessed=vector_count, transcendentals=0)
 
 
-def forward_kernel(
-    blocks,
-    capacity,
-    ring,
-    splits,
-    codes,
-    where,
-    left,
-    right,
-    vectors,
-    *refs,
-):
-    *parts, jac, todo, part, even, odd, sems = refs
+def forward_kernel(blocks, capacity, codes, where, left, right, vectors, *refs):
+    near, far, jac, todo, part, even, odd, sems = refs[-8:]
     spare = codes.shape[0]
     part[...] = jnp.zeros_like(part)
-
-    def wanted(place, code):
-        return lax.rem(lax.div(place, capacity), 2) == where[1]
-
-    found = collect(codes, todo, wanted)
+    start = 2 * capacity * where[0]
+    found = collect(codes, todo, start, 2 * capacity, lambda code: True)
     steps = (found + 1) // 2
 
     def decode(place):
         code = codes[place]
-        position = lax.div(place, 2 * capacity)
-        behind = lax.rem(where[0] - 1 - position + 2 * ring, ring)
-        return lax.rem(code, blocks), lax.div(code, blocks), lax.div(place, capacity), behind
+        group = lax.div(place, capacity)
+        away = jnp.where(lax.rem(group, 2) == where[1], 0, 1)
+        return lax.rem(code, blocks), lax.div(code, blocks), group, away
 
     def make(buffer, place):
         block, row, group, _ = decode(place)
@@ -103,14 +88,14 @@
         buffer[...] = (weight * (root * root - 1.0)).astype(bf16)
 
     def apply(buffer, place, keep):
-        block, row, _, behind = decode(place)
+        block, row, _, away = decode(place)
         chosen = vectors[:, pl.ds(pl.multiple_of(block * BLK_P, BLK_P), BLK_P)]
         term = lax.dot_general(
             buffer[...], chosen, (((1,), (1,)), ((), ())), preferred_element_type=f32
         )
         if keep is not None:
             term = jnp.where(keep, term, 0.0)
-        part[behind, :, pl.ds(pl.multiple_of(row * BLK_R, BLK_R), BLK_R)] += term.T
+        part[away, :, pl.ds(pl.multiple_of(row * BLK_R, BLK_R), BLK_R)] += term.T
 
     def save(buffer, parity, which, place):
         return pltpu.make_async_copy(buffer.at[parity], jac.at[place], sems.at[parity, which])
@@ -147,68 +132,56 @@
             save(even, parity, 0, 0).wait()
             save(odd, parity, 1, 0).wait()
 
-    each = ring // splits
-    for k in range(splits):
-        parts[k][...] = part[k * each : (k + 1) * each]
-
-
-def forward(codes, where, left, right, vectors, capacity, splits):
-    groups, _, width = left.shape
-    ring = groups // 2
+    near[...] = part[0]
+    far[...] = part[1]
+
+
+def forward(codes, where, left, right, vectors, capacity, jac):
+    _, _, width = left.shape
     blocks = right.shape[0]
     room = codes.shape[0]
     count = vectors.shape[0]
     vmem = pl.BlockSpec(memory_space=pltpu.VMEM)
     smem = pl.BlockSpec(memory_space=pltpu.SMEM)
+    hbm = pl.BlockSpec(memory_space=pltpu.HBM)
+    held = [] if jac is None else [jac]
     return pl.pallas_call(
-        functools.partial(forward_kernel, blocks, capacity, ring, splits),
-        out_shape=(jax.ShapeDtypeStruct((ring // splits, count, width), f32),) * splits
+        functools.partial(forward_kernel, blocks, capacity),
+        out_shape=(jax.ShapeDtypeStruct((count, width), f32),) * 2
         + (pltpu.HBM((room + 1, BLK_R, BLK_P), bf16),),
-        in_specs=[smem, smem, vmem, vmem, vmem],
-        out_specs=(vmem,) * splits + (pl.BlockSpec(memory_space=pltpu.HBM),),
+        in_specs=[smem, smem, vmem, vmem, vmem] + [hbm] * len(held),
+        out_specs=(vmem, vmem, hbm),
         scratch_shapes=[
-            pltpu.SMEM((room + 1,), jnp.int32),
-            pltpu.VMEM((ring, count, width), f32),
+            pltpu.SMEM((2 * capacity + 1,), jnp.int32),
+            pltpu.VMEM((2, count, width), f32),
             pltpu.VMEM((2, BLK_R, BLK_P), bf16),
             pltpu.VMEM((2, BLK_R, BLK_P), bf16),
             pltpu.SemaphoreType.DMA((2, 2)),
         ],
-        compiler_params=pltpu.CompilerParams(
-            vmem_limit_bytes=VMEM_BASE + 12 * ring * count * width
-        ),
-        cost_estimate=entry_cost(room // 4, count),
+        input_output_aliases={5: 2} if held else {},
+        compiler_params=pltpu.CompilerParams(vmem_limit_bytes=16 << 20),
+        cost_estimate=entry_cost(2 * capacity, count),
         name="forward",
-    )(codes, where, left, right, vectors)
-
-
-def backward_kernel(blocks, capacity, ring, codes, where, near_jac, far_jac, *refs):
+    )(codes, where, left, right, vectors, *held)
+
+
+def backward_kernel(blocks, capacity, ring, codes, where, jac, *refs):
     *pieces, out, gathered, todo, buffers, sems = refs
     here = out.shape[1] // BLK_P
     depth = buffers.shape[0]
 
-    def wanted(place, code):
+    def wanted(code):
         block = lax.rem(code, blocks)
         return (block >= where[2]) & (block < where[2] + here)
 
-    found = collect(codes, todo, wanted)
-
-    def is_near(place):
-        return lax.rem(lax.div(place, capacity), 2) == where[1]
-
-    def start(turn):
+    found = collect(codes, todo, 0, codes.shape[0], wanted)
+
+    def load(turn):
         slot = lax.rem(turn, depth)
-        place = todo[turn]
-
-        @pl.when(is_near(place))
-        def _():
-            pltpu.make_async_copy(near_jac.at[place], buffers.at[slot], sems.at[slot]).start()
-
-        @pl.when(~is_near(place))
-        def _():
-            pltpu.make_async_copy(far_jac.at[place], buffers.at[slot], sems.at[slot]).start()
+        return pltpu.make_async_copy(jac.at[todo[turn]], buffers.at[slot], sems.at[slot])
 
     def prime(turn, carry):
-        start(turn)
+        load(turn).start()
         return carry
 
     lax.fori_loop(0, jnp.minimum(found, depth - 1), prime, 0)
@@ -219,17 +192,18 @@
     def step(turn, carry):
         @pl.when(turn + depth - 1 < found)
         def _():
-            start(turn + depth - 1)
+            load(turn + depth - 1).start()
 
         place = todo[turn]
         code = codes[place]
         block, row = lax.rem(code, blocks) - where[2], lax.div(code, blocks)
         behind = lax.rem(where[0] - lax.div(place, 2 * capacity) + ring, ring)
-        piece = jnp.where(is_near(place), behind, ring + behind)
+        near = lax.rem(lax.div(place, capacity), 2) == where[1]
+        piece = jnp.where(near, behind, ring + behind)
         chosen = gathered[piece, :, pl.ds(pl.multiple_of(row * BLK_R, BLK_R), BLK_R)]
         at = pl.ds(pl.multiple_of(block * BLK_P, BLK_P), BLK_P)
         slot = lax.rem(turn, depth)
-        pltpu.make_async_copy(near_jac.at[0], buffers.at[slot], sems.at[slot]).wait()
+        load(turn).wait()
         out[:, at] += jnp.dot(chosen, buffers[slot], preferred_element_type=f32)
         return carry
 
@@ -241,7 +215,7 @@
     backward_kernel(blocks, capacity, ring, *inputs, out, gathered, todo, buffers, sems)
 
 
-def backward(codes, where, near_jac, far_jac, pieces, blocks, here, capacity):
+def backward(codes, where, jac, pieces, blocks, here, capacity):
     joined = not isinstance(pieces, list)
     smem = pl.BlockSpec(memory_space=pltpu.SMEM)
     vmem = pl.BlockSpec(memory_space=pltpu.VMEM)
@@ -255,7 +229,7 @@
     result = pl.pallas_call(
         functools.partial(kernel, blocks, capacity, total // 2),
         out_shape=terms if joined else (terms, gathered),
-        in_specs=[smem, smem, hbm, hbm] + [vmem] * len(sources),
+        in_specs=[smem, smem, hbm] + [vmem] * len(sources),
         out_specs=vmem if joined else (vmem, vmem),
         scratch_shapes=[
             pltpu.SMEM((codes.shape[0] + 1,), jnp.int32),
@@ -265,7 +239,7 @@
         compiler_params=pltpu.CompilerParams(vmem_limit_bytes=36 << 20),
         cost_estimate=entry_cost(codes.shape[0] // 8, count),
         name="backward",
-    )(codes, where, near_jac, far_jac, *sources)
+    )(codes, where, jac, *sources)
     return (result, pieces) if joined else result
 
 
@@ -305,9 +279,9 @@
     return lax.ppermute(array, axis, [(i, i ^ bit) for i in range(lax.axis_size(axis))])
 
 
-def onward(array, axis):
+def shift(array, axis, steps):
     size = lax.axis_size(axis)
-    return lax.ppermute(array, axis, [(i, (i + 2) % size) for i in range(size)])
+    return lax.ppermute(array, axis, [(i, (i + 2 * steps) % size) for i in range(size)])
 
 
 def body(
@@ -375,29 +349,34 @@
     side, position = me % 2, me // 2
     ring = holders // 2
 
-    splits = 2 if ring % 2 == 0 else 1
-    *far, far_jac = forward(
-        codes, jnp.stack([position, 1 - side]), left, right, vectors, capacity, splits
-    )
-    far = [swap(array, "rows", 1) for array in far]
-    near, near_jac = forward(codes, jnp.stack([position, side]), left, right, vectors, capacity, 1)
-    each = ring // splits
-    running = None
+    jac = None
+    waiting = []
+    arrived = []
     for k in range(ring):
-        own = near[k] + far[k // each][k % each]
-        running = own if running is None else own + onward(running, "rows")
-    outputs = running.astype(bf16)
-
-    same, across = [outputs], [swap(outputs, "rows", 1)]
-    for k in range(1, ring):
-        outputs = onward(outputs, "rows")
-        same.append(outputs)
-        across.append(swap(outputs, "rows", 1))
-    pieces = same + across
+        where = jnp.stack([(position + 2 * ring - 1 - k) % ring, side])
+        near, far, jac = forward(codes, where, left, right, vectors, capacity, jac)
+        waiting.append((near, swap(far, "rows", 1)))
+        if k > 0:
+            before, got = waiting[k - 1]
+            pair = before + got
+            older = arrived[: ring - 3]
+            codes, pair, older = lax.optimization_barrier((codes, pair, older))
+            arrived = older + arrived[ring - 3 :]
+            arrived.append(shift(pair, "rows", -k))
+    near, got = waiting[-1]
+    got, early = lax.optimization_barrier((got, arrived[:-1]))
+    arrived = early + arrived[-1:]
+    outputs = near + got
+    for pair in arrived:
+        outputs = outputs + pair
+    outputs = outputs.astype(bf16)
+
+    same = [outputs] + [shift(outputs, "rows", k) for k in range(1, ring)]
+    pieces = same + [swap(piece, "rows", 1) for piece in same]
 
     def terms(first, here, pieces):
         where = jnp.stack([position, side, first])
-        return backward(codes, where, near_jac, far_jac, pieces, blocks_here, here, capacity)
+        return backward(codes, where, jac, pieces, blocks_here, here, capacity)
 
     half = blocks_here // 2
     wide = half // 2 * BLK_P

time: 159 us -> 144 us (0.906)
  starting transfers between devices: 46.9 us -> 30 us
  Pallas kernels: 36.8 us -> 53.3 us
  waiting for transfers between devices: 63.2 us -> 48.8 us
    ppermute x11 -> x13, starting transfers between devices: 33 us -> 13.4 us  [swap(): lax.ppermute(array, axis, [(i, i ^ bit) for i in range(lax.axis_size(axis...]
    ppermute x6, waiting for transfers between devices: 28.6 us -> 10.2 us  [shift(): lax.ppermute(array, axis, [(i, (i + 2 * steps) % size) for i in range(siz...]
    pallas_call x2 -> x4, Pallas kernels: 17.9 us -> 29.8 us  [forward(): pl.pallas_call(functools.partial(forward_kernel, blocks, capacity), out_s...]
    pallas_call x3, Pallas kernels: 16.3 us -> 20.8 us  [backward(): pl.pallas_call(functools.partial(kernel, blocks, capacity, total // 2), o...]
    ppermute x11 -> x13, waiting for transfers between devices: 29.2 us -> 33.2 us  [swap(): lax.ppermute(array, axis, [(i, i ^ bit) for i in range(lax.axis_size(axis...]
    ppermute x6, starting transfers between devices: 6.65 us -> 9.37 us  [shift(): lax.ppermute(array, axis, [(i, (i + 2 * steps) % size) for i in range(siz...]
  transfers between devices with their start and end apart: 18 -> 20, of which waited for: 13 -> 12; matrix products, arithmetic and copies ran while one was open for 2% -> 3% of each run, Pallas kernels for 12% -> 23%
where the time goes in v2:
time: 144 us
  Pallas kernels  53.3 us (37%)
  waiting for transfers between devices  48.8 us (34%)
  starting transfers between devices  30 us (21%)
  other arithmetic  10 us (7%)
    ppermute x13, waiting for transfers between devices, swap(): lax.ppermute(array, axis, [(i, i ^ bit) for i in range(lax.axis_size(axis...  33.2 us
    pallas_call x4, Pallas kernels, forward(): pl.pallas_call(functools.partial(forward_kernel, blocks, capacity), out_s...  29.8 us
    pallas_call x3, Pallas kernels, backward(): pl.pallas_call(functools.partial(kernel, blocks, capacity, total // 2), o...  20.8 us
    ppermute x13, starting transfers between devices, swap(): lax.ppermute(array, axis, [(i, i ^ bit) for i in range(lax.axis_size(axis...  13.4 us
    ppermute x6, waiting for transfers between devices, shift(): lax.ppermute(array, axis, [(i, (i + 2 * steps) % size) for i in range(siz...  10.2 us
    ppermute x6, starting transfers between devices, shift(): lax.ppermute(array, axis, [(i, (i + 2 * steps) % size) for i in range(siz...  9.37 us
    all_to_all x1, starting transfers between devices, body(): left = lax.all_to_all(send, 'rows', split_axis=0, concat_axis=0, tiled=True)  7.25 us
    all_to_all x1, waiting for transfers between devices, body(): left = lax.all_to_all(send, 'rows', split_axis=0, concat_axis=0, tiled=True)  5.44 us
  transfers between devices with their start and end apart: 20, of which 12 were waited for; matrix products, arithmetic and copies ran while one was open for 3% of the time, Pallas kernels for 23%

profile of v2, /device:TPU:0, one launch (start us, length us, event | category | flops | bytes accessed | tf_op | source)
XLA Modules:
  0.0 144.3 jit_solution(13644303080930864839)
XLA Ops:
  0.8 0.9 select_reduce_fusion
  1.7 0.7 compare_select_fusion.4
  2.3 0.2 convert_reduce_fusion
  2.5 0.1 select_reduce_fusion.1
  2.7 0.1 convert_element_type.66
  2.7 0.7 stack.108
  3.4 0.7 fusion.11
  4.1 0.1 stack.91
  4.2 0.7 fusion.5
  4.9 7.3 %all-to-all-start = ((bf16[8,8,1024]{2,1,0:T(8,128)(2,1)}), bf16[8,8,1024]{2,1,0:T(8,128)(2,1)S(1)}, u32[]{:S(2)}, u32[]{:S(2)}) async-start(bf16[8,8,1024]{2,1,0:T(8,128)(2,1)} %fusion.5), calls=%async_computation | async-start | bytes 262144 | tf_op jit(solution)/shard_map/all_to_all | solution.py:333
  12.2 0.8 broadcast_in_dim.90
  13.0 0.8 multiply_convert_fusion
  13.8 0.1 broadcast_select_fusion
  13.9 0.1 pad_add_fusion
  14.0 0.1 pad_maximum_fusion.right
  14.1 5.4 %all-to-all-done.left = bf16[8,8,1024]{2,1,0:T(8,128)(2,1)S(1)} async-done(((bf16[8,8,1024]{2,1,0:T(8,128)(2,1)}), bf16[8,8,1024]{2,1,0:T(8,128)(2,1)S(1)}, u32[]{:S(2)}, u32[]{:S(2)}) %all-to-all-start) | async-done | bytes 131104 | tf_op jit(solution)/shard_map/all_to_all | solution.py:333
  19.5 0.1 reshape.102.codes.refs_0_
  19.6 8.6 %forward.4 = (f32[64,1024]{1,0:T(8,128)S(1)}, f32[64,1024]{1,0:T(8,128)S(1)}, bf16[129,256,512]{2,1,0:T(8,128)(2,1)}) custom-call(s32[128]{0:T(128)S(1)} %reshape.102.codes.refs_0_, s32[2]{0:T(128)S(1)} %get-tuple-element.73.where, bf16[8,8,1024]{2,1,0:T(8,128)(2,1)S(1)} %all-to-all-done.left, bf16[32,8,1024]{2,1,0:T(8,128)(2,1)S(1)} %pad_maximum_fusion.right, ...), custom_call_target="tpu_custom_call" | custom-call | flops 32 | bytes 64 | tf_op jit(solution)/shard_map/forward/pallas_call | solution.py:148
  28.2 0.1 collective-permute-start
  28.3 3.2 %forward.5 = (f32[64,1024]{1,0:T(8,128)S(1)}, f32[64,1024]{1,0:T(8,128)S(1)}, bf16[129,256,512]{2,1,0:T(8,128)(2,1)}) custom-call(s32[128]{0:T(128)S(1)} %reshape.102.codes.refs_0_, s32[2]{0:T(128)S(1)} %get-tuple-element.74.where, bf16[8,8,1024]{2,1,0:T(8,128)(2,1)S(1)} %all-to-all-done.left, ...), custom_call_target="tpu_custom_call", output_to_operand_aliasing={{2}: (5, {})} | custom-call | flops 32 | bytes 64 | tf_op jit(solution)/shard_map/forward/pallas_call | solution.py:148
  31.5 3.6 %collective-permute-start.1 = (f32[64,1024]{1,0:T(8,128)S(1)}, f32[64,1024]{1,0:T(8,128)S(1)}, u32[]{:S(2)}, u32[]{:S(2)}) collective-permute-start(f32[64,1024]{1,0:T(8,128)S(1)} %get-tuple-element.39), channel_id=1, source_target_pairs={{0,4},{4,0},{8,12},{12,8},{16,20},{20,16},{24,28},{28,24},{1,5},{5... | collective-permute-start | bytes 786440 | tf_op jit(solution)/shard_map/ppermute | solution.py:279
  35.1 0.1 collective-permute-done
  35.3 0.1 collective-permute-start.2
  35.3 0.1 pad_add_fusion.2
  35.4 6.3 %forward.6 = (f32[64,1024]{1,0:T(8,128)S(1)}, f32[64,1024]{1,0:T(8,128)S(1)}, bf16[129,256,512]{2,1,0:T(8,128)(2,1)}) custom-call(s32[128]{0:T(128)S(1)} %reshape.102.codes.refs_0_, s32[2]{0:T(128)S(1)} %get-tuple-element.75.where, bf16[8,8,1024]{2,1,0:T(8,128)(2,1)S(1)} %all-to-all-done.left, ...), custom_call_target="tpu_custom_call", output_to_operand_aliasing={{2}: (5, {})} | custom-call | flops 32 | bytes 64 | tf_op jit(solution)/shard_map/forward/pallas_call | solution.py:148
  41.7 1.5 %collective-permute-start.3 = (f32[64,1024]{1,0:T(8,128)S(1)}, f32[64,1024]{1,0:T(8,128)S(1)}, u32[]{:S(2)}, u32[]{:S(2)}) collective-permute-start(f32[64,1024]{1,0:T(8,128)S(1)} %get-tuple-element.44), channel_id=1, source_target_pairs={{0,4},{4,0},{8,12},{12,8},{16,20},{20,16},{24,28},{28,24},{1,5},{5... | collective-permute-start | bytes 786440 | tf_op jit(solution)/shard_map/ppermute | solution.py:279
  43.3 0.0 collective-permute-done.1
  43.3 4.2 %collective-permute-done.2 = f32[64,1024]{1,0:T(8,128)S(1)} collective-permute-done((f32[64,1024]{1,0:T(8,128)S(1)}, f32[64,1024]{1,0:T(8,128)S(1)}, u32[]{:S(2)}, u32[]{:S(2)}) %collective-permute-start.2) | collective-permute-done | bytes 262176 | tf_op jit(solution)/shard_map/ppermute | solution.py:284
  47.5 7.2 %collective-permute-start.5 = (f32[64,1024]{1,0:T(8,128)S(1)}, f32[64,1024]{1,0:T(8,128)S(1)}, u32[]{:S(2)}, u32[]{:S(2)}) collective-permute-start(f32[64,1024]{1,0:T(8,128)S(1)} %add.126), channel_id=1, source_target_pairs={{0,16},{4,20},{8,24},{12,28},{16,0},{20,4},{24,8},{28,12},{1,17},{... | collective-permute-start | bytes 786440 | tf_op jit(solution)/shard_map/ppermute | solution.py:284
  54.7 11.7 %forward.7 = (f32[64,1024]{1,0:T(8,128)S(1)}, f32[64,1024]{1,0:T(8,128)S(1)}, bf16[129,256,512]{2,1,0:T(8,128)(2,1)}) custom-call(s32[128]{0:T(128)S(1)} %reshape.102.codes.refs_0_, s32[2]{0:T(128)S(1)} %get-tuple-element.76.where, bf16[8,8,1024]{2,1,0:T(8,128)(2,1)S(1)} %all-to-all-done.left, ...), custom_call_target="tpu_custom_call", output_to_operand_aliasing={{2}: (5, {})} | custom-call | flops 32 | bytes 64 | tf_op jit(solution)/shard_map/forward/pallas_call | solution.py:148
  66.4 0.1 collective-permute-start.4
  66.6 0.1 collective-permute-start.6
  66.6 6.2 %collective-permute-done.4 = f32[64,1024]{1,0:T(8,128)S(1)} collective-permute-done((f32[64,1024]{1,0:T(8,128)S(1)}, f32[64,1024]{1,0:T(8,128)S(1)}, u32[]{:S(2)}, u32[]{:S(2)}) %collective-permute-start.4) | collective-permute-done | bytes 262176 | tf_op jit(solution)/shard_map/ppermute | solution.py:279
  72.9 4.2 %collective-permute-done.6 = f32[64,1024]{1,0:T(8,128)S(1)} collective-permute-done((f32[64,1024]{1,0:T(8,128)S(1)}, f32[64,1024]{1,0:T(8,128)S(1)}, u32[]{:S(2)}, u32[]{:S(2)}) %collective-permute-start.6) | collective-permute-done | bytes 262176 | tf_op jit(solution)/shard_map/ppermute | solution.py:284
  77.0 0.1 add_convert_fusion.refs_0_
  77.1 0.1 collective-permute-start.9
  77.2 0.1 collective-permute-start.8
  77.3 1.9 %collective-permute-start.7 = (bf16[64,1024]{1,0:T(8,128)(2,1)S(1)}, bf16[64,1024]{1,0:T(8,128)(2,1)S(1)}, u32[]{:S(2)}, u32[]{:S(2)}) collective-permute-start(bf16[64,1024]{1,0:T(8,128)(2,1)S(1)} %add_convert_fusion.refs_0_), channel_id=1, source_target_pairs={{0,8},{4,12},{8,16},{12,20},{16,24},{20,28},{24,0},{28,4},{1,9},{5... | collective-permute-start | bytes 393224 | tf_op jit(solution)/shard_map/ppermute | solution.py:284
  79.2 2.5 %collective-permute-start.10 = (bf16[64,1024]{1,0:T(8,128)(2,1)S(1)}, bf16[64,1024]{1,0:T(8,128)(2,1)S(1)}, u32[]{:S(2)}, u32[]{:S(2)}) collective-permute-start(bf16[64,1024]{1,0:T(8,128)(2,1)S(1)} %add_convert_fusion.refs_0_), channel_id=1, source_target_pairs={{0,4},{4,0},{8,12},{12,8},{16,20},{20,16},{24,28},{28,24},{1,5},{5... | collective-permute-start | bytes 393224 | tf_op jit(solution)/shard_map/ppermute | solution.py:279
  81.7 1.8 %collective-permute-done.9.refs_3_ = bf16[64,1024]{1,0:T(8,128)(2,1)S(1)} collective-permute-done((bf16[64,1024]{1,0:T(8,128)(2,1)S(1)}, bf16[64,1024]{1,0:T(8,128)(2,1)S(1)}, u32[]{:S(2)}, u32[]{:S(2)}) %collective-permute-start.9) | collective-permute-done | bytes 131104 | tf_op jit(solution)/shard_map/ppermute | solution.py:284
  83.6 2.5 %collective-permute-start.13 = (bf16[64,1024]{1,0:T(8,128)(2,1)S(1)}, bf16[64,1024]{1,0:T(8,128)(2,1)S(1)}, u32[]{:S(2)}, u32[]{:S(2)}) collective-permute-start(bf16[64,1024]{1,0:T(8,128)(2,1)S(1)} %collective-permute-done.9.refs_3_), channel_id=1, source_target_pairs={{0,4},{4,0},{8,12},{12,8},{16,20},{20,16},{24,28},{28,24},{1,5},{5... | collective-permute-start | bytes 393224 | tf_op jit(solution)/shard_map/ppermute | solution.py:279
  86.1 0.0 collective-permute-start.12
  86.1 2.4 %collective-permute-start.11 = (bf16[64,1024]{1,0:T(8,128)(2,1)S(1)}, bf16[64,1024]{1,0:T(8,128)(2,1)S(1)}, u32[]{:S(2)}, u32[]{:S(2)}) collective-permute-start(bf16[64,1024]{1,0:T(8,128)(2,1)S(1)} %collective-permute-done.7.refs_1_), channel_id=1, source_target_pairs={{0,4},{4,0},{8,12},{12,8},{16,20},{20,16},{24,28},{28,24},{1,5},{5... | collective-permute-start | bytes 393224 | tf_op jit(solution)/shard_map/ppermute | solution.py:279
  88.5 0.1 pad_add_fusion.6.where
  88.6 0.4 collective-permute-done.13.refs_7_
  89.0 2.0 %collective-permute-done.12.refs_6_ = bf16[64,1024]{1,0:T(8,128)(2,1)S(1)} collective-permute-done((bf16[64,1024]{1,0:T(8,128)(2,1)S(1)}, bf16[64,1024]{1,0:T(8,128)(2,1)S(1)}, u32[]{:S(2)}, u32[]{:S(2)}) %collective-permute-start.12) | collective-permute-done | bytes 131104 | tf_op jit(solution)/shard_map/ppermute | solution.py:279
  91.1 1.4 collective-permute-done.11.refs_5_
  92.5 10.2 %backward.3 = (f32[64,8192]{1,0:T(8,128)}, bf16[8,64,1024]{2,1,0:T(8,128)(2,1)S(1)}) custom-call(s32[128]{0:T(128)S(1)} %reshape.102.codes.refs_0_, s32[3]{0:T(128)S(1)} %pad_add_fusion.6.where, bf16[129,256,512]{2,1,0:T(8,128)(2,1)} %get-tuple-element.48.jac.refs_2_, bf16[64,1024]{1,0:T(8,128)(2,1)S(1)} %add_convert_fusion.refs_0_, ...), custom_call_target="tpu_custom_call" | custom-call | flops 16 | bytes 64 | tf_op jit(solution)/shard_map/backward/pallas_call | solution.py:229
  102.7 0.1 collective-permute-start.14
  102.8 0.1 pad_add_fusion.3.refs_1_
  102.8 5.6 %backward.4 = f32[64,4096]{1,0:T(8,128)S(1)} custom-call(s32[128]{0:T(128)S(1)} %reshape.102.codes.refs_0_, s32[3]{0:T(128)S(1)} %pad_add_fusion.3.refs_1_, bf16[129,256,512]{2,1,0:T(8,128)(2,1)} %get-tuple-element.48.jac.refs_2_, bf16[8,64,1024]{2,1,0:T(8,128)(2,1)S(1)} %get-tuple-element.57.refs_3_), custom_call_target="tpu_custom_call" | custom-call | flops 16 | bytes 64 | tf_op jit(solution)/shard_map/backward/pallas_call | solution.py:229
  108.4 1.3 fusion.2
  109.7 0.1 collective-permute-start.15
  109.8 0.1 pad_add_fusion.7.refs_1_
  109.9 5.0 %backward.5 = f32[64,4096]{1,0:T(8,128)S(1)} custom-call(s32[128]{0:T(128)S(1)} %reshape.102.codes.refs_0_, s32[3]{0:T(128)S(1)} %pad_add_fusion.7.refs_1_, bf16[129,256,512]{2,1,0:T(8,128)(2,1)} %get-tuple-element.48.jac.refs_2_, bf16[8,64,1024]{2,1,0:T(8,128)(2,1)S(1)} %get-tuple-element.57.refs_3_), custom_call_target="tpu_custom_call" | custom-call | flops 16 | bytes 64 | tf_op jit(solution)/shard_map/backward/pallas_call | solution.py:229
  114.9 9.0 %collective-permute-done.15 = bf16[64,4096]{1,0:T(8,128)(2,1)S(1)} collective-permute-done((bf16[64,4096]{1,0:T(8,128)(2,1)S(1)}, bf16[64,4096]{1,0:T(8,128)(2,1)S(1)}, u32[]{:S(2)}, u32[]{:S(2)}) %collective-permute-start.15) | collective-permute-done | bytes 524320 | tf_op jit(solution)/shard_map/ppermute | solution.py:279
  123.9 1.9 %convert_add_fusion.1 = (f32[64,4096]{1,0:T(8,128)S(1)}, bf16[64,4096]{1,0:T(8,128)(2,1)S(1)}) fusion(bf16[64,4096]{1,0:T(8,128)(2,1)S(1)} %collective-permute-done.15, f32[64,4096]{1,0:T(8,128)S(1)} %backward.4, f32[64,8192]{1,0:T(8,128)} %collective-permute-done.14, f32[64,4096]{1,0:T(8,128)S(1)} %backward.5), kind=kLoop, calls=%fused_computation.5 | loop fusion | flops 1835008 | bytes 6291456 | tf_op jit(solution)/shard_map/add | solution.py:394
  125.8 0.4 collective-permute-start.17
  126.2 13.0 %collective-permute-done.17 = bf16[64,4096]{1,0:T(8,128)(2,1)S(1)} collective-permute-done((bf16[64,4096]{1,0:T(8,128)(2,1)S(1)}, bf16[64,4096]{1,0:T(8,128)(2,1)S(1)}, u32[]{:S(2)}, u32[]{:S(2)}) %collective-permute-start.17) | collective-permute-done | bytes 524320 | tf_op jit(solution)/shard_map/ppermute | solution.py:279
  139.2 1.4 convert_add_fusion.refs_2_
  140.6 0.1 collective-permute-start.18
  140.7 1.7 %place.2.refs_0_ = f32[64,16384]{1,0:T(8,128)} custom-call(s32[1]{0:T(128)} %bitcast.where, f32[64,4096]{1,0:T(8,128)S(1)} %get-tuple-element.61.refs_0_, f32[64,4096]{1,0:T(8,128)S(1)} %collective-permute-done.16.refs_1_, f32[64,4096]{1,0:T(8,128)S(1)} %convert_add_fusion.refs_2_), custom_call_target="tpu_custom_call" | custom-call | tf_op jit(solution)/shard_map/place/pallas_call | solution.py:266
  142.4 0.9 collective-permute-done.18.refs_1_
  143.3 1.0 place.3
  (20 shorter events, 0.2 us)
Async XLA Ops:
  0.0 19.6 %copy-start = (bf16[64,16384]{1,0:T(8,128)(2,1)S(1)}, bf16[64,16384]{1,0:T(8,128)(2,1)}, u32[]{:S(2)}) copy-start(bf16[64,16384]{1,0:T(8,128)(2,1)} %vectors.7) | copy-start | bytes 6291460
  4.9 14.6 %all-to-all-start = ((bf16[8,8,1024]{2,1,0:T(8,128)(2,1)}), bf16[8,8,1024]{2,1,0:T(8,128)(2,1)S(1)}, u32[]{:S(2)}, u32[]{:S(2)}) async-start(bf16[8,8,1024]{2,1,0:T(8,128)(2,1)} %fusion.5), calls=%async_computation | async-start | bytes 262144 | tf_op jit(solution)/shard_map/all_to_all | solution.py:333
  28.2 7.0 %collective-permute-start = (f32[64,1024]{1,0:T(8,128)S(1)}, f32[64,1024]{1,0:T(8,128)S(1)}, u32[]{:S(2)}, u32[]{:S(2)}) collective-permute-start(f32[64,1024]{1,0:T(8,128)S(1)} %get-tuple-element.35), channel_id=1, source_target_pairs={{0,4},{4,0},{8,12},{12,8},{16,20},{20,16},{24,28},{28,24},{1,5},{5... | collective-permute-start | bytes 786440 | tf_op jit(solution)/shard_map/ppermute | solution.py:279
  31.5 11.7 %collective-permute-start.1 = (f32[64,1024]{1,0:T(8,128)S(1)}, f32[64,1024]{1,0:T(8,128)S(1)}, u32[]{:S(2)}, u32[]{:S(2)}) collective-permute-start(f32[64,1024]{1,0:T(8,128)S(1)} %get-tuple-element.39), channel_id=1, source_target_pairs={{0,4},{4,0},{8,12},{12,8},{16,20},{20,16},{24,28},{28,24},{1,5},{5... | collective-permute-start | bytes 786440 | tf_op jit(solution)/shard_map/ppermute | solution.py:279
  35.3 12.2 %collective-permute-start.2 = (f32[64,1024]{1,0:T(8,128)S(1)}, f32[64,1024]{1,0:T(8,128)S(1)}, u32[]{:S(2)}, u32[]{:S(2)}) collective-permute-start(f32[64,1024]{1,0:T(8,128)S(1)} %add.124), channel_id=1, source_target_pairs={{0,24},{4,28},{8,0},{12,4},{16,8},{20,12},{24,16},{28,20},{1,25},{... | collective-permute-start | bytes 786440 | tf_op jit(solution)/shard_map/ppermute | solution.py:284
  41.7 24.8 %collective-permute-start.3 = (f32[64,1024]{1,0:T(8,128)S(1)}, f32[64,1024]{1,0:T(8,128)S(1)}, u32[]{:S(2)}, u32[]{:S(2)}) collective-permute-start(f32[64,1024]{1,0:T(8,128)S(1)} %get-tuple-element.44), channel_id=1, source_target_pairs={{0,4},{4,0},{8,12},{12,8},{16,20},{20,16},{24,28},{28,24},{1,5},{5... | collective-permute-start | bytes 786440 | tf_op jit(solution)/shard_map/ppermute | solution.py:279
  47.5 19.2 %collective-permute-start.5 = (f32[64,1024]{1,0:T(8,128)S(1)}, f32[64,1024]{1,0:T(8,128)S(1)}, u32[]{:S(2)}, u32[]{:S(2)}) collective-permute-start(f32[64,1024]{1,0:T(8,128)S(1)} %add.126), channel_id=1, source_target_pairs={{0,16},{4,20},{8,24},{12,28},{16,0},{20,4},{24,8},{28,12},{1,17},{... | collective-permute-start | bytes 786440 | tf_op jit(solution)/shard_map/ppermute | solution.py:284
  66.4 6.4 %collective-permute-start.4 = (f32[64,1024]{1,0:T(8,128)S(1)}, f32[64,1024]{1,0:T(8,128)S(1)}, u32[]{:S(2)}, u32[]{:S(2)}) collective-permute-start(f32[64,1024]{1,0:T(8,128)S(1)} %get-tuple-element.50), channel_id=1, source_target_pairs={{0,4},{4,0},{8,12},{12,8},{16,20},{20,16},{24,28},{28,24},{1,5},{5... | collective-permute-start | bytes 786440 | tf_op jit(solution)/shard_map/ppermute | solution.py:279
  66.6 10.5 %collective-permute-start.6 = (f32[64,1024]{1,0:T(8,128)S(1)}, f32[64,1024]{1,0:T(8,128)S(1)}, u32[]{:S(2)}, u32[]{:S(2)}) collective-permute-start(f32[64,1024]{1,0:T(8,128)S(1)} %add.128), channel_id=1, source_target_pairs={{0,8},{4,12},{8,16},{12,20},{16,24},{20,28},{24,0},{28,4},{1,9},{5... | collective-permute-start | bytes 786440 | tf_op jit(solution)/shard_map/ppermute | solution.py:284
  77.1 6.4 %collective-permute-start.9 = (bf16[64,1024]{1,0:T(8,128)(2,1)S(1)}, bf16[64,1024]{1,0:T(8,128)(2,1)S(1)}, u32[]{:S(2)}, u32[]{:S(2)}) collective-permute-start(bf16[64,1024]{1,0:T(8,128)(2,1)S(1)} %add_convert_fusion.refs_0_), channel_id=1, source_target_pairs={{0,24},{4,28},{8,0},{12,4},{16,8},{20,12},{24,16},{28,20},{1,25},{... | collective-permute-start | bytes 393224 | tf_op jit(solution)/shard_map/ppermute | solution.py:284
  77.2 8.9 %collective-permute-start.8 = (bf16[64,1024]{1,0:T(8,128)(2,1)S(1)}, bf16[64,1024]{1,0:T(8,128)(2,1)S(1)}, u32[]{:S(2)}, u32[]{:S(2)}) collective-permute-start(bf16[64,1024]{1,0:T(8,128)(2,1)S(1)} %add_convert_fusion.refs_0_), channel_id=1, source_target_pairs={{0,16},{4,20},{8,24},{12,28},{16,0},{20,4},{24,8},{28,12},{1,17},{... | collective-permute-start | bytes 393224 | tf_op jit(solution)/shard_map/ppermute | solution.py:284
  77.3 8.9 %collective-permute-start.7 = (bf16[64,1024]{1,0:T(8,128)(2,1)S(1)}, bf16[64,1024]{1,0:T(8,128)(2,1)S(1)}, u32[]{:S(2)}, u32[]{:S(2)}) collective-permute-start(bf16[64,1024]{1,0:T(8,128)(2,1)S(1)} %add_convert_fusion.refs_0_), channel_id=1, source_target_pairs={{0,8},{4,12},{8,16},{12,20},{16,24},{20,28},{24,0},{28,4},{1,9},{5... | collective-permute-start | bytes 393224 | tf_op jit(solution)/shard_map/ppermute | solution.py:284
  79.2 9.4 %collective-permute-start.10 = (bf16[64,1024]{1,0:T(8,128)(2,1)S(1)}, bf16[64,1024]{1,0:T(8,128)(2,1)S(1)}, u32[]{:S(2)}, u32[]{:S(2)}) collective-permute-start(bf16[64,1024]{1,0:T(8,128)(2,1)S(1)} %add_convert_fusion.refs_0_), channel_id=1, source_target_pairs={{0,4},{4,0},{8,12},{12,8},{16,20},{20,16},{24,28},{28,24},{1,5},{5... | collective-permute-start | bytes 393224 | tf_op jit(solution)/shard_map/ppermute | solution.py:279
  83.6 5.5 %collective-permute-start.13 = (bf16[64,1024]{1,0:T(8,128)(2,1)S(1)}, bf16[64,1024]{1,0:T(8,128)(2,1)S(1)}, u32[]{:S(2)}, u32[]{:S(2)}) collective-permute-start(bf16[64,1024]{1,0:T(8,128)(2,1)S(1)} %collective-permute-done.9.refs_3_), channel_id=1, source_target_pairs={{0,4},{4,0},{8,12},{12,8},{16,20},{20,16},{24,28},{28,24},{1,5},{5... | collective-permute-start | bytes 393224 | tf_op jit(solution)/shard_map/ppermute | solution.py:279
  86.1 5.0 %collective-permute-start.12 = (bf16[64,1024]{1,0:T(8,128)(2,1)S(1)}, bf16[64,1024]{1,0:T(8,128)(2,1)S(1)}, u32[]{:S(2)}, u32[]{:S(2)}) collective-permute-start(bf16[64,1024]{1,0:T(8,128)(2,1)S(1)} %collective-permute-done.8.refs_2_), channel_id=1, source_target_pairs={{0,4},{4,0},{8,12},{12,8},{16,20},{20,16},{24,28},{28,24},{1,5},{5... | collective-permute-start | bytes 393224 | tf_op jit(solution)/shard_map/ppermute | solution.py:279
  86.1 6.3 %collective-permute-start.11 = (bf16[64,1024]{1,0:T(8,128)(2,1)S(1)}, bf16[64,1024]{1,0:T(8,128)(2,1)S(1)}, u32[]{:S(2)}, u32[]{:S(2)}) collective-permute-start(bf16[64,1024]{1,0:T(8,128)(2,1)S(1)} %collective-permute-done.7.refs_1_), channel_id=1, source_target_pairs={{0,4},{4,0},{8,12},{12,8},{16,20},{20,16},{24,28},{28,24},{1,5},{5... | collective-permute-start | bytes 393224 | tf_op jit(solution)/shard_map/ppermute | solution.py:279
  102.7 5.7 %collective-permute-start.14 = (f32[64,8192]{1,0:T(8,128)}, f32[64,8192]{1,0:T(8,128)}, u32[]{:S(2)}, u32[]{:S(2)}) collective-permute-start(f32[64,8192]{1,0:T(8,128)} %get-tuple-element.58), channel_id=1, source_target_pairs={{0,1},{1,0},{2,3},{3,2},{4,5},{5,4},{6,7},{7,6},{8,9},{9,8},{10,11... | collective-permute-start | bytes 6291464 | tf_op jit(solution)/shard_map/ppermute | solution.py:279
  109.7 14.2 %collective-permute-start.15 = (bf16[64,4096]{1,0:T(8,128)(2,1)S(1)}, bf16[64,4096]{1,0:T(8,128)(2,1)S(1)}, u32[]{:S(2)}, u32[]{:S(2)}) collective-permute-start(bf16[64,4096]{1,0:T(8,128)(2,1)S(1)} %fusion.2), channel_id=1, source_target_pairs={{0,2},{1,3},{2,0},{3,1},{4,6},{5,7},{6,4},{7,5},{8,10},{9,11},{10,... | collective-permute-start | bytes 1572872 | tf_op jit(solution)/shard_map/ppermute | solution.py:279
  125.8 13.4 %collective-permute-start.17 = (bf16[64,4096]{1,0:T(8,128)(2,1)S(1)}, bf16[64,4096]{1,0:T(8,128)(2,1)S(1)}, u32[]{:S(2)}, u32[]{:S(2)}) collective-permute-start(bf16[64,4096]{1,0:T(8,128)(2,1)S(1)} %get-tuple-element.62), channel_id=1, source_target_pairs={{0,2},{1,3},{2,0},{3,1},{4,6},{5,7},{6,4},{7,5},{8,10},{9,11},{10,... | collective-permute-start | bytes 1572872 | tf_op jit(solution)/shard_map/ppermute | solution.py:279
  126.1 14.5 %collective-permute-start.16 = (f32[64,4096]{1,0:T(8,128)S(1)}, f32[64,4096]{1,0:T(8,128)S(1)}, u32[]{:S(2)}, u32[]{:S(2)}) collective-permute-start(f32[64,4096]{1,0:T(8,128)S(1)} %get-tuple-element.61.refs_0_), channel_id=1, source_target_pairs={{0,1},{1,0},{2,3},{3,2},{4,5},{5,4},{6,7},{7,6},{8,9},{9,8},{10,11... | collective-permute-start | bytes 3145736 | tf_op jit(solution)/shard_map/ppermute | solution.py:279
  140.6 2.7 %collective-permute-start.18 = (f32[64,4096]{1,0:T(8,128)S(1)}, f32[64,4096]{1,0:T(8,128)S(1)}, u32[]{:S(2)}, u32[]{:S(2)}) collective-permute-start(f32[64,4096]{1,0:T(8,128)S(1)} %convert_add_fusion.refs_2_), channel_id=1, source_target_pairs={{0,1},{1,0},{2,3},{3,2},{4,5},{5,4},{6,7},{7,6},{8,9},{9,8},{10,11... | collective-permute-start | bytes 3145736 | tf_op jit(solution)/shard_map/ppermute | solution.py:279

commit v3 on v2

--- a/solution.py
+++ b/solution.py
@@ -23,7 +23,6 @@
     -1.8835629903409246,
     0.3106981920279389,
 )
-ROUNDER = 12582912.0
 
 
 def turn_constants():
@@ -59,28 +58,26 @@
     return pl.CostEstimate(flops=entries, bytes_accessed=vector_count, transcendentals=0)
 
 
-def forward_kernel(blocks, capacity, codes, where, left, right, vectors, *refs):
+def forward_kernel(blocks, capacity, stage, codes, left, right, vectors, *refs):
     near, far, jac, todo, part, even, odd, sems = refs[-8:]
     spare = codes.shape[0]
     part[...] = jnp.zeros_like(part)
-    start = 2 * capacity * where[0]
+    start = 2 * capacity * stage
     found = collect(codes, todo, start, 2 * capacity, lambda code: True)
     steps = (found + 1) // 2
 
     def decode(place):
         code = codes[place]
-        group = lax.div(place, capacity)
-        away = jnp.where(lax.rem(group, 2) == where[1], 0, 1)
-        return lax.rem(code, blocks), lax.div(code, blocks), group, away
+        return lax.rem(code, blocks), lax.div(code, blocks), lax.div(place - start, capacity)
 
     def make(buffer, place):
-        block, row, group, _ = decode(place)
-        angles = left[group, :, pl.ds(pl.multiple_of(row * BLK_R, BLK_R), BLK_R)]
+        block, row, away = decode(place)
+        angles = left[2 * stage + away, :, pl.ds(pl.multiple_of(row * BLK_R, BLK_R), BLK_R)]
         both = lax.dot_general(
             angles, right[block], (((0,), (0,)), ((), ())), preferred_element_type=f32
         )
         turns, weight = both[:, :BLK_P], both[:, BLK_P:]
-        rest = turns - ((turns + ROUNDER) - ROUNDER)
+        rest = turns - jnp.round(turns)
         square = rest * rest
         root = COS_POLY[4] * square + COS_POLY[3]
         for k in (2, 1, 0):
@@ -88,7 +85,7 @@
         buffer[...] = (weight * (root * root - 1.0)).astype(bf16)
 
     def apply(buffer, place, keep):
-        block, row, _, away = decode(place)
+        block, row, away = decode(place)
         chosen = vectors[:, pl.ds(pl.multiple_of(block * BLK_P, BLK_P), BLK_P)]
         term = lax.dot_general(
             buffer[...], chosen, (((1,), (1,)), ((), ())), preferred_element_type=f32
@@ -119,7 +116,7 @@
         save(odd, parity, 1, jnp.where(paired, second, spare)).start()
         return second
 
-    last = lax.fori_loop(0, steps, step, 0)
+    last = lax.fori_loop(0, steps, step, todo[0])
 
     @pl.when((found > 0) & (lax.rem(found, 2) == 0))
     def _():
@@ -136,8 +133,8 @@
     far[...] = part[1]
 
 
-def forward(codes, where, left, right, vectors, capacity, jac):
-    _, _, width = left.shape
+def forward(codes, stage, left, right, vectors, capacity, jac):
+    width = left.shape[2]
     blocks = right.shape[0]
     room = codes.shape[0]
     count = vectors.shape[0]
@@ -146,10 +143,10 @@
     hbm = pl.BlockSpec(memory_space=pltpu.HBM)
     held = [] if jac is None else [jac]
     return pl.pallas_call(
-        functools.partial(forward_kernel, blocks, capacity),
+        functools.partial(forward_kernel, blocks, capacity, stage),
         out_shape=(jax.ShapeDtypeStruct((count, width), f32),) * 2
         + (pltpu.HBM((room + 1, BLK_R, BLK_P), bf16),),
-        in_specs=[smem, smem, vmem, vmem, vmem] + [hbm] * len(held),
+        in_specs=[smem, vmem, vmem, vmem] + [hbm] * len(held),
         out_specs=(vmem, vmem, hbm),
         scratch_shapes=[
             pltpu.SMEM((2 * capacity + 1,), jnp.int32),
@@ -158,21 +155,21 @@
             pltpu.VMEM((2, BLK_R, BLK_P), bf16),
             pltpu.SemaphoreType.DMA((2, 2)),
         ],
-        input_output_aliases={5: 2} if held else {},
+        input_output_aliases={4: 2} if held else {},
         compiler_params=pltpu.CompilerParams(vmem_limit_bytes=16 << 20),
         cost_estimate=entry_cost(2 * capacity, count),
         name="forward",
-    )(codes, where, left, right, vectors, *held)
-
-
-def backward_kernel(blocks, capacity, ring, codes, where, jac, *refs):
+    )(codes, left, right, vectors, *held)
+
+
+def backward_kernel(blocks, capacity, codes, first, jac, *refs):
     *pieces, out, gathered, todo, buffers, sems = refs
     here = out.shape[1] // BLK_P
     depth = buffers.shape[0]
 
     def wanted(code):
         block = lax.rem(code, blocks)
-        return (block >= where[2]) & (block < where[2] + here)
+        return (block >= first[0]) & (block < first[0] + here)
 
     found = collect(codes, todo, 0, codes.shape[0], wanted)
 
@@ -196,10 +193,8 @@
 
         place = todo[turn]
         code = codes[place]
-        block, row = lax.rem(code, blocks) - where[2], lax.div(code, blocks)
-        behind = lax.rem(where[0] - lax.div(place, 2 * capacity) + ring, ring)
-        near = lax.rem(lax.div(place, capacity), 2) == where[1]
-        piece = jnp.where(near, behind, ring + behind)
+        block, row = lax.rem(code, blocks) - first[0], lax.div(code, blocks)
+        piece = lax.div(place, capacity)
         chosen = gathered[piece, :, pl.ds(pl.multiple_of(row * BLK_R, BLK_R), BLK_R)]
         at = pl.ds(pl.multiple_of(block * BLK_P, BLK_P), BLK_P)
         slot = lax.rem(turn, depth)
@@ -210,12 +205,12 @@
     lax.fori_loop(0, found, step, 0)
 
 
-def joined_backward_kernel(blocks, capacity, ring, *refs):
+def joined_backward_kernel(blocks, capacity, *refs):
     *inputs, gathered, out, todo, buffers, sems = refs
-    backward_kernel(blocks, capacity, ring, *inputs, out, gathered, todo, buffers, sems)
-
-
-def backward(codes, where, jac, pieces, blocks, here, capacity):
+    backward_kernel(blocks, capacity, *inputs, out, gathered, todo, buffers, sems)
+
+
+def backward(codes, first, jac, pieces, blocks, here, capacity):
     joined = not isinstance(pieces, list)
     smem = pl.BlockSpec(memory_space=pltpu.SMEM)
     vmem = pl.BlockSpec(memory_space=pltpu.VMEM)
@@ -227,7 +222,7 @@
     gathered = jax.ShapeDtypeStruct((total, count, width), bf16)
     kernel = joined_backward_kernel if joined else backward_kernel
     result = pl.pallas_call(
-        functools.partial(kernel, blocks, capacity, total // 2),
+        functools.partial(kernel, blocks, capacity),
         out_shape=terms if joined else (terms, gathered),
         in_specs=[smem, smem, hbm] + [vmem] * len(sources),
         out_specs=vmem if joined else (vmem, vmem),
@@ -239,7 +234,7 @@
         compiler_params=pltpu.CompilerParams(vmem_limit_bytes=36 << 20),
         cost_estimate=entry_cost(codes.shape[0] // 8, count),
         name="backward",
-    )(codes, where, jac, *sources)
+    )(codes, first, jac, *sources)
     return (result, pieces) if joined else result
 
 
@@ -279,9 +274,9 @@
     return lax.ppermute(array, axis, [(i, i ^ bit) for i in range(lax.axis_size(axis))])
 
 
-def shift(array, axis, steps):
+def shift(array, axis, steps, bit=0):
     size = lax.axis_size(axis)
-    return lax.ppermute(array, axis, [(i, (i + 2 * steps) % size) for i in range(size)])
+    return lax.ppermute(array, axis, [(i, (i + 2 * steps) % size ^ bit) for i in range(size)])
 
 
 def body(
@@ -318,20 +313,22 @@
     wanted = (
         jnp.sum(jnp.where(target[None, :] == room_ids[:, None], code[None, :] + 1, 0), axis=1) - 1
     )
-    wanted = wanted.reshape(holders, 1, capacity).astype(f32)
-
-    angle_rows = jnp.stack(
-        angle_pieces(row_angle.astype(f32)) + [row_weight.astype(f32)], axis=0
+    wanted = jnp.pad(wanted.astype(f32), (0, width - slots))
+
+    mine = jnp.stack(
+        angle_pieces(row_angle.astype(f32)) + [row_weight.astype(f32), wanted], axis=0
+    ).astype(bf16)
+    ring = holders // 2
+    lefts = []
+    for k in range(1, ring + 1):
+        lefts.append(shift(mine, "rows", k) if k < ring else mine)
+        lefts.append(shift(mine, "rows", k % ring, 1))
+    left = lax.optimization_barrier(jnp.stack(lefts))
+    me = lax.axis_index("rows")
+    codes = lax.dynamic_slice(
+        left, (0, PIECES - 1, me * capacity), (holders, 1, capacity)
     )
-    send = jnp.concatenate(
-        [
-            jnp.broadcast_to(angle_rows[None], (holders, PIECES - 1, width)),
-            jnp.pad(wanted, ((0, 0), (0, 0), (0, width - capacity))),
-        ],
-        axis=1,
-    ).astype(bf16)
-    left = lax.all_to_all(send, "rows", split_axis=0, concat_axis=0, tiled=True)
-    codes = left[:, PIECES - 1, :capacity].astype(jnp.int32).reshape(holders * capacity)
+    codes = codes.astype(jnp.int32).reshape(holders * capacity)
 
     freq = wear_freq.reshape(blocks_here, 1, BLK_P)
     scale = (param_scale.astype(f32) * (1.0 / math.sqrt(8.0 * BLK_P))).astype(bf16)
@@ -344,17 +341,13 @@
         ],
         axis=2,
     )
-    me = lax.axis_index("rows")
     core = lax.axis_index("grp") % 2
-    side, position = me % 2, me // 2
-    ring = holders // 2
 
     jac = None
     waiting = []
     arrived = []
     for k in range(ring):
-        where = jnp.stack([(position + 2 * ring - 1 - k) % ring, side])
-        near, far, jac = forward(codes, where, left, right, vectors, capacity, jac)
+        near, far, jac = forward(codes, k, left, right, vectors, capacity, jac)
         waiting.append((near, swap(far, "rows", 1)))
         if k > 0:
             before, got = waiting[k - 1]
@@ -371,21 +364,19 @@
         outputs = outputs + pair
     outputs = outputs.astype(bf16)
 
-    same = [outputs] + [shift(outputs, "rows", k) for k in range(1, ring)]
-    pieces = same + [swap(piece, "rows", 1) for piece in same]
-
-    def terms(first, here, pieces):
-        where = jnp.stack([position, side, first])
-        return backward(codes, where, jac, pieces, blocks_here, here, capacity)
-
-    half = blocks_here // 2
-    wide = half // 2 * BLK_P
-    given, pieces = terms((1 - core) * half, half, pieces)
-    given = swap(given, "grp", 1)
+    same = [shift(outputs, "rows", k) for k in range(1, ring)] + [outputs]
+    pieces = [piece for near in same for piece in (near, swap(near, "rows", 1))]
+
+    def terms(first, pieces):
+        return backward(codes, first.reshape(1), jac, pieces, blocks_here, quarter, capacity)
+
+    quarter = blocks_here // 4
     sums = []
     for chunk in range(2):
-        kept, _ = terms(core * half + chunk * half // 2, half // 2, pieces)
-        chunk_sum = kept + given[:, chunk * wide : (chunk + 1) * wide]
+        given, pieces = terms((2 * (1 - core) + chunk) * quarter, pieces)
+        given = swap(given, "grp", 1)
+        kept, pieces = terms((2 * core + chunk) * quarter, pieces)
+        chunk_sum = kept + given
         bit = 2
         while bit < members:
             rounded = lax.reduce_precision(chunk_sum, 8, 7)

time: 144 us -> 146 us (1.014)
  Pallas kernels: 53.3 us -> 44.5 us
  starting transfers between devices: 30 us -> 34.8 us
  waiting for transfers between devices: 48.8 us -> 52 us
  local copies, waits for them, and re-layouts: 1.06 us -> 4.1 us
    ppermute x6 -> x13, waiting for transfers between devices: 10.2 us -> 23.7 us  [shift(): lax.ppermute(array, axis, [(i, (i + 2 * steps) % size ^ bit) for i in ran...]
    ppermute x6 -> x13, starting transfers between devices: 9.37 us -> 20.8 us  [shift(): lax.ppermute(array, axis, [(i, (i + 2 * steps) % size ^ bit) for i in ran...]
    pallas_call x7 -> x8, Pallas kernels: 50.6 us -> 41.8 us  [the longest x4 22.6 us: forward(): pl.pallas_call(functools.partial(forward_kernel, blocks, capacity, stage)...]
    all_to_all x1 -> x0, starting transfers between devices: 7.25 us -> none  [body(): left = lax.all_to_all(send, 'rows', split_axis=0, concat_axis=0, tiled=True)]
    all_to_all x1 -> x0, waiting for transfers between devices: 5.44 us -> none  [body(): left = lax.all_to_all(send, 'rows', split_axis=0, concat_axis=0, tiled=True)]
    ppermute x13 -> x14, waiting for transfers between devices: 33.2 us -> 28.3 us  [swap(): lax.ppermute(array, axis, [(i, i ^ bit) for i in range(lax.axis_size(axis...]
    convert_element_type x1 -> x2, other arithmetic: 1.32 us -> 3.48 us  [body(): sent = rounded.astype(bf16)]
    unnamed x2 -> x9, local copies, waits for them, and re-layouts: 0.01 us -> 1.61 us
  transfers between devices with their start and end apart: 20 -> 27, of which waited for: 12 -> 11; matrix products, arithmetic and copies ran while one was open for 3% -> 4% of each run, Pallas kernels for 23% -> 22%
where the time goes in v3:
time: 146 us; the launch traced here: 147 us
  waiting for transfers between devices  52 us (36%)
  Pallas kernels  44.5 us (30%)
  starting transfers between devices  34.8 us (24%)
  other arithmetic  10.2 us (7%)
  local copies, waits for them, and re-layouts  4.1 us (3%)
    ppermute x14, waiting for transfers between devices, swap(): lax.ppermute(array, axis, [(i, i ^ bit) for i in range(lax.axis_size(axis...  28.3 us
    ppermute x13, waiting for transfers between devices, shift(): lax.ppermute(array, axis, [(i, (i + 2 * steps) % size ^ bit) for i in ran...  23.7 us
    pallas_call x4, Pallas kernels, forward(): pl.pallas_call(functools.partial(forward_kernel, blocks, capacity, stage)...  22.6 us
    ppermute x13, starting transfers between devices, shift(): lax.ppermute(array, axis, [(i, (i + 2 * steps) % size ^ bit) for i in ran...  20.8 us
    pallas_call x4, Pallas kernels, backward(): pl.pallas_call(functools.partial(kernel, blocks, capacity), out_shape=ter...  19.2 us
    ppermute x14, starting transfers between devices, swap(): lax.ppermute(array, axis, [(i, i ^ bit) for i in range(lax.axis_size(axis...  14.1 us
    convert_element_type x2, other arithmetic, body(): sent = rounded.astype(bf16)  3.48 us
    add x2, other arithmetic, body(): chunk_sum = rounded + swap(sent, 'grp', bit).astype(f32)  2.94 us
  transfers between devices with their start and end apart: 27, of which 11 were waited for; matrix products, arithmetic and copies ran while one was open for 4% of the time, Pallas kernels for 22%

profile of v3, /device:TPU:0, one launch (start us, length us, event | category | flops | bytes accessed | tf_op | source)
XLA Modules:
  0.0 146.6 jit_solution(13269404557032753765)
XLA Ops:
  0.0 0.7 fusion.5
  0.8 0.7 stack.85
  2.1 0.9 select_reduce_fusion
  3.0 0.7 compare_select_fusion.4
  3.6 0.2 convert_reduce_fusion
  3.8 0.1 select_reduce_fusion.1
  4.0 0.1 stack.87
  4.0 3.1 %collective-permute-start = (bf16[8,1024]{1,0:T(8,128)(2,1)S(1)}, bf16[8,1024]{1,0:T(8,128)(2,1)S(1)}, u32[]{:S(2)}, u32[]{:S(2)}) collective-permute-start(bf16[8,1024]{1,0:T(8,128)(2,1)S(1)} %stack.87), channel_id=1, source_target_pairs={{0,8},{4,12},{8,16},{12,20},{16,24},{20,28},{24,0},{28,4},{1,9},{5... | collective-permute-start | bytes 49160 | tf_op jit(solution)/shard_map/ppermute | solution.py:279
  7.1 2.5 %collective-permute-start.1 = (bf16[8,1024]{1,0:T(8,128)(2,1)S(1)}, bf16[8,1024]{1,0:T(8,128)(2,1)S(1)}, u32[]{:S(2)}, u32[]{:S(2)}) collective-permute-start(bf16[8,1024]{1,0:T(8,128)(2,1)S(1)} %stack.87), channel_id=1, source_target_pairs={{0,12},{4,8},{8,20},{12,16},{16,28},{20,24},{24,4},{28,0},{1,13},{... | collective-permute-start | bytes 49160 | tf_op jit(solution)/shard_map/ppermute | solution.py:279
  9.6 1.2 collective-permute-start.2
  10.9 1.7 %collective-permute-start.3 = (bf16[8,1024]{1,0:T(8,128)(2,1)S(1)}, bf16[8,1024]{1,0:T(8,128)(2,1)S(1)}, u32[]{:S(2)}, u32[]{:S(2)}) collective-permute-start(bf16[8,1024]{1,0:T(8,128)(2,1)S(1)} %stack.87), channel_id=1, source_target_pairs={{0,20},{4,16},{8,28},{12,24},{16,4},{20,0},{24,12},{28,8},{1,21},{... | collective-permute-start | bytes 49160 | tf_op jit(solution)/shard_map/ppermute | solution.py:279
  12.5 2.2 %collective-permute-start.4 = (bf16[8,1024]{1,0:T(8,128)(2,1)S(1)}, bf16[8,1024]{1,0:T(8,128)(2,1)S(1)}, u32[]{:S(2)}, u32[]{:S(2)}) collective-permute-start(bf16[8,1024]{1,0:T(8,128)(2,1)S(1)} %stack.87), channel_id=1, source_target_pairs={{0,24},{4,28},{8,0},{12,4},{16,8},{20,12},{24,16},{28,20},{1,25},{... | collective-permute-start | bytes 49160 | tf_op jit(solution)/shard_map/ppermute | solution.py:279
  14.8 0.8 multiply_convert_fusion
  15.6 0.8 broadcast_in_dim.83
  16.4 0.1 broadcast_select_fusion
  16.6 0.7 stack.100
  17.3 0.1 stack.102
  17.4 1.4 collective-permute-start.5
  18.8 0.4 collective-permute-start.6
  19.3 2.8 %collective-permute-done.5 = bf16[8,1024]{1,0:T(8,128)(2,1)S(1)} collective-permute-done((bf16[8,1024]{1,0:T(8,128)(2,1)S(1)}, bf16[8,1024]{1,0:T(8,128)(2,1)S(1)}, u32[]{:S(2)}, u32[]{:S(2)}) %collective-permute-start.5) | collective-permute-done | bytes 16416 | tf_op jit(solution)/shard_map/ppermute | solution.py:279
  22.1 0.5 collective-permute-done.6
  22.6 0.1 convert_reduce_fusion.1
  22.7 0.1 reshape.222.codes.refs_0_
  22.8 1.6 %copy-done = bf16[64,16384]{1,0:T(8,128)(2,1)S(1)} copy-done((bf16[64,16384]{1,0:T(8,128)(2,1)S(1)}, bf16[64,16384]{1,0:T(8,128)(2,1)}, u32[]{:S(2)}) %copy-start) | copy-done | bytes 2097176
  24.4 6.7 %forward.4 = (f32[64,1024]{1,0:T(8,128)S(1)}, f32[64,1024]{1,0:T(8,128)S(1)}, bf16[129,256,512]{2,1,0:T(8,128)(2,1)}) custom-call(s32[128]{0:T(128)S(1)} %reshape.222.codes.refs_0_, bf16[8,8,1024]{2,1,0:T(8,128)(2,1)S(1)} %constant_dynamic-update-slice_fusion.left, bf16[32,8,1024]{2,1,0:T(8,128)(2,1)S(1)} %pad_maximum_fusion.right, bf16[64,16384]{1,0:T(8,128)(2,1)S(1)} %copy-done), custom_call_target="tpu_custom_call" | custom-call | flops 32 | bytes 64 | tf_op jit(solution)/shard_map/forward/pallas_call | solution.py:145
  31.1 0.1 collective-permute-start.7
  31.2 4.6 %forward.5 = (f32[64,1024]{1,0:T(8,128)S(1)}, f32[64,1024]{1,0:T(8,128)S(1)}, bf16[129,256,512]{2,1,0:T(8,128)(2,1)}) custom-call(s32[128]{0:T(128)S(1)} %reshape.222.codes.refs_0_, bf16[8,8,1024]{2,1,0:T(8,128)(2,1)S(1)} %constant_dynamic-update-slice_fusion.left, bf16[32,8,1024]{2,1,0:T(8,128)(2,1)S(1)} %pad_maximum_fusion.right, ...), custom_call_target="tpu_custom_call", output_to_operand_aliasing={{2}: (4, {})} | custom-call | flops 32 | bytes 64 | tf_op jit(solution)/shard_map/forward/pallas_call | solution.py:145
  35.8 2.8 %collective-permute-start.8 = (f32[64,1024]{1,0:T(8,128)S(1)}, f32[64,1024]{1,0:T(8,128)S(1)}, u32[]{:S(2)}, u32[]{:S(2)}) collective-permute-start(f32[64,1024]{1,0:T(8,128)S(1)} %get-tuple-element.39), channel_id=1, source_target_pairs={{0,4},{4,0},{8,12},{12,8},{16,20},{20,16},{24,28},{28,24},{1,5},{5... | collective-permute-start | bytes 786440 | tf_op jit(solution)/shard_map/ppermute | solution.py:274
  38.6 2.1 %collective-permute-start.9 = (f32[64,1024]{1,0:T(8,128)S(1)}, f32[64,1024]{1,0:T(8,128)S(1)}, u32[]{:S(2)}, u32[]{:S(2)}) collective-permute-start(f32[64,1024]{1,0:T(8,128)S(1)} %add.88), channel_id=1, source_target_pairs={{0,24},{4,28},{8,0},{12,4},{16,8},{20,12},{24,16},{28,20},{1,25},{... | collective-permute-start | bytes 786440 | tf_op jit(solution)/shard_map/ppermute | solution.py:279
  40.7 7.5 %forward.6 = (f32[64,1024]{1,0:T(8,128)S(1)}, f32[64,1024]{1,0:T(8,128)S(1)}, bf16[129,256,512]{2,1,0:T(8,128)(2,1)}) custom-call(s32[128]{0:T(128)S(1)} %reshape.222.codes.refs_0_, bf16[8,8,1024]{2,1,0:T(8,128)(2,1)S(1)} %constant_dynamic-update-slice_fusion.left, bf16[32,8,1024]{2,1,0:T(8,128)(2,1)S(1)} %pad_maximum_fusion.right, ...), custom_call_target="tpu_custom_call", output_to_operand_aliasing={{2}: (4, {})} | custom-call | flops 32 | bytes 64 | tf_op jit(solution)/shard_map/forward/pallas_call | solution.py:145
  48.2 2.1 %collective-permute-start.10 = (f32[64,1024]{1,0:T(8,128)S(1)}, f32[64,1024]{1,0:T(8,128)S(1)}, u32[]{:S(2)}, u32[]{:S(2)}) collective-permute-start(f32[64,1024]{1,0:T(8,128)S(1)} %get-tuple-element.44), channel_id=1, source_target_pairs={{0,4},{4,0},{8,12},{12,8},{16,20},{20,16},{24,28},{28,24},{1,5},{5... | collective-permute-start | bytes 786440 | tf_op jit(solution)/shard_map/ppermute | solution.py:274
  50.3 3.8 %forward.7 = (f32[64,1024]{1,0:T(8,128)S(1)}, f32[64,1024]{1,0:T(8,128)S(1)}, bf16[129,256,512]{2,1,0:T(8,128)(2,1)}) custom-call(s32[128]{0:T(128)S(1)} %reshape.222.codes.refs_0_, bf16[8,8,1024]{2,1,0:T(8,128)(2,1)S(1)} %constant_dynamic-update-slice_fusion.left, bf16[32,8,1024]{2,1,0:T(8,128)(2,1)S(1)} %pad_maximum_fusion.right, ...), custom_call_target="tpu_custom_call", output_to_operand_aliasing={{2}: (4, {})} | custom-call | flops 32 | bytes 64 | tf_op jit(solution)/shard_map/forward/pallas_call | solution.py:145
  54.1 1.6 %collective-permute-start.11 = (f32[64,1024]{1,0:T(8,128)S(1)}, f32[64,1024]{1,0:T(8,128)S(1)}, u32[]{:S(2)}, u32[]{:S(2)}) collective-permute-start(f32[64,1024]{1,0:T(8,128)S(1)} %get-tuple-element.50), channel_id=1, source_target_pairs={{0,4},{4,0},{8,12},{12,8},{16,20},{20,16},{24,28},{28,24},{1,5},{5... | collective-permute-start | bytes 786440 | tf_op jit(solution)/shard_map/ppermute | solution.py:274
  55.7 0.7 collective-permute-start.12
  56.4 1.6 %collective-permute-start.13 = (f32[64,1024]{1,0:T(8,128)S(1)}, f32[64,1024]{1,0:T(8,128)S(1)}, u32[]{:S(2)}, u32[]{:S(2)}) collective-permute-start(f32[64,1024]{1,0:T(8,128)S(1)} %add.90), channel_id=1, source_target_pairs={{0,8},{4,12},{8,16},{12,20},{16,24},{20,28},{24,0},{28,4},{1,9},{5... | collective-permute-start | bytes 786440 | tf_op jit(solution)/shard_map/ppermute | solution.py:279
  58.1 3.4 %collective-permute-done.11 = f32[64,1024]{1,0:T(8,128)S(1)} collective-permute-done((f32[64,1024]{1,0:T(8,128)S(1)}, f32[64,1024]{1,0:T(8,128)S(1)}, u32[]{:S(2)}, u32[]{:S(2)}) %collective-permute-start.11) | collective-permute-done | bytes 262176 | tf_op jit(solution)/shard_map/ppermute | solution.py:274
  61.4 13.7 %collective-permute-done.12 = f32[64,1024]{1,0:T(8,128)S(1)} collective-permute-done((f32[64,1024]{1,0:T(8,128)S(1)}, f32[64,1024]{1,0:T(8,128)S(1)}, u32[]{:S(2)}, u32[]{:S(2)}) %collective-permute-start.12) | collective-permute-done | bytes 262176 | tf_op jit(solution)/shard_map/ppermute | solution.py:279
  75.2 0.1 add_convert_fusion.refs_6_
  75.3 0.2 collective-permute-start.16
  75.6 3.6 %collective-permute-start.18 = (bf16[64,1024]{1,0:T(8,128)(2,1)S(1)}, bf16[64,1024]{1,0:T(8,128)(2,1)S(1)}, u32[]{:S(2)}, u32[]{:S(2)}) collective-permute-start(bf16[64,1024]{1,0:T(8,128)(2,1)S(1)} %add_convert_fusion.refs_6_), channel_id=1, source_target_pairs={{0,24},{4,28},{8,0},{12,4},{16,8},{20,12},{24,16},{28,20},{1,25},{... | collective-permute-start | bytes 393224 | tf_op jit(solution)/shard_map/ppermute | solution.py:279
  79.2 1.9 %collective-permute-start.20 = (bf16[64,1024]{1,0:T(8,128)(2,1)S(1)}, bf16[64,1024]{1,0:T(8,128)(2,1)S(1)}, u32[]{:S(2)}, u32[]{:S(2)}) collective-permute-start(bf16[64,1024]{1,0:T(8,128)(2,1)S(1)} %add_convert_fusion.refs_6_), channel_id=1, source_target_pairs={{0,4},{4,0},{8,12},{12,8},{16,20},{20,16},{24,28},{28,24},{1,5},{5... | collective-permute-start | bytes 393224 | tf_op jit(solution)/shard_map/ppermute | solution.py:274
  81.0 2.0 %collective-permute-done.14.refs_0_ = bf16[64,1024]{1,0:T(8,128)(2,1)S(1)} collective-permute-done((bf16[64,1024]{1,0:T(8,128)(2,1)S(1)}, bf16[64,1024]{1,0:T(8,128)(2,1)S(1)}, u32[]{:S(2)}, u32[]{:S(2)}) %collective-permute-start.14) | collective-permute-done | bytes 131104 | tf_op jit(solution)/shard_map/ppermute | solution.py:279
  83.1 4.6 %collective-permute-done.16.refs_2_ = bf16[64,1024]{1,0:T(8,128)(2,1)S(1)} collective-permute-done((bf16[64,1024]{1,0:T(8,128)(2,1)S(1)}, bf16[64,1024]{1,0:T(8,128)(2,1)S(1)}, u32[]{:S(2)}, u32[]{:S(2)}) %collective-permute-start.16) | collective-permute-done | bytes 131104 | tf_op jit(solution)/shard_map/ppermute | solution.py:279
  87.7 1.1 collective-permute-start.17
  88.8 0.9 collective-permute-start.19
  89.7 4.2 %collective-permute-done.17.refs_3_ = bf16[64,1024]{1,0:T(8,128)(2,1)S(1)} collective-permute-done((bf16[64,1024]{1,0:T(8,128)(2,1)S(1)}, bf16[64,1024]{1,0:T(8,128)(2,1)S(1)}, u32[]{:S(2)}, u32[]{:S(2)}) %collective-permute-start.17) | collective-permute-done | bytes 131104 | tf_op jit(solution)/shard_map/ppermute | solution.py:274
  93.9 2.8 %collective-permute-done.19.refs_5_ = bf16[64,1024]{1,0:T(8,128)(2,1)S(1)} collective-permute-done((bf16[64,1024]{1,0:T(8,128)(2,1)S(1)}, bf16[64,1024]{1,0:T(8,128)(2,1)S(1)}, u32[]{:S(2)}, u32[]{:S(2)}) %collective-permute-start.19) | collective-permute-done | bytes 131104 | tf_op jit(solution)/shard_map/ppermute | solution.py:274
  96.7 4.9 %backward.4 = (f32[64,4096]{1,0:T(8,128)S(1)}, bf16[8,64,1024]{2,1,0:T(8,128)(2,1)S(1)}) custom-call(s32[128]{0:T(128)S(1)} %reshape.222.codes.refs_0_, s32[1]{0:T(128)} %bitcast.10.first, bf16[129,256,512]{2,1,0:T(8,128)(2,1)} %get-tuple-element.48.jac.refs_2_, bf16[64,1024]{1,0:T(8,128)(2,1)S(1)} %collective-permute-done.14.refs_0_, ...), custom_call_target="tpu_custom_call" | custom-call | flops 16 | bytes 64 | tf_op jit(solution)/shard_map/backward/pallas_call | solution.py:224
  101.6 0.9 collective-permute-start.21
  102.5 5.3 %backward.5 = f32[64,4096]{1,0:T(8,128)S(1)} custom-call(s32[128]{0:T(128)S(1)} %reshape.222.codes.refs_0_, s32[1]{0:T(128)} %bitcast.9.refs_1_, bf16[129,256,512]{2,1,0:T(8,128)(2,1)} %get-tuple-element.48.jac.refs_2_, bf16[8,64,1024]{2,1,0:T(8,128)(2,1)S(1)} %get-tuple-element.57.refs_3_), custom_call_target="tpu_custom_call" | custom-call | flops 16 | bytes 64 | tf_op jit(solution)/shard_map/backward/pallas_call | solution.py:224
  107.8 2.1 %fusion = bf16[64,4096]{1,0:T(8,128)(2,1)} fusion(f32[64,4096]{1,0:T(8,128)S(1)} %backward.5, f32[64,4096]{1,0:T(8,128)} %collective-permute-done.21), kind=kLoop, calls=%fused_computation.5 | loop fusion | flops 786432 | bytes 2621440 | tf_op jit(solution)/shard_map/convert_element_type | solution.py:383
  109.9 4.2 %backward.7 = f32[64,4096]{1,0:T(8,128)S(1)} custom-call(s32[128]{0:T(128)S(1)} %reshape.222.codes.refs_0_, s32[1]{0:T(128)} %bitcast.12.refs_1_, bf16[129,256,512]{2,1,0:T(8,128)(2,1)} %get-tuple-element.48.jac.refs_2_, bf16[8,64,1024]{2,1,0:T(8,128)(2,1)S(1)} %get-tuple-element.57.refs_3_), custom_call_target="tpu_custom_call" | custom-call | flops 16 | bytes 64 | tf_op jit(solution)/shard_map/backward/pallas_call | solution.py:224
  114.2 2.4 %collective-permute-start.22 = (f32[64,4096]{1,0:T(8,128)S(1)}, f32[64,4096]{1,0:T(8,128)}, u32[]{:S(2)}, u32[]{:S(2)}) collective-permute-start(f32[64,4096]{1,0:T(8,128)S(1)} %backward.7), channel_id=1, source_target_pairs={{0,1},{1,0},{2,3},{3,2},{4,5},{5,4},{6,7},{7,6},{8,9},{9,8},{10,11... | collective-permute-start | bytes 3145736 | tf_op jit(solution)/shard_map/ppermute | solution.py:274
  116.6 4.7 %backward.6 = f32[64,4096]{1,0:T(8,128)S(1)} custom-call(s32[128]{0:T(128)S(1)} %reshape.222.codes.refs_0_, s32[1]{0:T(128)} %bitcast.11.refs_1_, bf16[129,256,512]{2,1,0:T(8,128)(2,1)} %get-tuple-element.48.jac.refs_2_, bf16[8,64,1024]{2,1,0:T(8,128)(2,1)S(1)} %get-tuple-element.57.refs_3_), custom_call_target="tpu_custom_call" | custom-call | flops 16 | bytes 64 | tf_op jit(solution)/shard_map/backward/pallas_call | solution.py:224
  121.3 3.5 %collective-permute-done.23 = bf16[64,4096]{1,0:T(8,128)(2,1)} collective-permute-done((bf16[64,4096]{1,0:T(8,128)(2,1)}, bf16[64,4096]{1,0:T(8,128)(2,1)}, u32[]{:S(2)}, u32[]{:S(2)}) %collective-permute-start.23) | collective-permute-done | bytes 524320 | tf_op jit(solution)/shard_map/ppermute | solution.py:274
  124.8 1.5 %convert_add_fusion.1.refs_0_ = f32[64,4096]{1,0:T(8,128)S(1)} fusion(bf16[64,4096]{1,0:T(8,128)(2,1)} %collective-permute-done.23, f32[64,4096]{1,0:T(8,128)S(1)} %backward.5, f32[64,4096]{1,0:T(8,128)} %collective-permute-done.21), kind=kLoop, calls=%fused_computation.1 | loop fusion | flops 1048576 | bytes 3670016 | tf_op jit(solution)/shard_map/add | solution.py:385
  126.4 1.4 fusion.1
  127.7 0.3 collective-permute-start.25
  128.0 13.5 %collective-permute-done.25 = bf16[64,4096]{1,0:T(8,128)(2,1)S(1)} collective-permute-done((bf16[64,4096]{1,0:T(8,128)(2,1)S(1)}, bf16[64,4096]{1,0:T(8,128)(2,1)S(1)}, u32[]{:S(2)}, u32[]{:S(2)}) %collective-permute-start.25) | collective-permute-done | bytes 524320 | tf_op jit(solution)/shard_map/ppermute | solution.py:274
  141.5 1.4 convert_add_fusion.refs_2_
  142.9 0.1 collective-permute-start.26
  143.0 1.7 %place.2.refs_0_ = f32[64,16384]{1,0:T(8,128)} custom-call(s32[1]{0:T(128)} %bitcast.where, f32[64,4096]{1,0:T(8,128)S(1)} %convert_add_fusion.1.refs_0_, f32[64,4096]{1,0:T(8,128)S(1)} %collective-permute-done.24.refs_1_, f32[64,4096]{1,0:T(8,128)S(1)} %convert_add_fusion.refs_2_), custom_call_target="tpu_custom_call" | custom-call | tf_op jit(solution)/shard_map/place/pallas_call | solution.py:261
  144.7 0.9 collective-permute-done.26.refs_1_
  145.6 1.0 place.3
  (53 shorter events, 0.4 us)
Async XLA Ops:
  4.0 13.4 %collective-permute-start = (bf16[8,1024]{1,0:T(8,128)(2,1)S(1)}, bf16[8,1024]{1,0:T(8,128)(2,1)S(1)}, u32[]{:S(2)}, u32[]{:S(2)}) collective-permute-start(bf16[8,1024]{1,0:T(8,128)(2,1)S(1)} %stack.87), channel_id=1, source_target_pairs={{0,8},{4,12},{8,16},{12,20},{16,24},{20,28},{24,0},{28,4},{1,9},{5... | collective-permute-start | bytes 49160 | tf_op jit(solution)/shard_map/ppermute | solution.py:279
  7.1 11.7 %collective-permute-start.1 = (bf16[8,1024]{1,0:T(8,128)(2,1)S(1)}, bf16[8,1024]{1,0:T(8,128)(2,1)S(1)}, u32[]{:S(2)}, u32[]{:S(2)}) collective-permute-start(bf16[8,1024]{1,0:T(8,128)(2,1)S(1)} %stack.87), channel_id=1, source_target_pairs={{0,12},{4,8},{8,20},{12,16},{16,28},{20,24},{24,4},{28,0},{1,13},{... | collective-permute-start | bytes 49160 | tf_op jit(solution)/shard_map/ppermute | solution.py:279
  9.6 9.6 %collective-permute-start.2 = (bf16[8,1024]{1,0:T(8,128)(2,1)S(1)}, bf16[8,1024]{1,0:T(8,128)(2,1)S(1)}, u32[]{:S(2)}, u32[]{:S(2)}) collective-permute-start(bf16[8,1024]{1,0:T(8,128)(2,1)S(1)} %stack.87), channel_id=1, source_target_pairs={{0,16},{4,20},{8,24},{12,28},{16,0},{20,4},{24,8},{28,12},{1,17},{... | collective-permute-start | bytes 49160 | tf_op jit(solution)/shard_map/ppermute | solution.py:279
  10.9 8.4 %collective-permute-start.3 = (bf16[8,1024]{1,0:T(8,128)(2,1)S(1)}, bf16[8,1024]{1,0:T(8,128)(2,1)S(1)}, u32[]{:S(2)}, u32[]{:S(2)}) collective-permute-start(bf16[8,1024]{1,0:T(8,128)(2,1)S(1)} %stack.87), channel_id=1, source_target_pairs={{0,20},{4,16},{8,28},{12,24},{16,4},{20,0},{24,12},{28,8},{1,21},{... | collective-permute-start | bytes 49160 | tf_op jit(solution)/shard_map/ppermute | solution.py:279
  12.5 6.7 %collective-permute-start.4 = (bf16[8,1024]{1,0:T(8,128)(2,1)S(1)}, bf16[8,1024]{1,0:T(8,128)(2,1)S(1)}, u32[]{:S(2)}, u32[]{:S(2)}) collective-permute-start(bf16[8,1024]{1,0:T(8,128)(2,1)S(1)} %stack.87), channel_id=1, source_target_pairs={{0,24},{4,28},{8,0},{12,4},{16,8},{20,12},{24,16},{28,20},{1,25},{... | collective-permute-start | bytes 49160 | tf_op jit(solution)/shard_map/ppermute | solution.py:279
  17.4 4.7 %collective-permute-start.5 = (bf16[8,1024]{1,0:T(8,128)(2,1)S(1)}, bf16[8,1024]{1,0:T(8,128)(2,1)S(1)}, u32[]{:S(2)}, u32[]{:S(2)}) collective-permute-start(bf16[8,1024]{1,0:T(8,128)(2,1)S(1)} %stack.87), channel_id=1, source_target_pairs={{0,28},{4,24},{8,4},{12,0},{16,12},{20,8},{24,20},{28,16},{1,29},{... | collective-permute-start | bytes 49160 | tf_op jit(solution)/shard_map/ppermute | solution.py:279
  18.8 3.7 %collective-permute-start.6 = (bf16[8,1024]{1,0:T(8,128)(2,1)S(1)}, bf16[8,1024]{1,0:T(8,128)(2,1)S(1)}, u32[]{:S(2)}, u32[]{:S(2)}) collective-permute-start(bf16[8,1024]{1,0:T(8,128)(2,1)S(1)} %stack.87), channel_id=1, source_target_pairs={{0,4},{4,0},{8,12},{12,8},{16,20},{20,16},{24,28},{28,24},{1,5},{5... | collective-permute-start | bytes 49160 | tf_op jit(solution)/shard_map/ppermute | solution.py:279
  22.8 1.6 %copy-start = (bf16[64,16384]{1,0:T(8,128)(2,1)S(1)}, bf16[64,16384]{1,0:T(8,128)(2,1)}, u32[]{:S(2)}) copy-start(bf16[64,16384]{1,0:T(8,128)(2,1)} %vectors.7) | copy-start | bytes 6291460
  31.1 7.5 %collective-permute-start.7 = (f32[64,1024]{1,0:T(8,128)S(1)}, f32[64,1024]{1,0:T(8,128)S(1)}, u32[]{:S(2)}, u32[]{:S(2)}) collective-permute-start(f32[64,1024]{1,0:T(8,128)S(1)} %get-tuple-element.35), channel_id=1, source_target_pairs={{0,4},{4,0},{8,12},{12,8},{16,20},{20,16},{24,28},{28,24},{1,5},{5... | collective-permute-start | bytes 786440 | tf_op jit(solution)/shard_map/ppermute | solution.py:274
  35.8 14.5 %collective-permute-start.8 = (f32[64,1024]{1,0:T(8,128)S(1)}, f32[64,1024]{1,0:T(8,128)S(1)}, u32[]{:S(2)}, u32[]{:S(2)}) collective-permute-start(f32[64,1024]{1,0:T(8,128)S(1)} %get-tuple-element.39), channel_id=1, source_target_pairs={{0,4},{4,0},{8,12},{12,8},{16,20},{20,16},{24,28},{28,24},{1,5},{5... | collective-permute-start | bytes 786440 | tf_op jit(solution)/shard_map/ppermute | solution.py:274
  38.6 11.7 %collective-permute-start.9 = (f32[64,1024]{1,0:T(8,128)S(1)}, f32[64,1024]{1,0:T(8,128)S(1)}, u32[]{:S(2)}, u32[]{:S(2)}) collective-permute-start(f32[64,1024]{1,0:T(8,128)S(1)} %add.88), channel_id=1, source_target_pairs={{0,24},{4,28},{8,0},{12,4},{16,8},{20,12},{24,16},{28,20},{1,25},{... | collective-permute-start | bytes 786440 | tf_op jit(solution)/shard_map/ppermute | solution.py:279
  48.2 8.2 %collective-permute-start.10 = (f32[64,1024]{1,0:T(8,128)S(1)}, f32[64,1024]{1,0:T(8,128)S(1)}, u32[]{:S(2)}, u32[]{:S(2)}) collective-permute-start(f32[64,1024]{1,0:T(8,128)S(1)} %get-tuple-element.44), channel_id=1, source_target_pairs={{0,4},{4,0},{8,12},{12,8},{16,20},{20,16},{24,28},{28,24},{1,5},{5... | collective-permute-start | bytes 786440 | tf_op jit(solution)/shard_map/ppermute | solution.py:274
  54.1 7.3 %collective-permute-start.11 = (f32[64,1024]{1,0:T(8,128)S(1)}, f32[64,1024]{1,0:T(8,128)S(1)}, u32[]{:S(2)}, u32[]{:S(2)}) collective-permute-start(f32[64,1024]{1,0:T(8,128)S(1)} %get-tuple-element.50), channel_id=1, source_target_pairs={{0,4},{4,0},{8,12},{12,8},{16,20},{20,16},{24,28},{28,24},{1,5},{5... | collective-permute-start | bytes 786440 | tf_op jit(solution)/shard_map/ppermute | solution.py:274
  55.7 19.5 %collective-permute-start.12 = (f32[64,1024]{1,0:T(8,128)S(1)}, f32[64,1024]{1,0:T(8,128)S(1)}, u32[]{:S(2)}, u32[]{:S(2)}) collective-permute-start(f32[64,1024]{1,0:T(8,128)S(1)} %add.89), channel_id=1, source_target_pairs={{0,16},{4,20},{8,24},{12,28},{16,0},{20,4},{24,8},{28,12},{1,17},{... | collective-permute-start | bytes 786440 | tf_op jit(solution)/shard_map/ppermute | solution.py:279
  56.4 18.8 %collective-permute-start.13 = (f32[64,1024]{1,0:T(8,128)S(1)}, f32[64,1024]{1,0:T(8,128)S(1)}, u32[]{:S(2)}, u32[]{:S(2)}) collective-permute-start(f32[64,1024]{1,0:T(8,128)S(1)} %add.90), channel_id=1, source_target_pairs={{0,8},{4,12},{8,16},{12,20},{16,24},{20,28},{24,0},{28,4},{1,9},{5... | collective-permute-start | bytes 786440 | tf_op jit(solution)/shard_map/ppermute | solution.py:279
  75.3 7.8 %collective-permute-start.14 = (bf16[64,1024]{1,0:T(8,128)(2,1)S(1)}, bf16[64,1024]{1,0:T(8,128)(2,1)S(1)}, u32[]{:S(2)}, u32[]{:S(2)}) collective-permute-start(bf16[64,1024]{1,0:T(8,128)(2,1)S(1)} %add_convert_fusion.refs_6_), channel_id=1, source_target_pairs={{0,8},{4,12},{8,16},{12,20},{16,24},{20,28},{24,0},{28,4},{1,9},{5... | collective-permute-start | bytes 393224 | tf_op jit(solution)/shard_map/ppermute | solution.py:279
  75.3 12.3 %collective-permute-start.16 = (bf16[64,1024]{1,0:T(8,128)(2,1)S(1)}, bf16[64,1024]{1,0:T(8,128)(2,1)S(1)}, u32[]{:S(2)}, u32[]{:S(2)}) collective-permute-start(bf16[64,1024]{1,0:T(8,128)(2,1)S(1)} %add_convert_fusion.refs_6_), channel_id=1, source_target_pairs={{0,16},{4,20},{8,24},{12,28},{16,0},{20,4},{24,8},{28,12},{1,17},{... | collective-permute-start | bytes 393224 | tf_op jit(solution)/shard_map/ppermute | solution.py:279
  75.6 13.2 %collective-permute-start.18 = (bf16[64,1024]{1,0:T(8,128)(2,1)S(1)}, bf16[64,1024]{1,0:T(8,128)(2,1)S(1)}, u32[]{:S(2)}, u32[]{:S(2)}) collective-permute-start(bf16[64,1024]{1,0:T(8,128)(2,1)S(1)} %add_convert_fusion.refs_6_), channel_id=1, source_target_pairs={{0,24},{4,28},{8,0},{12,4},{16,8},{20,12},{24,16},{28,20},{1,25},{... | collective-permute-start | bytes 393224 | tf_op jit(solution)/shard_map/ppermute | solution.py:279
  79.2 10.5 %collective-permute-start.20 = (bf16[64,1024]{1,0:T(8,128)(2,1)S(1)}, bf16[64,1024]{1,0:T(8,128)(2,1)S(1)}, u32[]{:S(2)}, u32[]{:S(2)}) collective-permute-start(bf16[64,1024]{1,0:T(8,128)(2,1)S(1)} %add_convert_fusion.refs_6_), channel_id=1, source_target_pairs={{0,4},{4,0},{8,12},{12,8},{16,20},{20,16},{24,28},{28,24},{1,5},{5... | collective-permute-start | bytes 393224 | tf_op jit(solution)/shard_map/ppermute | solution.py:274
  83.1 6.7 %collective-permute-start.15 = (bf16[64,1024]{1,0:T(8,128)(2,1)S(1)}, bf16[64,1024]{1,0:T(8,128)(2,1)S(1)}, u32[]{:S(2)}, u32[]{:S(2)}) collective-permute-start(bf16[64,1024]{1,0:T(8,128)(2,1)S(1)} %collective-permute-done.14.refs_0_), channel_id=1, source_target_pairs={{0,4},{4,0},{8,12},{12,8},{16,20},{20,16},{24,28},{28,24},{1,5},{5... | collective-permute-start | bytes 393224 | tf_op jit(solution)/shard_map/ppermute | solution.py:274
  87.7 6.2 %collective-permute-start.17 = (bf16[64,1024]{1,0:T(8,128)(2,1)S(1)}, bf16[64,1024]{1,0:T(8,128)(2,1)S(1)}, u32[]{:S(2)}, u32[]{:S(2)}) collective-permute-start(bf16[64,1024]{1,0:T(8,128)(2,1)S(1)} %collective-permute-done.16.refs_2_), channel_id=1, source_target_pairs={{0,4},{4,0},{8,12},{12,8},{16,20},{20,16},{24,28},{28,24},{1,5},{5... | collective-permute-start | bytes 393224 | tf_op jit(solution)/shard_map/ppermute | solution.py:274
  88.8 7.9 %collective-permute-start.19 = (bf16[64,1024]{1,0:T(8,128)(2,1)S(1)}, bf16[64,1024]{1,0:T(8,128)(2,1)S(1)}, u32[]{:S(2)}, u32[]{:S(2)}) collective-permute-start(bf16[64,1024]{1,0:T(8,128)(2,1)S(1)} %collective-permute-done.18.refs_4_), channel_id=1, source_target_pairs={{0,4},{4,0},{8,12},{12,8},{16,20},{20,16},{24,28},{28,24},{1,5},{5... | collective-permute-start | bytes 393224 | tf_op jit(solution)/shard_map/ppermute | solution.py:274
  101.6 6.2 %collective-permute-start.21 = (f32[64,4096]{1,0:T(8,128)S(1)}, f32[64,4096]{1,0:T(8,128)}, u32[]{:S(2)}, u32[]{:S(2)}) collective-permute-start(f32[64,4096]{1,0:T(8,128)S(1)} %get-tuple-element.58), channel_id=1, source_target_pairs={{0,1},{1,0},{2,3},{3,2},{4,5},{5,4},{6,7},{7,6},{8,9},{9,8},{10,11... | collective-permute-start | bytes 3145736 | tf_op jit(solution)/shard_map/ppermute | solution.py:274
  109.9 14.9 %collective-permute-start.23 = (bf16[64,4096]{1,0:T(8,128)(2,1)}, bf16[64,4096]{1,0:T(8,128)(2,1)}, u32[]{:S(2)}, u32[]{:S(2)}) collective-permute-start(bf16[64,4096]{1,0:T(8,128)(2,1)} %fusion), channel_id=1, source_target_pairs={{0,2},{1,3},{2,0},{3,1},{4,6},{5,7},{6,4},{7,5},{8,10},{9,11},{10,... | collective-permute-start | bytes 1572872 | tf_op jit(solution)/shard_map/ppermute | solution.py:274
  114.2 12.2 %collective-permute-start.22 = (f32[64,4096]{1,0:T(8,128)S(1)}, f32[64,4096]{1,0:T(8,128)}, u32[]{:S(2)}, u32[]{:S(2)}) collective-permute-start(f32[64,4096]{1,0:T(8,128)S(1)} %backward.7), channel_id=1, source_target_pairs={{0,1},{1,0},{2,3},{3,2},{4,5},{5,4},{6,7},{7,6},{8,9},{9,8},{10,11... | collective-permute-start | bytes 3145736 | tf_op jit(solution)/shard_map/ppermute | solution.py:274
  127.7 13.8 %collective-permute-start.25 = (bf16[64,4096]{1,0:T(8,128)(2,1)S(1)}, bf16[64,4096]{1,0:T(8,128)(2,1)S(1)}, u32[]{:S(2)}, u32[]{:S(2)}) collective-permute-start(bf16[64,4096]{1,0:T(8,128)(2,1)S(1)} %fusion.1), channel_id=1, source_target_pairs={{0,2},{1,3},{2,0},{3,1},{4,6},{5,7},{6,4},{7,5},{8,10},{9,11},{10,... | collective-permute-start | bytes 1572872 | tf_op jit(solution)/shard_map/ppermute | solution.py:274
  128.0 15.0 %collective-permute-start.24 = (f32[64,4096]{1,0:T(8,128)S(1)}, f32[64,4096]{1,0:T(8,128)S(1)}, u32[]{:S(2)}, u32[]{:S(2)}) collective-permute-start(f32[64,4096]{1,0:T(8,128)S(1)} %convert_add_fusion.1.refs_0_), channel_id=1, source_target_pairs={{0,1},{1,0},{2,3},{3,2},{4,5},{5,4},{6,7},{7,6},{8,9},{9,8},{10,11... | collective-permute-start | bytes 3145736 | tf_op jit(solution)/shard_map/ppermute | solution.py:274
  142.9 2.7 %collective-permute-start.26 = (f32[64,4096]{1,0:T(8,128)S(1)}, f32[64,4096]{1,0:T(8,128)S(1)}, u32[]{:S(2)}, u32[]{:S(2)}) collective-permute-start(f32[64,4096]{1,0:T(8,128)S(1)} %convert_add_fusion.refs_2_), channel_id=1, source_target_pairs={{0,1},{1,0},{2,3},{3,2},{4,5},{5,4},{6,7},{7,6},{8,9},{9,8},{10,11... | collective-permute-start | bytes 3145736 | tf_op jit(solution)/shard_map/ppermute | solution.py:274

commit v4 on v2

--- a/solution.py
+++ b/solution.py
@@ -23,7 +23,6 @@
     -1.8835629903409246,
     0.3106981920279389,
 )
-ROUNDER = 12582912.0
 
 
 def turn_constants():
@@ -46,13 +45,13 @@
     return out
 
 
-def collect(codes, todo, start, places, wanted):
+def collect(codes, todo, start, places, low, high):
     def visit(step, found):
         todo[found] = start + step
         code = codes[start + step]
-        return found + ((code >= 0) & wanted(code)).astype(jnp.int32)
-
-    return lax.fori_loop(0, places, visit, 0)
+        return found + ((code >= low) & (code < high)).astype(jnp.int32)
+
+    return lax.fori_loop(0, places, visit, 0, unroll=8 if places % 8 == 0 else 1)
 
 
 def entry_cost(entries, vector_count):
@@ -62,16 +61,17 @@
 def forward_kernel(blocks, capacity, codes, where, left, right, vectors, *refs):
     near, far, jac, todo, part, even, odd, sems = refs[-8:]
     spare = codes.shape[0]
+    rows = left.shape[2] // BLK_R
     part[...] = jnp.zeros_like(part)
     start = 2 * capacity * where[0]
-    found = collect(codes, todo, start, 2 * capacity, lambda code: True)
+    found = collect(codes, todo, start, 2 * capacity, 0, blocks * rows)
     steps = (found + 1) // 2
 
     def decode(place):
         code = codes[place]
         group = lax.div(place, capacity)
         away = jnp.where(lax.rem(group, 2) == where[1], 0, 1)
-        return lax.rem(code, blocks), lax.div(code, blocks), group, away
+        return lax.div(code, rows), lax.rem(code, rows), group, away
 
     def make(buffer, place):
         block, row, group, _ = decode(place)
@@ -80,7 +80,7 @@
             angles, right[block], (((0,), (0,)), ((), ())), preferred_element_type=f32
         )
         turns, weight = both[:, :BLK_P], both[:, BLK_P:]
-        rest = turns - ((turns + ROUNDER) - ROUNDER)
+        rest = turns - jnp.round(turns)
         square = rest * rest
         root = COS_POLY[4] * square + COS_POLY[3]
         for k in (2, 1, 0):
@@ -119,7 +119,7 @@
         save(odd, parity, 1, jnp.where(paired, second, spare)).start()
         return second
 
-    last = lax.fori_loop(0, steps, step, 0)
+    last = lax.fori_loop(0, steps, step, todo[0])
 
     @pl.when((found > 0) & (lax.rem(found, 2) == 0))
     def _():
@@ -165,16 +165,13 @@
     )(codes, where, left, right, vectors, *held)
 
 
-def backward_kernel(blocks, capacity, ring, codes, where, jac, *refs):
+def backward_kernel(capacity, ring, codes, where, jac, *refs):
     *pieces, out, gathered, todo, buffers, sems = refs
     here = out.shape[1] // BLK_P
     depth = buffers.shape[0]
 
-    def wanted(code):
-        block = lax.rem(code, blocks)
-        return (block >= where[2]) & (block < where[2] + here)
-
-    found = collect(codes, todo, 0, codes.shape[0], wanted)
+    rows = gathered.shape[2] // BLK_R
+    found = collect(codes, todo, 0, codes.shape[0], where[2] * rows, (where[2] + here) * rows)
 
     def load(turn):
         slot = lax.rem(turn, depth)
@@ -196,7 +193,7 @@
 
         place = todo[turn]
         code = codes[place]
-        block, row = lax.rem(code, blocks) - where[2], lax.div(code, blocks)
+        block, row = lax.div(code, rows) - where[2], lax.rem(code, rows)
         behind = lax.rem(where[0] - lax.div(place, 2 * capacity) + ring, ring)
         near = lax.rem(lax.div(place, capacity), 2) == where[1]
         piece = jnp.where(near, behind, ring + behind)
@@ -210,12 +207,12 @@
     lax.fori_loop(0, found, step, 0)
 
 
-def joined_backward_kernel(blocks, capacity, ring, *refs):
+def joined_backward_kernel(capacity, ring, *refs):
     *inputs, gathered, out, todo, buffers, sems = refs
-    backward_kernel(blocks, capacity, ring, *inputs, out, gathered, todo, buffers, sems)
-
-
-def backward(codes, where, jac, pieces, blocks, here, capacity):
+    backward_kernel(capacity, ring, *inputs, out, gathered, todo, buffers, sems)
+
+
+def backward(codes, where, jac, pieces, here, capacity):
     joined = not isinstance(pieces, list)
     smem = pl.BlockSpec(memory_space=pltpu.SMEM)
     vmem = pl.BlockSpec(memory_space=pltpu.VMEM)
@@ -227,7 +224,7 @@
     gathered = jax.ShapeDtypeStruct((total, count, width), bf16)
     kernel = joined_backward_kernel if joined else backward_kernel
     result = pl.pallas_call(
-        functools.partial(kernel, blocks, capacity, total // 2),
+        functools.partial(kernel, capacity, total // 2),
         out_shape=terms if joined else (terms, gathered),
         in_specs=[smem, smem, hbm] + [vmem] * len(sources),
         out_specs=vmem if joined else (vmem, vmem),
@@ -312,7 +309,7 @@
     holder = jnp.where(live, stored // blocks_here, -1)
     earlier = (holder[:, None] == holder[None, :]) & (slot_ids[None, :] < slot_ids[:, None])
     places = jnp.sum(earlier.astype(jnp.int32), axis=1)
-    code = entry_row * blocks_here + stored % blocks_here
+    code = stored % blocks_here * (width // BLK_R) + entry_row
     target = jnp.where(live, holder * capacity + places, -1)
     room_ids = jnp.arange(holders * capacity, dtype=jnp.int32)
     wanted = (
@@ -374,18 +371,17 @@
     same = [outputs] + [shift(outputs, "rows", k) for k in range(1, ring)]
     pieces = same + [swap(piece, "rows", 1) for piece in same]
 
-    def terms(first, here, pieces):
+    def terms(first, pieces):
         where = jnp.stack([position, side, first])
-        return backward(codes, where, jac, pieces, blocks_here, here, capacity)
-
-    half = blocks_here // 2
-    wide = half // 2 * BLK_P
-    given, pieces = terms((1 - core) * half, half, pieces)
-    given = swap(given, "grp", 1)
+        return backward(codes, where, jac, pieces, quarter, capacity)
+
+    quarter = blocks_here // 4
     sums = []
     for chunk in range(2):
-        kept, _ = terms(core * half + chunk * half // 2, half // 2, pieces)
-        chunk_sum = kept + given[:, chunk * wide : (chunk + 1) * wide]
+        given, pieces = terms((2 * (1 - core) + chunk) * quarter, pieces)
+        given = swap(given, "grp", 1)
+        kept, pieces = terms((2 * core + chunk) * quarter, pieces)
+        chunk_sum = kept + given
         bit = 2
         while bit < members:
             rounded = lax.reduce_precision(chunk_sum, 8, 7)

time: 144 us -> 134 us (0.931)
  Pallas kernels: 53.3 us -> 36 us
  starting transfers between devices: 30 us -> 41.5 us
  other arithmetic: 10 us -> 5.85 us
  local copies, waits for them, and re-layouts: 1.06 us -> 4.25 us
  waiting for transfers between devices: 48.8 us -> 46.5 us
    ppermute x13 -> x14, starting transfers between devices: 13.4 us -> 26.8 us  [swap(): lax.ppermute(array, axis, [(i, i ^ bit) for i in range(lax.axis_size(axis...]
    pallas_call x4, Pallas kernels: 29.8 us -> 19.2 us  [forward(): pl.pallas_call(functools.partial(forward_kernel, blocks, capacity), out_s...]
    ppermute x13 -> x14, waiting for transfers between devices: 33.2 us -> 23 us  [swap(): lax.ppermute(array, axis, [(i, i ^ bit) for i in range(lax.axis_size(axis...]
    ppermute x6, waiting for transfers between devices: 10.2 us -> 18 us  [shift(): lax.ppermute(array, axis, [(i, (i + 2 * steps) % size) for i in range(siz...]
    pallas_call x3 -> x4, Pallas kernels: 20.8 us -> 14.1 us  [backward(): pl.pallas_call(functools.partial(kernel, capacity, total // 2), out_shape...]
    unnamed x2 -> x4, local copies, waits for them, and re-layouts: 0.01 us -> 3.18 us
    add x2, other arithmetic: 3.27 us -> 0.28 us  [body(): chunk_sum = rounded + swap(sent, 'grp', bit).astype(f32)]
    ppermute x6, starting transfers between devices: 9.37 us -> 7.49 us  [shift(): lax.ppermute(array, axis, [(i, (i + 2 * steps) % size) for i in range(siz...]
  transfers between devices with their start and end apart: 20 -> 21, of which waited for: 12 -> 9; matrix products, arithmetic and copies ran while one was open for 3% -> 2% of each run, Pallas kernels for 23% -> 21%
where the time goes in v4:
time: 134 us; the launch traced here: 135 us
  waiting for transfers between devices  46.5 us (35%)
  starting transfers between devices  41.5 us (31%)
  Pallas kernels  36 us (27%)
  other arithmetic  5.85 us (4%)
  local copies, waits for them, and re-layouts  4.25 us (3%)
    ppermute x14, starting transfers between devices, swap(): lax.ppermute(array, axis, [(i, i ^ bit) for i in range(lax.axis_size(axis...  26.8 us
    ppermute x14, waiting for transfers between devices, swap(): lax.ppermute(array, axis, [(i, i ^ bit) for i in range(lax.axis_size(axis...  23 us
    pallas_call x4, Pallas kernels, forward(): pl.pallas_call(functools.partial(forward_kernel, blocks, capacity), out_s...  19.2 us
    ppermute x6, waiting for transfers between devices, shift(): lax.ppermute(array, axis, [(i, (i + 2 * steps) % size) for i in range(siz...  18 us
    pallas_call x4, Pallas kernels, backward(): pl.pallas_call(functools.partial(kernel, capacity, total // 2), out_shape...  14.1 us
    ppermute x6, starting transfers between devices, shift(): lax.ppermute(array, axis, [(i, (i + 2 * steps) % size) for i in range(siz...  7.49 us
    all_to_all x1, starting transfers between devices, body(): left = lax.all_to_all(send, 'rows', split_axis=0, concat_axis=0, tiled=True)  7.25 us
    all_to_all x1, waiting for transfers between devices, body(): left = lax.all_to_all(send, 'rows', split_axis=0, concat_axis=0, tiled=True)  5.44 us
  transfers between devices with their start and end apart: 21, of which 9 were waited for; matrix products, arithmetic and copies ran while one was open for 2% of the time, Pallas kernels for 21%

profile of v4, /device:TPU:0, one launch (start us, length us, event | category | flops | bytes accessed | tf_op | source)
XLA Modules:
  0.0 135.0 jit_solution(14367238388673962324)
XLA Ops:
  0.7 0.9 select_reduce_fusion
  1.5 0.7 compare_select_fusion.4
  2.2 0.2 convert_reduce_fusion
  2.4 0.1 select_reduce_fusion.1
  2.5 0.1 convert_element_type.66
  2.6 0.7 stack.118
  3.3 0.7 fusion.9
  4.0 0.1 stack.99
  4.0 0.7 fusion.3
  4.7 7.3 %all-to-all-start = ((bf16[8,8,1024]{2,1,0:T(8,128)(2,1)}), bf16[8,8,1024]{2,1,0:T(8,128)(2,1)S(1)}, u32[]{:S(2)}, u32[]{:S(2)}) async-start(bf16[8,8,1024]{2,1,0:T(8,128)(2,1)} %fusion.3), calls=%async_computation | async-start | bytes 262144 | tf_op jit(solution)/shard_map/all_to_all | solution.py:330
  12.0 0.8 broadcast_in_dim.90
  12.8 0.8 multiply_convert_fusion
  13.6 0.1 broadcast_select_fusion
  13.8 0.1 pad_add_fusion
  13.8 0.1 pad_maximum_fusion.right
  13.9 5.4 %all-to-all-done.left = bf16[8,8,1024]{2,1,0:T(8,128)(2,1)S(1)} async-done(((bf16[8,8,1024]{2,1,0:T(8,128)(2,1)}), bf16[8,8,1024]{2,1,0:T(8,128)(2,1)S(1)}, u32[]{:S(2)}, u32[]{:S(2)}) %all-to-all-start) | async-done | bytes 131104 | tf_op jit(solution)/shard_map/all_to_all | solution.py:330
  19.4 0.1 reshape.102.codes.refs_0_
  19.4 1.6 %copy-done = bf16[64,16384]{1,0:T(8,128)(2,1)S(1)} copy-done((bf16[64,16384]{1,0:T(8,128)(2,1)S(1)}, bf16[64,16384]{1,0:T(8,128)(2,1)}, u32[]{:S(2)}) %copy-start) | copy-done | bytes 2097176
  21.0 3.7 %forward.4 = (f32[64,1024]{1,0:T(8,128)S(1)}, f32[64,1024]{1,0:T(8,128)S(1)}, bf16[129,256,512]{2,1,0:T(8,128)(2,1)}) custom-call(s32[128]{0:T(128)S(1)} %reshape.102.codes.refs_0_, s32[2]{0:T(128)S(1)} %get-tuple-element.76.where, bf16[8,8,1024]{2,1,0:T(8,128)(2,1)S(1)} %all-to-all-done.left, bf16[32,8,1024]{2,1,0:T(8,128)(2,1)S(1)} %pad_maximum_fusion.right, ...), custom_call_target="tpu_custom_call" | custom-call | flops 32 | bytes 64 | tf_op jit(solution)/shard_map/forward/pallas_call | solution.py:148
  24.7 1.8 %collective-permute-start = (f32[64,1024]{1,0:T(8,128)S(1)}, f32[64,1024]{1,0:T(8,128)S(1)}, u32[]{:S(2)}, u32[]{:S(2)}) collective-permute-start(f32[64,1024]{1,0:T(8,128)S(1)} %get-tuple-element.35), channel_id=1, source_target_pairs={{0,4},{4,0},{8,12},{12,8},{16,20},{20,16},{24,28},{28,24},{1,5},{5... | collective-permute-start | bytes 786440 | tf_op jit(solution)/shard_map/ppermute | solution.py:276
  26.5 1.6 %copy-done.1 = bf16[64,16384]{1,0:T(8,128)(2,1)S(1)} copy-done((bf16[64,16384]{1,0:T(8,128)(2,1)S(1)}, bf16[64,16384]{1,0:T(8,128)(2,1)}, u32[]{:S(2)}) %copy-start.1) | copy-done | bytes 2097176
  28.1 5.9 %forward.5 = (f32[64,1024]{1,0:T(8,128)S(1)}, f32[64,1024]{1,0:T(8,128)S(1)}, bf16[129,256,512]{2,1,0:T(8,128)(2,1)}) custom-call(s32[128]{0:T(128)S(1)} %reshape.102.codes.refs_0_, s32[2]{0:T(128)S(1)} %get-tuple-element.77.where, bf16[8,8,1024]{2,1,0:T(8,128)(2,1)S(1)} %all-to-all-done.left, ...), custom_call_target="tpu_custom_call", output_to_operand_aliasing={{2}: (5, {})} | custom-call | flops 32 | bytes 64 | tf_op jit(solution)/shard_map/forward/pallas_call | solution.py:148
  34.0 0.4 collective-permute-start.1
  34.4 0.0 collective-permute-done
  34.4 4.3 %collective-permute-start.2 = (f32[64,1024]{1,0:T(8,128)S(1)}, f32[64,1024]{1,0:T(8,128)S(1)}, u32[]{:S(2)}, u32[]{:S(2)}) collective-permute-start(f32[64,1024]{1,0:T(8,128)S(1)} %add.127), channel_id=1, source_target_pairs={{0,24},{4,28},{8,0},{12,4},{16,8},{20,12},{24,16},{28,20},{1,25},{... | collective-permute-start | bytes 786440 | tf_op jit(solution)/shard_map/ppermute | solution.py:281
  38.7 0.1 pad_add_fusion.2
  38.8 4.4 %forward.6 = (f32[64,1024]{1,0:T(8,128)S(1)}, f32[64,1024]{1,0:T(8,128)S(1)}, bf16[129,256,512]{2,1,0:T(8,128)(2,1)}) custom-call(s32[128]{0:T(128)S(1)} %reshape.102.codes.refs_0_, s32[2]{0:T(128)S(1)} %get-tuple-element.78.where, bf16[8,8,1024]{2,1,0:T(8,128)(2,1)S(1)} %all-to-all-done.left, ...), custom_call_target="tpu_custom_call", output_to_operand_aliasing={{2}: (5, {})} | custom-call | flops 32 | bytes 64 | tf_op jit(solution)/shard_map/forward/pallas_call | solution.py:148
  43.2 0.9 collective-permute-start.3
  44.2 0.1 collective-permute-start.5
  44.3 5.2 %forward.7 = (f32[64,1024]{1,0:T(8,128)S(1)}, f32[64,1024]{1,0:T(8,128)S(1)}, bf16[129,256,512]{2,1,0:T(8,128)(2,1)}) custom-call(s32[128]{0:T(128)S(1)} %reshape.102.codes.refs_0_, s32[2]{0:T(128)S(1)} %get-tuple-element.79.where, bf16[8,8,1024]{2,1,0:T(8,128)(2,1)S(1)} %all-to-all-done.left, ...), custom_call_target="tpu_custom_call", output_to_operand_aliasing={{2}: (5, {})} | custom-call | flops 32 | bytes 64 | tf_op jit(solution)/shard_map/forward/pallas_call | solution.py:148
  49.4 3.5 %collective-permute-start.4 = (f32[64,1024]{1,0:T(8,128)S(1)}, f32[64,1024]{1,0:T(8,128)S(1)}, u32[]{:S(2)}, u32[]{:S(2)}) collective-permute-start(f32[64,1024]{1,0:T(8,128)S(1)} %get-tuple-element.50), channel_id=1, source_target_pairs={{0,4},{4,0},{8,12},{12,8},{16,20},{20,16},{24,28},{28,24},{1,5},{5... | collective-permute-start | bytes 786440 | tf_op jit(solution)/shard_map/ppermute | solution.py:276
  53.0 0.1 collective-permute-start.6
  53.0 8.9 %collective-permute-done.5 = f32[64,1024]{1,0:T(8,128)S(1)} collective-permute-done((f32[64,1024]{1,0:T(8,128)S(1)}, f32[64,1024]{1,0:T(8,128)S(1)}, u32[]{:S(2)}, u32[]{:S(2)}) %collective-permute-start.5) | collective-permute-done | bytes 262176 | tf_op jit(solution)/shard_map/ppermute | solution.py:281
  61.9 0.1 add_convert_fusion.refs_0_
  62.0 1.8 %collective-permute-start.9 = (bf16[64,1024]{1,0:T(8,128)(2,1)S(1)}, bf16[64,1024]{1,0:T(8,128)(2,1)S(1)}, u32[]{:S(2)}, u32[]{:S(2)}) collective-permute-start(bf16[64,1024]{1,0:T(8,128)(2,1)S(1)} %add_convert_fusion.refs_0_), channel_id=1, source_target_pairs={{0,24},{4,28},{8,0},{12,4},{16,8},{20,12},{24,16},{28,20},{1,25},{... | collective-permute-start | bytes 393224 | tf_op jit(solution)/shard_map/ppermute | solution.py:281
  63.9 1.2 collective-permute-start.7
  65.1 0.1 pad_add_fusion.8
  65.2 0.1 collective-permute-start.10
  65.2 2.6 %collective-permute-done.9.refs_3_ = bf16[64,1024]{1,0:T(8,128)(2,1)S(1)} collective-permute-done((bf16[64,1024]{1,0:T(8,128)(2,1)S(1)}, bf16[64,1024]{1,0:T(8,128)(2,1)S(1)}, u32[]{:S(2)}, u32[]{:S(2)}) %collective-permute-start.9) | collective-permute-done | bytes 131104 | tf_op jit(solution)/shard_map/ppermute | solution.py:281
  67.8 0.1 collective-permute-start.13
  67.9 6.5 %collective-permute-done.8.refs_2_ = bf16[64,1024]{1,0:T(8,128)(2,1)S(1)} collective-permute-done((bf16[64,1024]{1,0:T(8,128)(2,1)S(1)}, bf16[64,1024]{1,0:T(8,128)(2,1)S(1)}, u32[]{:S(2)}, u32[]{:S(2)}) %collective-permute-start.8) | collective-permute-done | bytes 131104 | tf_op jit(solution)/shard_map/ppermute | solution.py:281
  74.4 0.5 collective-permute-start.12
  74.9 1.5 %collective-permute-start.11 = (bf16[64,1024]{1,0:T(8,128)(2,1)S(1)}, bf16[64,1024]{1,0:T(8,128)(2,1)S(1)}, u32[]{:S(2)}, u32[]{:S(2)}) collective-permute-start(bf16[64,1024]{1,0:T(8,128)(2,1)S(1)} %collective-permute-done.7.refs_1_), channel_id=1, source_target_pairs={{0,4},{4,0},{8,12},{12,8},{16,20},{20,16},{24,28},{28,24},{1,5},{5... | collective-permute-start | bytes 393224 | tf_op jit(solution)/shard_map/ppermute | solution.py:276
  76.5 0.1 pad_add_fusion.7
  76.5 4.3 %collective-permute-done.12.refs_6_ = bf16[64,1024]{1,0:T(8,128)(2,1)S(1)} collective-permute-done((bf16[64,1024]{1,0:T(8,128)(2,1)S(1)}, bf16[64,1024]{1,0:T(8,128)(2,1)S(1)}, u32[]{:S(2)}, u32[]{:S(2)}) %collective-permute-start.12) | collective-permute-done | bytes 131104 | tf_op jit(solution)/shard_map/ppermute | solution.py:276
  80.8 1.4 %collective-permute-done.11.refs_5_ = bf16[64,1024]{1,0:T(8,128)(2,1)S(1)} collective-permute-done((bf16[64,1024]{1,0:T(8,128)(2,1)S(1)}, bf16[64,1024]{1,0:T(8,128)(2,1)S(1)}, u32[]{:S(2)}, u32[]{:S(2)}) %collective-permute-start.11) | collective-permute-done | bytes 131104 | tf_op jit(solution)/shard_map/ppermute | solution.py:276
  82.2 3.1 %backward.4 = (f32[64,4096]{1,0:T(8,128)S(1)}, bf16[8,64,1024]{2,1,0:T(8,128)(2,1)S(1)}) custom-call(s32[128]{0:T(128)S(1)} %reshape.102.codes.refs_0_, s32[3]{0:T(128)S(1)} %get-tuple-element.72.where, bf16[129,256,512]{2,1,0:T(8,128)(2,1)} %get-tuple-element.48.jac.refs_2_, bf16[64,1024]{1,0:T(8,128)(2,1)S(1)} %add_convert_fusion.refs_0_, ...), custom_call_target="tpu_custom_call" | custom-call | flops 16 | bytes 64 | tf_op jit(solution)/shard_map/backward/pallas_call | solution.py:226
  85.3 0.1 collective-permute-start.14
  85.4 4.4 %backward.5 = f32[64,4096]{1,0:T(8,128)S(1)} custom-call(s32[128]{0:T(128)S(1)} %reshape.102.codes.refs_0_, s32[3]{0:T(128)S(1)} %get-tuple-element.73.refs_1_, bf16[129,256,512]{2,1,0:T(8,128)(2,1)} %get-tuple-element.48.jac.refs_2_, bf16[8,64,1024]{2,1,0:T(8,128)(2,1)S(1)} %get-tuple-element.57.refs_3_), custom_call_target="tpu_custom_call" | custom-call | flops 16 | bytes 64 | tf_op jit(solution)/shard_map/backward/pallas_call | solution.py:226
  89.8 0.1 fusion
  89.9 16.1 %collective-permute-start.16 = (bf16[64,4096]{1,0:T(8,128)(2,1)S(1)}, bf16[64,4096]{1,0:T(8,128)(2,1)S(1)}, u32[]{:S(2)}, u32[]{:S(2)}) collective-permute-start(bf16[64,4096]{1,0:T(8,128)(2,1)S(1)} %fusion), channel_id=1, source_target_pairs={{0,2},{1,3},{2,0},{3,1},{4,6},{5,7},{6,4},{7,5},{8,10},{9,11},{10,... | collective-permute-start | bytes 1572872 | tf_op jit(solution)/shard_map/ppermute | solution.py:276
  106.0 3.6 %backward.7 = f32[64,4096]{1,0:T(8,128)S(1)} custom-call(s32[128]{0:T(128)S(1)} %reshape.102.codes.refs_0_, s32[3]{0:T(128)S(1)} %get-tuple-element.63.refs_1_, bf16[129,256,512]{2,1,0:T(8,128)(2,1)} %get-tuple-element.48.jac.refs_2_, bf16[8,64,1024]{2,1,0:T(8,128)(2,1)S(1)} %get-tuple-element.57.refs_3_), custom_call_target="tpu_custom_call" | custom-call | flops 16 | bytes 64 | tf_op jit(solution)/shard_map/backward/pallas_call | solution.py:226
  109.6 0.1 collective-permute-start.15
  109.7 3.1 %backward.6 = f32[64,4096]{1,0:T(8,128)S(1)} custom-call(s32[128]{0:T(128)S(1)} %reshape.102.codes.refs_0_, s32[3]{0:T(128)S(1)} %get-tuple-element.71.refs_1_, bf16[129,256,512]{2,1,0:T(8,128)(2,1)} %get-tuple-element.48.jac.refs_2_, bf16[8,64,1024]{2,1,0:T(8,128)(2,1)S(1)} %get-tuple-element.57.refs_3_), custom_call_target="tpu_custom_call" | custom-call | flops 16 | bytes 64 | tf_op jit(solution)/shard_map/backward/pallas_call | solution.py:226
  112.7 5.1 %collective-permute-done.16 = bf16[64,4096]{1,0:T(8,128)(2,1)S(1)} collective-permute-done((bf16[64,4096]{1,0:T(8,128)(2,1)S(1)}, bf16[64,4096]{1,0:T(8,128)(2,1)S(1)}, u32[]{:S(2)}, u32[]{:S(2)}) %collective-permute-start.16) | collective-permute-done | bytes 524320 | tf_op jit(solution)/shard_map/ppermute | solution.py:276
  117.8 0.1 convert_add_fusion.1.refs_0_
  117.9 0.1 fusion.1
  118.1 1.8 %collective-permute-start.18 = (bf16[64,4096]{1,0:T(8,128)(2,1)S(1)}, bf16[64,4096]{1,0:T(8,128)(2,1)S(1)}, u32[]{:S(2)}, u32[]{:S(2)}) collective-permute-start(bf16[64,4096]{1,0:T(8,128)(2,1)S(1)} %fusion.1), channel_id=1, source_target_pairs={{0,2},{1,3},{2,0},{3,1},{4,6},{5,7},{6,4},{7,5},{8,10},{9,11},{10,... | collective-permute-start | bytes 1572872 | tf_op jit(solution)/shard_map/ppermute | solution.py:276
  119.9 11.3 %collective-permute-done.18 = bf16[64,4096]{1,0:T(8,128)(2,1)S(1)} collective-permute-done((bf16[64,4096]{1,0:T(8,128)(2,1)S(1)}, bf16[64,4096]{1,0:T(8,128)(2,1)S(1)}, u32[]{:S(2)}, u32[]{:S(2)}) %collective-permute-start.18) | collective-permute-done | bytes 524320 | tf_op jit(solution)/shard_map/ppermute | solution.py:276
  131.1 0.1 convert_add_fusion.refs_2_
  131.3 0.1 collective-permute-start.19
  131.4 1.7 %place.2.refs_0_ = f32[64,16384]{1,0:T(8,128)} custom-call(s32[1]{0:T(128)} %bitcast.where, f32[64,4096]{1,0:T(8,128)S(1)} %convert_add_fusion.1.refs_0_, f32[64,4096]{1,0:T(8,128)S(1)} %collective-permute-done.17.refs_1_, f32[64,4096]{1,0:T(8,128)S(1)} %convert_add_fusion.refs_2_), custom_call_target="tpu_custom_call" | custom-call | tf_op jit(solution)/shard_map/place/pallas_call | solution.py:263
  133.1 0.9 collective-permute-done.19.refs_1_
  134.0 1.0 place.3
  (25 shorter events, 0.2 us)
Async XLA Ops:
  4.7 14.6 %all-to-all-start = ((bf16[8,8,1024]{2,1,0:T(8,128)(2,1)}), bf16[8,8,1024]{2,1,0:T(8,128)(2,1)S(1)}, u32[]{:S(2)}, u32[]{:S(2)}) async-start(bf16[8,8,1024]{2,1,0:T(8,128)(2,1)} %fusion.3), calls=%async_computation | async-start | bytes 262144 | tf_op jit(solution)/shard_map/all_to_all | solution.py:330
  19.4 1.6 %copy-start = (bf16[64,16384]{1,0:T(8,128)(2,1)S(1)}, bf16[64,16384]{1,0:T(8,128)(2,1)}, u32[]{:S(2)}) copy-start(bf16[64,16384]{1,0:T(8,128)(2,1)} %vectors.7) | copy-start | bytes 6291460
  24.7 9.7 %collective-permute-start = (f32[64,1024]{1,0:T(8,128)S(1)}, f32[64,1024]{1,0:T(8,128)S(1)}, u32[]{:S(2)}, u32[]{:S(2)}) collective-permute-start(f32[64,1024]{1,0:T(8,128)S(1)} %get-tuple-element.35), channel_id=1, source_target_pairs={{0,4},{4,0},{8,12},{12,8},{16,20},{20,16},{24,28},{28,24},{1,5},{5... | collective-permute-start | bytes 786440 | tf_op jit(solution)/shard_map/ppermute | solution.py:276
  26.5 1.6 %copy-start.1 = (bf16[64,16384]{1,0:T(8,128)(2,1)S(1)}, bf16[64,16384]{1,0:T(8,128)(2,1)}, u32[]{:S(2)}) copy-start(bf16[64,16384]{1,0:T(8,128)(2,1)} %vectors.7) | copy-start | bytes 6291460
  34.0 10.2 %collective-permute-start.1 = (f32[64,1024]{1,0:T(8,128)S(1)}, f32[64,1024]{1,0:T(8,128)S(1)}, u32[]{:S(2)}, u32[]{:S(2)}) collective-permute-start(f32[64,1024]{1,0:T(8,128)S(1)} %get-tuple-element.39), channel_id=1, source_target_pairs={{0,4},{4,0},{8,12},{12,8},{16,20},{20,16},{24,28},{28,24},{1,5},{5... | collective-permute-start | bytes 786440 | tf_op jit(solution)/shard_map/ppermute | solution.py:276
  34.4 9.7 %collective-permute-start.2 = (f32[64,1024]{1,0:T(8,128)S(1)}, f32[64,1024]{1,0:T(8,128)S(1)}, u32[]{:S(2)}, u32[]{:S(2)}) collective-permute-start(f32[64,1024]{1,0:T(8,128)S(1)} %add.127), channel_id=1, source_target_pairs={{0,24},{4,28},{8,0},{12,4},{16,8},{20,12},{24,16},{28,20},{1,25},{... | collective-permute-start | bytes 786440 | tf_op jit(solution)/shard_map/ppermute | solution.py:281
  43.2 9.7 %collective-permute-start.3 = (f32[64,1024]{1,0:T(8,128)S(1)}, f32[64,1024]{1,0:T(8,128)S(1)}, u32[]{:S(2)}, u32[]{:S(2)}) collective-permute-start(f32[64,1024]{1,0:T(8,128)S(1)} %get-tuple-element.44), channel_id=1, source_target_pairs={{0,4},{4,0},{8,12},{12,8},{16,20},{20,16},{24,28},{28,24},{1,5},{5... | collective-permute-start | bytes 786440 | tf_op jit(solution)/shard_map/ppermute | solution.py:276
  44.2 17.8 %collective-permute-start.5 = (f32[64,1024]{1,0:T(8,128)S(1)}, f32[64,1024]{1,0:T(8,128)S(1)}, u32[]{:S(2)}, u32[]{:S(2)}) collective-permute-start(f32[64,1024]{1,0:T(8,128)S(1)} %add.129), channel_id=1, source_target_pairs={{0,16},{4,20},{8,24},{12,28},{16,0},{20,4},{24,8},{28,12},{1,17},{... | collective-permute-start | bytes 786440 | tf_op jit(solution)/shard_map/ppermute | solution.py:281
  49.4 12.5 %collective-permute-start.4 = (f32[64,1024]{1,0:T(8,128)S(1)}, f32[64,1024]{1,0:T(8,128)S(1)}, u32[]{:S(2)}, u32[]{:S(2)}) collective-permute-start(f32[64,1024]{1,0:T(8,128)S(1)} %get-tuple-element.50), channel_id=1, source_target_pairs={{0,4},{4,0},{8,12},{12,8},{16,20},{20,16},{24,28},{28,24},{1,5},{5... | collective-permute-start | bytes 786440 | tf_op jit(solution)/shard_map/ppermute | solution.py:276
  53.0 9.0 %collective-permute-start.6 = (f32[64,1024]{1,0:T(8,128)S(1)}, f32[64,1024]{1,0:T(8,128)S(1)}, u32[]{:S(2)}, u32[]{:S(2)}) collective-permute-start(f32[64,1024]{1,0:T(8,128)S(1)} %add.131), channel_id=1, source_target_pairs={{0,8},{4,12},{8,16},{12,20},{16,24},{20,28},{24,0},{28,4},{1,9},{5... | collective-permute-start | bytes 786440 | tf_op jit(solution)/shard_map/ppermute | solution.py:281
  62.0 5.8 %collective-permute-start.9 = (bf16[64,1024]{1,0:T(8,128)(2,1)S(1)}, bf16[64,1024]{1,0:T(8,128)(2,1)S(1)}, u32[]{:S(2)}, u32[]{:S(2)}) collective-permute-start(bf16[64,1024]{1,0:T(8,128)(2,1)S(1)} %add_convert_fusion.refs_0_), channel_id=1, source_target_pairs={{0,24},{4,28},{8,0},{12,4},{16,8},{20,12},{24,16},{28,20},{1,25},{... | collective-permute-start | bytes 393224 | tf_op jit(solution)/shard_map/ppermute | solution.py:281
  63.9 10.6 %collective-permute-start.8 = (bf16[64,1024]{1,0:T(8,128)(2,1)S(1)}, bf16[64,1024]{1,0:T(8,128)(2,1)S(1)}, u32[]{:S(2)}, u32[]{:S(2)}) collective-permute-start(bf16[64,1024]{1,0:T(8,128)(2,1)S(1)} %add_convert_fusion.refs_0_), channel_id=1, source_target_pairs={{0,16},{4,20},{8,24},{12,28},{16,0},{20,4},{24,8},{28,12},{1,17},{... | collective-permute-start | bytes 393224 | tf_op jit(solution)/shard_map/ppermute | solution.py:281
  63.9 11.0 %collective-permute-start.7 = (bf16[64,1024]{1,0:T(8,128)(2,1)S(1)}, bf16[64,1024]{1,0:T(8,128)(2,1)S(1)}, u32[]{:S(2)}, u32[]{:S(2)}) collective-permute-start(bf16[64,1024]{1,0:T(8,128)(2,1)S(1)} %add_convert_fusion.refs_0_), channel_id=1, source_target_pairs={{0,8},{4,12},{8,16},{12,20},{16,24},{20,28},{24,0},{28,4},{1,9},{5... | collective-permute-start | bytes 393224 | tf_op jit(solution)/shard_map/ppermute | solution.py:281
  65.2 11.4 %collective-permute-start.10 = (bf16[64,1024]{1,0:T(8,128)(2,1)S(1)}, bf16[64,1024]{1,0:T(8,128)(2,1)S(1)}, u32[]{:S(2)}, u32[]{:S(2)}) collective-permute-start(bf16[64,1024]{1,0:T(8,128)(2,1)S(1)} %add_convert_fusion.refs_0_), channel_id=1, source_target_pairs={{0,4},{4,0},{8,12},{12,8},{16,20},{20,16},{24,28},{28,24},{1,5},{5... | collective-permute-start | bytes 393224 | tf_op jit(solution)/shard_map/ppermute | solution.py:276
  67.8 8.7 %collective-permute-start.13 = (bf16[64,1024]{1,0:T(8,128)(2,1)S(1)}, bf16[64,1024]{1,0:T(8,128)(2,1)S(1)}, u32[]{:S(2)}, u32[]{:S(2)}) collective-permute-start(bf16[64,1024]{1,0:T(8,128)(2,1)S(1)} %collective-permute-done.9.refs_3_), channel_id=1, source_target_pairs={{0,4},{4,0},{8,12},{12,8},{16,20},{20,16},{24,28},{28,24},{1,5},{5... | collective-permute-start | bytes 393224 | tf_op jit(solution)/shard_map/ppermute | solution.py:276
  74.4 6.4 %collective-permute-start.12 = (bf16[64,1024]{1,0:T(8,128)(2,1)S(1)}, bf16[64,1024]{1,0:T(8,128)(2,1)S(1)}, u32[]{:S(2)}, u32[]{:S(2)}) collective-permute-start(bf16[64,1024]{1,0:T(8,128)(2,1)S(1)} %collective-permute-done.8.refs_2_), channel_id=1, source_target_pairs={{0,4},{4,0},{8,12},{12,8},{16,20},{20,16},{24,28},{28,24},{1,5},{5... | collective-permute-start | bytes 393224 | tf_op jit(solution)/shard_map/ppermute | solution.py:276
  74.9 7.3 %collective-permute-start.11 = (bf16[64,1024]{1,0:T(8,128)(2,1)S(1)}, bf16[64,1024]{1,0:T(8,128)(2,1)S(1)}, u32[]{:S(2)}, u32[]{:S(2)}) collective-permute-start(bf16[64,1024]{1,0:T(8,128)(2,1)S(1)} %collective-permute-done.7.refs_1_), channel_id=1, source_target_pairs={{0,4},{4,0},{8,12},{12,8},{16,20},{20,16},{24,28},{28,24},{1,5},{5... | collective-permute-start | bytes 393224 | tf_op jit(solution)/shard_map/ppermute | solution.py:276
  85.3 4.4 %collective-permute-start.14 = (f32[64,4096]{1,0:T(8,128)S(1)}, f32[64,4096]{1,0:T(8,128)S(1)}, u32[]{:S(2)}, u32[]{:S(2)}) collective-permute-start(f32[64,4096]{1,0:T(8,128)S(1)} %get-tuple-element.58), channel_id=1, source_target_pairs={{0,1},{1,0},{2,3},{3,2},{4,5},{5,4},{6,7},{7,6},{8,9},{9,8},{10,11... | collective-permute-start | bytes 3145736 | tf_op jit(solution)/shard_map/ppermute | solution.py:276
  89.9 27.9 %collective-permute-start.16 = (bf16[64,4096]{1,0:T(8,128)(2,1)S(1)}, bf16[64,4096]{1,0:T(8,128)(2,1)S(1)}, u32[]{:S(2)}, u32[]{:S(2)}) collective-permute-start(bf16[64,4096]{1,0:T(8,128)(2,1)S(1)} %fusion), channel_id=1, source_target_pairs={{0,2},{1,3},{2,0},{3,1},{4,6},{5,7},{6,4},{7,5},{8,10},{9,11},{10,... | collective-permute-start | bytes 1572872 | tf_op jit(solution)/shard_map/ppermute | solution.py:276
  109.6 8.4 %collective-permute-start.15 = (f32[64,4096]{1,0:T(8,128)S(1)}, f32[64,4096]{1,0:T(8,128)S(1)}, u32[]{:S(2)}, u32[]{:S(2)}) collective-permute-start(f32[64,4096]{1,0:T(8,128)S(1)} %backward.7), channel_id=1, source_target_pairs={{0,1},{1,0},{2,3},{3,2},{4,5},{5,4},{6,7},{7,6},{8,9},{9,8},{10,11... | collective-permute-start | bytes 3145736 | tf_op jit(solution)/shard_map/ppermute | solution.py:276
  118.1 13.1 %collective-permute-start.18 = (bf16[64,4096]{1,0:T(8,128)(2,1)S(1)}, bf16[64,4096]{1,0:T(8,128)(2,1)S(1)}, u32[]{:S(2)}, u32[]{:S(2)}) collective-permute-start(bf16[64,4096]{1,0:T(8,128)(2,1)S(1)} %fusion.1), channel_id=1, source_target_pairs={{0,2},{1,3},{2,0},{3,1},{4,6},{5,7},{6,4},{7,5},{8,10},{9,11},{10,... | collective-permute-start | bytes 1572872 | tf_op jit(solution)/shard_map/ppermute | solution.py:276
  119.9 11.5 %collective-permute-start.17 = (f32[64,4096]{1,0:T(8,128)S(1)}, f32[64,4096]{1,0:T(8,128)S(1)}, u32[]{:S(2)}, u32[]{:S(2)}) collective-permute-start(f32[64,4096]{1,0:T(8,128)S(1)} %convert_add_fusion.1.refs_0_), channel_id=1, source_target_pairs={{0,1},{1,0},{2,3},{3,2},{4,5},{5,4},{6,7},{7,6},{8,9},{9,8},{10,11... | collective-permute-start | bytes 3145736 | tf_op jit(solution)/shard_map/ppermute | solution.py:276
  131.3 2.7 %collective-permute-start.19 = (f32[64,4096]{1,0:T(8,128)S(1)}, f32[64,4096]{1,0:T(8,128)S(1)}, u32[]{:S(2)}, u32[]{:S(2)}) collective-permute-start(f32[64,4096]{1,0:T(8,128)S(1)} %convert_add_fusion.refs_2_), channel_id=1, source_target_pairs={{0,1},{1,0},{2,3},{3,2},{4,5},{5,4},{6,7},{7,6},{8,9},{9,8},{10,11... | collective-permute-start | bytes 3145736 | tf_op jit(solution)/shard_map/ppermute | solution.py:276

commit v5 on v4

--- a/solution.py
+++ b/solution.py
@@ -59,7 +59,7 @@
 
 
 def forward_kernel(blocks, capacity, codes, where, left, right, vectors, *refs):
-    near, far, jac, todo, part, even, odd, sems = refs[-8:]
+    near, far, jac, todo, part, even, odd, chosen, sems, chosen_sems = refs[-10:]
     spare = codes.shape[0]
     rows = left.shape[2] // BLK_R
     part[...] = jnp.zeros_like(part)
@@ -87,11 +87,20 @@
             root = root * square + COS_POLY[k]
         buffer[...] = (weight * (root * root - 1.0)).astype(bf16)
 
-    def apply(buffer, place, keep):
-        block, row, _, away = decode(place)
-        chosen = vectors[:, pl.ds(pl.multiple_of(block * BLK_P, BLK_P), BLK_P)]
+    def fetch(turn, which, place):
+        slot = lax.rem(turn, 3)
+        at = pl.ds(pl.multiple_of(decode(place)[0] * BLK_P, BLK_P), BLK_P)
+        return pltpu.make_async_copy(
+            vectors.at[:, at], chosen.at[slot, which], chosen_sems.at[slot, which]
+        )
+
+    def apply(buffer, place, turn, which, keep):
+        _, row, _, away = decode(place)
         term = lax.dot_general(
-            buffer[...], chosen, (((1,), (1,)), ((), ())), preferred_element_type=f32
+            buffer[...],
+            chosen[lax.rem(turn, 3), which],
+            (((1,), (1,)), ((), ())),
+            preferred_element_type=f32,
         )
         if keep is not None:
             term = jnp.where(keep, term, 0.0)
@@ -100,21 +109,38 @@
     def save(buffer, parity, which, place):
         return pltpu.make_async_copy(buffer.at[parity], jac.at[place], sems.at[parity, which])
 
+    def entries(turn):
+        paired = 2 * turn + 1 < found
+        return todo[2 * turn], todo[jnp.where(paired, 2 * turn + 1, 2 * turn)], paired
+
+    def fetch_both(turn):
+        first, second, _ = entries(turn)
+        fetch(turn, 0, first).start()
+        fetch(turn, 1, second).start()
+
+    @pl.when(steps > 0)
+    def _():
+        fetch_both(0)
+
     def step(turn, before):
         parity = lax.rem(turn, 2)
-        first = todo[2 * turn]
-        paired = 2 * turn + 1 < found
-        second = todo[jnp.where(paired, 2 * turn + 1, 2 * turn)]
+        first, second, paired = entries(turn)
+
+        @pl.when(turn + 1 < steps)
+        def _():
+            fetch_both(turn + 1)
 
         @pl.when(turn >= 2)
         def _():
             save(even, parity, 0, 0).wait()
             save(odd, parity, 1, 0).wait()
 
-        apply(odd.at[1 - parity], before, turn > 0)
+        fetch(turn, 0, first).wait()
+        fetch(turn, 1, second).wait()
+        apply(odd.at[1 - parity], before, turn + 2, 1, turn > 0)
         make(even.at[parity], first)
         save(even, parity, 0, first).start()
-        apply(even.at[parity], first, None)
+        apply(even.at[parity], first, turn, 0, None)
         make(odd.at[parity], second)
         save(odd, parity, 1, jnp.where(paired, second, spare)).start()
         return second
@@ -123,7 +149,7 @@
 
     @pl.when((found > 0) & (lax.rem(found, 2) == 0))
     def _():
-        apply(odd.at[lax.rem(steps + 1, 2)], last, None)
+        apply(odd.at[lax.rem(steps + 1, 2)], last, steps + 2, 1, None)
 
     for back in (1, 2):
         @pl.when(steps >= back)
@@ -149,14 +175,16 @@
         functools.partial(forward_kernel, blocks, capacity),
         out_shape=(jax.ShapeDtypeStruct((count, width), f32),) * 2
         + (pltpu.HBM((room + 1, BLK_R, BLK_P), bf16),),
-        in_specs=[smem, smem, vmem, vmem, vmem] + [hbm] * len(held),
+        in_specs=[smem, smem, vmem, vmem, hbm] + [hbm] * len(held),
         out_specs=(vmem, vmem, hbm),
         scratch_shapes=[
             pltpu.SMEM((2 * capacity + 1,), jnp.int32),
             pltpu.VMEM((2, count, width), f32),
             pltpu.VMEM((2, BLK_R, BLK_P), bf16),
             pltpu.VMEM((2, BLK_R, BLK_P), bf16),
+            pltpu.VMEM((3, 2, count, BLK_P), bf16),
             pltpu.SemaphoreType.DMA((2, 2)),
+            pltpu.SemaphoreType.DMA((3, 2)),
         ],
         input_output_aliases={5: 2} if held else {},
         compiler_params=pltpu.CompilerParams(vmem_limit_bytes=16 << 20),
@@ -343,6 +371,7 @@
     )
     me = lax.axis_index("rows")
     core = lax.axis_index("grp") % 2
+    vectors = pltpu.with_memory_space_constraint(vectors, pltpu.HBM)
     side, position = me % 2, me // 2
     ring = holders // 2
 

time: 134 us -> 140 us (1.045); the launches traced: 135 us -> 138 us
  Pallas kernels: 36 us -> 53.6 us
  starting transfers between devices: 41.5 us -> 31.4 us
  local copies, waits for them, and re-layouts: 4.25 us -> 1.06 us
    pallas_call x4, Pallas kernels: 19.2 us -> 33.2 us  [forward(): pl.pallas_call(functools.partial(forward_kernel, blocks, capacity), out_s...]
    ppermute x14, starting transfers between devices: 26.8 us -> 13.6 us  [swap(): lax.ppermute(array, axis, [(i, i ^ bit) for i in range(lax.axis_size(axis...]
    ppermute x6, waiting for transfers between devices: 18 us -> 11.3 us  [shift(): lax.ppermute(array, axis, [(i, (i + 2 * steps) % size) for i in range(siz...]
    ppermute x14, waiting for transfers between devices: 23 us -> 28.7 us  [swap(): lax.ppermute(array, axis, [(i, i ^ bit) for i in range(lax.axis_size(axis...]
    pallas_call x4, Pallas kernels: 14.1 us -> 17.6 us  [backward(): pl.pallas_call(functools.partial(kernel, capacity, total // 2), out_shape...]
    unnamed x4 -> x0, local copies, waits for them, and re-layouts: 3.18 us -> none
    ppermute x6, starting transfers between devices: 7.49 us -> 10.5 us  [shift(): lax.ppermute(array, axis, [(i, (i + 2 * steps) % size) for i in range(siz...]
  transfers between devices with their start and end apart: 21 -> 21, of which waited for: 9 -> 12; matrix products, arithmetic and copies ran while one was open for 2% -> 2% of each run, Pallas kernels for 21% -> 28%
where the time goes in v5:
time: 140 us; the launch traced here: 138 us
  Pallas kernels  53.6 us (38%)
  waiting for transfers between devices  45.4 us (32%)
  starting transfers between devices  31.4 us (22%)
  other arithmetic  5.85 us (4%)
    pallas_call x4, Pallas kernels, forward(): pl.pallas_call(functools.partial(forward_kernel, blocks, capacity), out_s...  33.2 us
    ppermute x14, waiting for transfers between devices, swap(): lax.ppermute(array, axis, [(i, i ^ bit) for i in range(lax.axis_size(axis...  28.7 us
    pallas_call x4, Pallas kernels, backward(): pl.pallas_call(functools.partial(kernel, capacity, total // 2), out_shape...  17.6 us
    ppermute x14, starting transfers between devices, swap(): lax.ppermute(array, axis, [(i, i ^ bit) for i in range(lax.axis_size(axis...  13.6 us
    ppermute x6, waiting for transfers between devices, shift(): lax.ppermute(array, axis, [(i, (i + 2 * steps) % size) for i in range(siz...  11.3 us
    ppermute x6, starting transfers between devices, shift(): lax.ppermute(array, axis, [(i, (i + 2 * steps) % size) for i in range(siz...  10.5 us
    all_to_all x1, starting transfers between devices, body(): left = lax.all_to_all(send, 'rows', split_axis=0, concat_axis=0, tiled=True)  7.25 us
    all_to_all x1, waiting for transfers between devices, body(): left = lax.all_to_all(send, 'rows', split_axis=0, concat_axis=0, tiled=True)  5.44 us
  transfers between devices with their start and end apart: 21, of which 12 were waited for; matrix products, arithmetic and copies ran while one was open for 2% of the time, Pallas kernels for 28%

profile of v5, /device:TPU:0, one launch (start us, length us, event | category | flops | bytes accessed | tf_op | source)
XLA Modules:
  0.0 138.2 jit_solution(7513116086411557007)
XLA Ops:
  0.7 0.9 select_reduce_fusion
  1.5 0.7 compare_select_fusion.4
  2.2 0.2 convert_reduce_fusion
  2.4 0.1 select_reduce_fusion.1
  2.5 0.1 convert_element_type.66
  2.6 0.7 stack.118
  3.3 0.7 fusion.9
  4.0 0.1 stack.99
  4.0 0.7 fusion.3
  4.7 7.3 %all-to-all-start = ((bf16[8,8,1024]{2,1,0:T(8,128)(2,1)}), bf16[8,8,1024]{2,1,0:T(8,128)(2,1)S(1)}, u32[]{:S(2)}, u32[]{:S(2)}) async-start(bf16[8,8,1024]{2,1,0:T(8,128)(2,1)} %fusion.3), calls=%async_computation | async-start | bytes 262144 | tf_op jit(solution)/shard_map/all_to_all | solution.py:358
  12.0 0.8 broadcast_in_dim.90
  12.8 0.8 multiply_convert_fusion
  13.6 0.1 broadcast_select_fusion
  13.8 0.1 pad_add_fusion
  13.9 5.4 %all-to-all-done.left = bf16[8,8,1024]{2,1,0:T(8,128)(2,1)S(1)} async-done(((bf16[8,8,1024]{2,1,0:T(8,128)(2,1)}), bf16[8,8,1024]{2,1,0:T(8,128)(2,1)S(1)}, u32[]{:S(2)}, u32[]{:S(2)}) %all-to-all-start) | async-done | bytes 131104 | tf_op jit(solution)/shard_map/all_to_all | solution.py:358
  19.4 0.1 reshape.102.codes.refs_0_
  19.4 9.1 %forward.4 = (f32[64,1024]{1,0:T(8,128)S(1)}, f32[64,1024]{1,0:T(8,128)S(1)}, bf16[129,256,512]{2,1,0:T(8,128)(2,1)}) custom-call(s32[128]{0:T(128)S(1)} %reshape.102.codes.refs_0_, s32[2]{0:T(128)S(1)} %get-tuple-element.76.where, bf16[8,8,1024]{2,1,0:T(8,128)(2,1)S(1)} %all-to-all-done.left, bf16[32,8,1024]{2,1,0:T(8,128)(2,1)S(1)} %pad_maximum_fusion.right, ...), custom_call_target="tpu_custom_call" | custom-call | flops 32 | bytes 64 | tf_op jit(solution)/shard_map/forward/pallas_call | solution.py:174
  28.6 0.3 collective-permute-start
  28.9 6.6 %forward.5 = (f32[64,1024]{1,0:T(8,128)S(1)}, f32[64,1024]{1,0:T(8,128)S(1)}, bf16[129,256,512]{2,1,0:T(8,128)(2,1)}) custom-call(s32[128]{0:T(128)S(1)} %reshape.102.codes.refs_0_, s32[2]{0:T(128)S(1)} %get-tuple-element.77.where, bf16[8,8,1024]{2,1,0:T(8,128)(2,1)S(1)} %all-to-all-done.left, ...), custom_call_target="tpu_custom_call", output_to_operand_aliasing={{2}: (5, {})} | custom-call | flops 32 | bytes 64 | tf_op jit(solution)/shard_map/forward/pallas_call | solution.py:174
  35.5 0.9 collective-permute-start.1
  36.5 0.7 collective-permute-start.2
  37.1 0.1 pad_add_fusion.2
  37.2 4.9 %forward.6 = (f32[64,1024]{1,0:T(8,128)S(1)}, f32[64,1024]{1,0:T(8,128)S(1)}, bf16[129,256,512]{2,1,0:T(8,128)(2,1)}) custom-call(s32[128]{0:T(128)S(1)} %reshape.102.codes.refs_0_, s32[2]{0:T(128)S(1)} %get-tuple-element.78.where, bf16[8,8,1024]{2,1,0:T(8,128)(2,1)S(1)} %all-to-all-done.left, ...), custom_call_target="tpu_custom_call", output_to_operand_aliasing={{2}: (5, {})} | custom-call | flops 32 | bytes 64 | tf_op jit(solution)/shard_map/forward/pallas_call | solution.py:174
  42.1 4.6 %collective-permute-start.3 = (f32[64,1024]{1,0:T(8,128)S(1)}, f32[64,1024]{1,0:T(8,128)S(1)}, u32[]{:S(2)}, u32[]{:S(2)}) collective-permute-start(f32[64,1024]{1,0:T(8,128)S(1)} %get-tuple-element.44), channel_id=1, source_target_pairs={{0,4},{4,0},{8,12},{12,8},{16,20},{20,16},{24,28},{28,24},{1,5},{5... | collective-permute-start | bytes 786440 | tf_op jit(solution)/shard_map/ppermute | solution.py:304
  46.7 2.1 %collective-permute-done.2 = f32[64,1024]{1,0:T(8,128)S(1)} collective-permute-done((f32[64,1024]{1,0:T(8,128)S(1)}, f32[64,1024]{1,0:T(8,128)S(1)}, u32[]{:S(2)}, u32[]{:S(2)}) %collective-permute-start.2) | collective-permute-done | bytes 262176 | tf_op jit(solution)/shard_map/ppermute | solution.py:309
  48.8 7.7 %collective-permute-start.5 = (f32[64,1024]{1,0:T(8,128)S(1)}, f32[64,1024]{1,0:T(8,128)S(1)}, u32[]{:S(2)}, u32[]{:S(2)}) collective-permute-start(f32[64,1024]{1,0:T(8,128)S(1)} %add.129), channel_id=1, source_target_pairs={{0,16},{4,20},{8,24},{12,28},{16,0},{20,4},{24,8},{28,12},{1,17},{... | collective-permute-start | bytes 786440 | tf_op jit(solution)/shard_map/ppermute | solution.py:309
  56.5 12.6 %forward.7 = (f32[64,1024]{1,0:T(8,128)S(1)}, f32[64,1024]{1,0:T(8,128)S(1)}, bf16[129,256,512]{2,1,0:T(8,128)(2,1)}) custom-call(s32[128]{0:T(128)S(1)} %reshape.102.codes.refs_0_, s32[2]{0:T(128)S(1)} %get-tuple-element.79.where, bf16[8,8,1024]{2,1,0:T(8,128)(2,1)S(1)} %all-to-all-done.left, ...), custom_call_target="tpu_custom_call", output_to_operand_aliasing={{2}: (5, {})} | custom-call | flops 32 | bytes 64 | tf_op jit(solution)/shard_map/forward/pallas_call | solution.py:174
  69.1 2.6 %collective-permute-start.4 = (f32[64,1024]{1,0:T(8,128)S(1)}, f32[64,1024]{1,0:T(8,128)S(1)}, u32[]{:S(2)}, u32[]{:S(2)}) collective-permute-start(f32[64,1024]{1,0:T(8,128)S(1)} %get-tuple-element.50), channel_id=1, source_target_pairs={{0,4},{4,0},{8,12},{12,8},{16,20},{20,16},{24,28},{28,24},{1,5},{5... | collective-permute-start | bytes 786440 | tf_op jit(solution)/shard_map/ppermute | solution.py:304
  71.8 0.1 collective-permute-start.6
  71.9 5.2 %collective-permute-done.4 = f32[64,1024]{1,0:T(8,128)S(1)} collective-permute-done((f32[64,1024]{1,0:T(8,128)S(1)}, f32[64,1024]{1,0:T(8,128)S(1)}, u32[]{:S(2)}, u32[]{:S(2)}) %collective-permute-start.4) | collective-permute-done | bytes 262176 | tf_op jit(solution)/shard_map/ppermute | solution.py:304
  77.0 4.8 %collective-permute-done.6 = f32[64,1024]{1,0:T(8,128)S(1)} collective-permute-done((f32[64,1024]{1,0:T(8,128)S(1)}, f32[64,1024]{1,0:T(8,128)S(1)}, u32[]{:S(2)}, u32[]{:S(2)}) %collective-permute-start.6) | collective-permute-done | bytes 262176 | tf_op jit(solution)/shard_map/ppermute | solution.py:309
  81.8 0.1 add_convert_fusion.refs_0_
  81.9 0.1 collective-permute-start.9
  82.0 0.7 collective-permute-start.8
  82.6 1.4 collective-permute-start.7
  84.0 0.1 pad_add_fusion.8
  84.1 0.3 collective-permute-start.10
  84.4 4.0 %collective-permute-done.9.refs_3_ = bf16[64,1024]{1,0:T(8,128)(2,1)S(1)} collective-permute-done((bf16[64,1024]{1,0:T(8,128)(2,1)S(1)}, bf16[64,1024]{1,0:T(8,128)(2,1)S(1)}, u32[]{:S(2)}, u32[]{:S(2)}) %collective-permute-start.9) | collective-permute-done | bytes 131104 | tf_op jit(solution)/shard_map/ppermute | solution.py:309
  88.3 0.3 collective-permute-start.13
  88.6 1.7 %collective-permute-start.12 = (bf16[64,1024]{1,0:T(8,128)(2,1)S(1)}, bf16[64,1024]{1,0:T(8,128)(2,1)S(1)}, u32[]{:S(2)}, u32[]{:S(2)}) collective-permute-start(bf16[64,1024]{1,0:T(8,128)(2,1)S(1)} %collective-permute-done.8.refs_2_), channel_id=1, source_target_pairs={{0,4},{4,0},{8,12},{12,8},{16,20},{20,16},{24,28},{28,24},{1,5},{5... | collective-permute-start | bytes 393224 | tf_op jit(solution)/shard_map/ppermute | solution.py:304
  90.4 0.4 collective-permute-done.7.refs_1_
  90.8 0.3 collective-permute-start.11
  91.1 0.1 pad_add_fusion.7
  91.1 2.2 %collective-permute-done.13.refs_7_ = bf16[64,1024]{1,0:T(8,128)(2,1)S(1)} collective-permute-done((bf16[64,1024]{1,0:T(8,128)(2,1)S(1)}, bf16[64,1024]{1,0:T(8,128)(2,1)S(1)}, u32[]{:S(2)}, u32[]{:S(2)}) %collective-permute-start.13) | collective-permute-done | bytes 131104 | tf_op jit(solution)/shard_map/ppermute | solution.py:304
  93.3 1.4 %collective-permute-done.12.refs_6_ = bf16[64,1024]{1,0:T(8,128)(2,1)S(1)} collective-permute-done((bf16[64,1024]{1,0:T(8,128)(2,1)S(1)}, bf16[64,1024]{1,0:T(8,128)(2,1)S(1)}, u32[]{:S(2)}, u32[]{:S(2)}) %collective-permute-start.12) | collective-permute-done | bytes 131104 | tf_op jit(solution)/shard_map/ppermute | solution.py:304
  94.7 1.4 %collective-permute-done.11.refs_5_ = bf16[64,1024]{1,0:T(8,128)(2,1)S(1)} collective-permute-done((bf16[64,1024]{1,0:T(8,128)(2,1)S(1)}, bf16[64,1024]{1,0:T(8,128)(2,1)S(1)}, u32[]{:S(2)}, u32[]{:S(2)}) %collective-permute-start.11) | collective-permute-done | bytes 131104 | tf_op jit(solution)/shard_map/ppermute | solution.py:304
  96.1 4.6 %backward.4 = (f32[64,4096]{1,0:T(8,128)S(1)}, bf16[8,64,1024]{2,1,0:T(8,128)(2,1)S(1)}) custom-call(s32[128]{0:T(128)S(1)} %reshape.102.codes.refs_0_, s32[3]{0:T(128)S(1)} %get-tuple-element.72.where, bf16[129,256,512]{2,1,0:T(8,128)(2,1)} %get-tuple-element.48.jac.refs_2_, bf16[64,1024]{1,0:T(8,128)(2,1)S(1)} %add_convert_fusion.refs_0_, ...), custom_call_target="tpu_custom_call" | custom-call | flops 16 | bytes 64 | tf_op jit(solution)/shard_map/backward/pallas_call | solution.py:254
  100.7 0.1 collective-permute-start.14
  100.7 4.5 %backward.5 = f32[64,4096]{1,0:T(8,128)S(1)} custom-call(s32[128]{0:T(128)S(1)} %reshape.102.codes.refs_0_, s32[3]{0:T(128)S(1)} %get-tuple-element.73.refs_1_, bf16[129,256,512]{2,1,0:T(8,128)(2,1)} %get-tuple-element.48.jac.refs_2_, bf16[8,64,1024]{2,1,0:T(8,128)(2,1)S(1)} %get-tuple-element.57.refs_3_), custom_call_target="tpu_custom_call" | custom-call | flops 16 | bytes 64 | tf_op jit(solution)/shard_map/backward/pallas_call | solution.py:254
  105.3 0.1 fusion
  105.4 1.2 collective-permute-start.16
  106.6 4.9 %backward.7 = f32[64,4096]{1,0:T(8,128)S(1)} custom-call(s32[128]{0:T(128)S(1)} %reshape.102.codes.refs_0_, s32[3]{0:T(128)S(1)} %get-tuple-element.63.refs_1_, bf16[129,256,512]{2,1,0:T(8,128)(2,1)} %get-tuple-element.48.jac.refs_2_, bf16[8,64,1024]{2,1,0:T(8,128)(2,1)S(1)} %get-tuple-element.57.refs_3_), custom_call_target="tpu_custom_call" | custom-call | flops 16 | bytes 64 | tf_op jit(solution)/shard_map/backward/pallas_call | solution.py:254
  111.5 0.9 collective-permute-start.15
  112.5 3.6 %backward.6 = f32[64,4096]{1,0:T(8,128)S(1)} custom-call(s32[128]{0:T(128)S(1)} %reshape.102.codes.refs_0_, s32[3]{0:T(128)S(1)} %get-tuple-element.71.refs_1_, bf16[129,256,512]{2,1,0:T(8,128)(2,1)} %get-tuple-element.48.jac.refs_2_, bf16[8,64,1024]{2,1,0:T(8,128)(2,1)S(1)} %get-tuple-element.57.refs_3_), custom_call_target="tpu_custom_call" | custom-call | flops 16 | bytes 64 | tf_op jit(solution)/shard_map/backward/pallas_call | solution.py:254
  116.1 4.1 %collective-permute-done.16 = bf16[64,4096]{1,0:T(8,128)(2,1)S(1)} collective-permute-done((bf16[64,4096]{1,0:T(8,128)(2,1)S(1)}, bf16[64,4096]{1,0:T(8,128)(2,1)S(1)}, u32[]{:S(2)}, u32[]{:S(2)}) %collective-permute-start.16) | collective-permute-done | bytes 524320 | tf_op jit(solution)/shard_map/ppermute | solution.py:304
  120.2 0.1 convert_add_fusion.1.refs_0_
  120.3 0.1 fusion.1
  120.4 0.4 collective-permute-start.18
  120.8 13.5 %collective-permute-done.18 = bf16[64,4096]{1,0:T(8,128)(2,1)S(1)} collective-permute-done((bf16[64,4096]{1,0:T(8,128)(2,1)S(1)}, bf16[64,4096]{1,0:T(8,128)(2,1)S(1)}, u32[]{:S(2)}, u32[]{:S(2)}) %collective-permute-start.18) | collective-permute-done | bytes 524320 | tf_op jit(solution)/shard_map/ppermute | solution.py:304
  134.3 0.1 convert_add_fusion.refs_2_
  134.5 0.1 collective-permute-start.19
  134.6 1.7 %place.2.refs_0_ = f32[64,16384]{1,0:T(8,128)} custom-call(s32[1]{0:T(128)} %bitcast.where, f32[64,4096]{1,0:T(8,128)S(1)} %convert_add_fusion.1.refs_0_, f32[64,4096]{1,0:T(8,128)S(1)} %collective-permute-done.17.refs_1_, f32[64,4096]{1,0:T(8,128)S(1)} %convert_add_fusion.refs_2_), custom_call_target="tpu_custom_call" | custom-call | tf_op jit(solution)/shard_map/place/pallas_call | solution.py:291
  136.3 0.9 collective-permute-done.19.refs_1_
  137.2 1.0 place.3
  (21 shorter events, 0.3 us)
Async XLA Ops:
  4.7 14.6 %all-to-all-start = ((bf16[8,8,1024]{2,1,0:T(8,128)(2,1)}), bf16[8,8,1024]{2,1,0:T(8,128)(2,1)S(1)}, u32[]{:S(2)}, u32[]{:S(2)}) async-start(bf16[8,8,1024]{2,1,0:T(8,128)(2,1)} %fusion.3), calls=%async_computation | async-start | bytes 262144 | tf_op jit(solution)/shard_map/all_to_all | solution.py:358
  28.6 7.8 %collective-permute-start = (f32[64,1024]{1,0:T(8,128)S(1)}, f32[64,1024]{1,0:T(8,128)S(1)}, u32[]{:S(2)}, u32[]{:S(2)}) collective-permute-start(f32[64,1024]{1,0:T(8,128)S(1)} %get-tuple-element.35), channel_id=1, source_target_pairs={{0,4},{4,0},{8,12},{12,8},{16,20},{20,16},{24,28},{28,24},{1,5},{5... | collective-permute-start | bytes 786440 | tf_op jit(solution)/shard_map/ppermute | solution.py:304
  35.5 11.2 %collective-permute-start.1 = (f32[64,1024]{1,0:T(8,128)S(1)}, f32[64,1024]{1,0:T(8,128)S(1)}, u32[]{:S(2)}, u32[]{:S(2)}) collective-permute-start(f32[64,1024]{1,0:T(8,128)S(1)} %get-tuple-element.39), channel_id=1, source_target_pairs={{0,4},{4,0},{8,12},{12,8},{16,20},{20,16},{24,28},{28,24},{1,5},{5... | collective-permute-start | bytes 786440 | tf_op jit(solution)/shard_map/ppermute | solution.py:304
  36.5 12.4 %collective-permute-start.2 = (f32[64,1024]{1,0:T(8,128)S(1)}, f32[64,1024]{1,0:T(8,128)S(1)}, u32[]{:S(2)}, u32[]{:S(2)}) collective-permute-start(f32[64,1024]{1,0:T(8,128)S(1)} %add.127), channel_id=1, source_target_pairs={{0,24},{4,28},{8,0},{12,4},{16,8},{20,12},{24,16},{28,20},{1,25},{... | collective-permute-start | bytes 786440 | tf_op jit(solution)/shard_map/ppermute | solution.py:309
  42.1 29.6 %collective-permute-start.3 = (f32[64,1024]{1,0:T(8,128)S(1)}, f32[64,1024]{1,0:T(8,128)S(1)}, u32[]{:S(2)}, u32[]{:S(2)}) collective-permute-start(f32[64,1024]{1,0:T(8,128)S(1)} %get-tuple-element.44), channel_id=1, source_target_pairs={{0,4},{4,0},{8,12},{12,8},{16,20},{20,16},{24,28},{28,24},{1,5},{5... | collective-permute-start | bytes 786440 | tf_op jit(solution)/shard_map/ppermute | solution.py:304
  48.8 23.0 %collective-permute-start.5 = (f32[64,1024]{1,0:T(8,128)S(1)}, f32[64,1024]{1,0:T(8,128)S(1)}, u32[]{:S(2)}, u32[]{:S(2)}) collective-permute-start(f32[64,1024]{1,0:T(8,128)S(1)} %add.129), channel_id=1, source_target_pairs={{0,16},{4,20},{8,24},{12,28},{16,0},{20,4},{24,8},{28,12},{1,17},{... | collective-permute-start | bytes 786440 | tf_op jit(solution)/shard_map/ppermute | solution.py:309
  69.1 7.9 %collective-permute-start.4 = (f32[64,1024]{1,0:T(8,128)S(1)}, f32[64,1024]{1,0:T(8,128)S(1)}, u32[]{:S(2)}, u32[]{:S(2)}) collective-permute-start(f32[64,1024]{1,0:T(8,128)S(1)} %get-tuple-element.50), channel_id=1, source_target_pairs={{0,4},{4,0},{8,12},{12,8},{16,20},{20,16},{24,28},{28,24},{1,5},{5... | collective-permute-start | bytes 786440 | tf_op jit(solution)/shard_map/ppermute | solution.py:304
  71.8 10.0 %collective-permute-start.6 = (f32[64,1024]{1,0:T(8,128)S(1)}, f32[64,1024]{1,0:T(8,128)S(1)}, u32[]{:S(2)}, u32[]{:S(2)}) collective-permute-start(f32[64,1024]{1,0:T(8,128)S(1)} %add.131), channel_id=1, source_target_pairs={{0,8},{4,12},{8,16},{12,20},{16,24},{20,28},{24,0},{28,4},{1,9},{5... | collective-permute-start | bytes 786440 | tf_op jit(solution)/shard_map/ppermute | solution.py:309
  81.9 6.4 %collective-permute-start.9 = (bf16[64,1024]{1,0:T(8,128)(2,1)S(1)}, bf16[64,1024]{1,0:T(8,128)(2,1)S(1)}, u32[]{:S(2)}, u32[]{:S(2)}) collective-permute-start(bf16[64,1024]{1,0:T(8,128)(2,1)S(1)} %add_convert_fusion.refs_0_), channel_id=1, source_target_pairs={{0,24},{4,28},{8,0},{12,4},{16,8},{20,12},{24,16},{28,20},{1,25},{... | collective-permute-start | bytes 393224 | tf_op jit(solution)/shard_map/ppermute | solution.py:309
  82.0 6.7 %collective-permute-start.8 = (bf16[64,1024]{1,0:T(8,128)(2,1)S(1)}, bf16[64,1024]{1,0:T(8,128)(2,1)S(1)}, u32[]{:S(2)}, u32[]{:S(2)}) collective-permute-start(bf16[64,1024]{1,0:T(8,128)(2,1)S(1)} %add_convert_fusion.refs_0_), channel_id=1, source_target_pairs={{0,16},{4,20},{8,24},{12,28},{16,0},{20,4},{24,8},{28,12},{1,17},{... | collective-permute-start | bytes 393224 | tf_op jit(solution)/shard_map/ppermute | solution.py:309
  82.6 8.1 %collective-permute-start.7 = (bf16[64,1024]{1,0:T(8,128)(2,1)S(1)}, bf16[64,1024]{1,0:T(8,128)(2,1)S(1)}, u32[]{:S(2)}, u32[]{:S(2)}) collective-permute-start(bf16[64,1024]{1,0:T(8,128)(2,1)S(1)} %add_convert_fusion.refs_0_), channel_id=1, source_target_pairs={{0,8},{4,12},{8,16},{12,20},{16,24},{20,28},{24,0},{28,4},{1,9},{5... | collective-permute-start | bytes 393224 | tf_op jit(solution)/shard_map/ppermute | solution.py:309
  84.1 7.1 %collective-permute-start.10 = (bf16[64,1024]{1,0:T(8,128)(2,1)S(1)}, bf16[64,1024]{1,0:T(8,128)(2,1)S(1)}, u32[]{:S(2)}, u32[]{:S(2)}) collective-permute-start(bf16[64,1024]{1,0:T(8,128)(2,1)S(1)} %add_convert_fusion.refs_0_), channel_id=1, source_target_pairs={{0,4},{4,0},{8,12},{12,8},{16,20},{20,16},{24,28},{28,24},{1,5},{5... | collective-permute-start | bytes 393224 | tf_op jit(solution)/shard_map/ppermute | solution.py:304
  88.3 5.0 %collective-permute-start.13 = (bf16[64,1024]{1,0:T(8,128)(2,1)S(1)}, bf16[64,1024]{1,0:T(8,128)(2,1)S(1)}, u32[]{:S(2)}, u32[]{:S(2)}) collective-permute-start(bf16[64,1024]{1,0:T(8,128)(2,1)S(1)} %collective-permute-done.9.refs_3_), channel_id=1, source_target_pairs={{0,4},{4,0},{8,12},{12,8},{16,20},{20,16},{24,28},{28,24},{1,5},{5... | collective-permute-start | bytes 393224 | tf_op jit(solution)/shard_map/ppermute | solution.py:304
  88.6 6.1 %collective-permute-start.12 = (bf16[64,1024]{1,0:T(8,128)(2,1)S(1)}, bf16[64,1024]{1,0:T(8,128)(2,1)S(1)}, u32[]{:S(2)}, u32[]{:S(2)}) collective-permute-start(bf16[64,1024]{1,0:T(8,128)(2,1)S(1)} %collective-permute-done.8.refs_2_), channel_id=1, source_target_pairs={{0,4},{4,0},{8,12},{12,8},{16,20},{20,16},{24,28},{28,24},{1,5},{5... | collective-permute-start | bytes 393224 | tf_op jit(solution)/shard_map/ppermute | solution.py:304
  90.8 5.3 %collective-permute-start.11 = (bf16[64,1024]{1,0:T(8,128)(2,1)S(1)}, bf16[64,1024]{1,0:T(8,128)(2,1)S(1)}, u32[]{:S(2)}, u32[]{:S(2)}) collective-permute-start(bf16[64,1024]{1,0:T(8,128)(2,1)S(1)} %collective-permute-done.7.refs_1_), channel_id=1, source_target_pairs={{0,4},{4,0},{8,12},{12,8},{16,20},{20,16},{24,28},{28,24},{1,5},{5... | collective-permute-start | bytes 393224 | tf_op jit(solution)/shard_map/ppermute | solution.py:304
  100.7 4.6 %collective-permute-start.14 = (f32[64,4096]{1,0:T(8,128)S(1)}, f32[64,4096]{1,0:T(8,128)S(1)}, u32[]{:S(2)}, u32[]{:S(2)}) collective-permute-start(f32[64,4096]{1,0:T(8,128)S(1)} %get-tuple-element.58), channel_id=1, source_target_pairs={{0,1},{1,0},{2,3},{3,2},{4,5},{5,4},{6,7},{7,6},{8,9},{9,8},{10,11... | collective-permute-start | bytes 3145736 | tf_op jit(solution)/shard_map/ppermute | solution.py:304
  105.4 14.8 %collective-permute-start.16 = (bf16[64,4096]{1,0:T(8,128)(2,1)S(1)}, bf16[64,4096]{1,0:T(8,128)(2,1)S(1)}, u32[]{:S(2)}, u32[]{:S(2)}) collective-permute-start(bf16[64,4096]{1,0:T(8,128)(2,1)S(1)} %fusion), channel_id=1, source_target_pairs={{0,2},{1,3},{2,0},{3,1},{4,6},{5,7},{6,4},{7,5},{8,10},{9,11},{10,... | collective-permute-start | bytes 1572872 | tf_op jit(solution)/shard_map/ppermute | solution.py:304
  111.5 8.8 %collective-permute-start.15 = (f32[64,4096]{1,0:T(8,128)S(1)}, f32[64,4096]{1,0:T(8,128)S(1)}, u32[]{:S(2)}, u32[]{:S(2)}) collective-permute-start(f32[64,4096]{1,0:T(8,128)S(1)} %backward.7), channel_id=1, source_target_pairs={{0,1},{1,0},{2,3},{3,2},{4,5},{5,4},{6,7},{7,6},{8,9},{9,8},{10,11... | collective-permute-start | bytes 3145736 | tf_op jit(solution)/shard_map/ppermute | solution.py:304
  120.4 13.9 %collective-permute-start.18 = (bf16[64,4096]{1,0:T(8,128)(2,1)S(1)}, bf16[64,4096]{1,0:T(8,128)(2,1)S(1)}, u32[]{:S(2)}, u32[]{:S(2)}) collective-permute-start(bf16[64,4096]{1,0:T(8,128)(2,1)S(1)} %fusion.1), channel_id=1, source_target_pairs={{0,2},{1,3},{2,0},{3,1},{4,6},{5,7},{6,4},{7,5},{8,10},{9,11},{10,... | collective-permute-start | bytes 1572872 | tf_op jit(solution)/shard_map/ppermute | solution.py:304
  120.8 13.8 %collective-permute-start.17 = (f32[64,4096]{1,0:T(8,128)S(1)}, f32[64,4096]{1,0:T(8,128)S(1)}, u32[]{:S(2)}, u32[]{:S(2)}) collective-permute-start(f32[64,4096]{1,0:T(8,128)S(1)} %convert_add_fusion.1.refs_0_), channel_id=1, source_target_pairs={{0,1},{1,0},{2,3},{3,2},{4,5},{5,4},{6,7},{7,6},{8,9},{9,8},{10,11... | collective-permute-start | bytes 3145736 | tf_op jit(solution)/shard_map/ppermute | solution.py:304
  134.5 2.7 %collective-permute-start.19 = (f32[64,4096]{1,0:T(8,128)S(1)}, f32[64,4096]{1,0:T(8,128)S(1)}, u32[]{:S(2)}, u32[]{:S(2)}) collective-permute-start(f32[64,4096]{1,0:T(8,128)S(1)} %convert_add_fusion.refs_2_), channel_id=1, source_target_pairs={{0,1},{1,0},{2,3},{3,2},{4,5},{5,4},{6,7},{7,6},{8,9},{9,8},{10,11... | collective-permute-start | bytes 3145736 | tf_op jit(solution)/shard_map/ppermute | solution.py:304

commit v6 on v4

--- a/solution.py
+++ b/solution.py
@@ -59,12 +59,16 @@
 
 
 def forward_kernel(blocks, capacity, codes, where, left, right, vectors, *refs):
-    near, far, jac, todo, part, even, odd, sems = refs[-8:]
+    near, far, jac, todo, columns, part, even, odd, sems = refs[-9:]
     spare = codes.shape[0]
     rows = left.shape[2] // BLK_R
     part[...] = jnp.zeros_like(part)
     start = 2 * capacity * where[0]
     found = collect(codes, todo, start, 2 * capacity, 0, blocks * rows)
+    for k in range(2):
+        for at in range(0, left.shape[2], 128):
+            lanes = left[2 * where[0] + k, :, at : at + 128]
+            columns[k, at : at + 128, :] = lanes.astype(f32).T.astype(bf16)
     steps = (found + 1) // 2
 
     def decode(place):
@@ -75,9 +79,9 @@
 
     def make(buffer, place):
         block, row, group, _ = decode(place)
-        angles = left[group, :, pl.ds(pl.multiple_of(row * BLK_R, BLK_R), BLK_R)]
-        both = lax.dot_general(
-            angles, right[block], (((0,), (0,)), ((), ())), preferred_element_type=f32
+        at = pl.ds(pl.multiple_of(row * BLK_R, BLK_R), BLK_R)
+        both = jnp.dot(
+            columns[lax.rem(group, 2), at, :], right[block], preferred_element_type=f32
         )
         turns, weight = both[:, :BLK_P], both[:, BLK_P:]
         rest = turns - jnp.round(turns)
@@ -153,6 +157,7 @@
         out_specs=(vmem, vmem, hbm),
         scratch_shapes=[
             pltpu.SMEM((2 * capacity + 1,), jnp.int32),
+            pltpu.VMEM((2, width, PIECES), bf16),
             pltpu.VMEM((2, count, width), f32),
             pltpu.VMEM((2, BLK_R, BLK_P), bf16),
             pltpu.VMEM((2, BLK_R, BLK_P), bf16),
@@ -240,34 +245,41 @@
     return (result, pieces) if joined else result
 
 
-def place_kernel(quarters, where, *refs):
-    *sources, out, sems = refs
-    sources = sources[-len(quarters) :]
-    wide = sources[0].shape[1]
+def place_kernel(quarters, addends, where, *refs):
+    *sources, out, sums, sems = refs
+    sources = sources[-addends * len(quarters) :]
+    wide = sums.shape[2]
     copies = []
     for k, (mine, chunk) in enumerate(quarters):
+        total = sources[addends * k][...].astype(f32)
+        for source in sources[addends * k + 1 : addends * (k + 1)]:
+            total = total + source[...].astype(f32)
+        sums[k] = total
         half = where[0] if mine else 1 - where[0]
         at = pl.ds(pl.multiple_of((2 * half + chunk) * wide, wide), wide)
-        copies.append(pltpu.make_async_copy(sources[k], out.at[:, at], sems.at[k]))
-    for copy in copies:
-        copy.start()
+        copies.append(pltpu.make_async_copy(sums.at[k], out.at[:, at], sems.at[k]))
+        copies[-1].start()
     for copy in copies:
         copy.wait()
 
 
-def place(where, into, quarters, sources):
+def place(where, into, quarters, groups):
     hbm = pl.BlockSpec(memory_space=pl.ANY)
     vmem = pl.BlockSpec(memory_space=pltpu.VMEM)
+    sources = [array for group in groups for array in group]
     count, wide = sources[0].shape
     held = [] if into is None else [into]
     return pl.pallas_call(
-        functools.partial(place_kernel, quarters),
+        functools.partial(place_kernel, quarters, len(groups[0])),
         out_shape=jax.ShapeDtypeStruct((count, 4 * wide), f32),
         in_specs=[pl.BlockSpec(memory_space=pltpu.SMEM)] + [hbm] * len(held) + [vmem] * len(sources),
         out_specs=hbm,
-        scratch_shapes=[pltpu.SemaphoreType.DMA((len(quarters),))],
+        scratch_shapes=[
+            pltpu.VMEM((len(quarters), count, wide), f32),
+            pltpu.SemaphoreType.DMA((len(quarters),)),
+        ],
         input_output_aliases={1: 0} if held else {},
-        compiler_params=pltpu.CompilerParams(vmem_limit_bytes=8 << 20),
+        compiler_params=pltpu.CompilerParams(vmem_limit_bytes=10 << 20),
         name="place",
     )(where, *held, *sources)
 
@@ -376,6 +388,7 @@
         return backward(codes, where, jac, pieces, quarter, capacity)
 
     quarter = blocks_here // 4
+    pairs = []
     sums = []
     for chunk in range(2):
         given, pieces = terms((2 * (1 - core) + chunk) * quarter, pieces)
@@ -383,17 +396,21 @@
         kept, pieces = terms((2 * core + chunk) * quarter, pieces)
         chunk_sum = kept + given
         bit = 2
+        pair = (chunk_sum, jnp.zeros_like(chunk_sum))
         while bit < members:
             rounded = lax.reduce_precision(chunk_sum, 8, 7)
             sent = rounded.astype(bf16)
             codes, sent, sums = lax.optimization_barrier((codes, sent, sums))
-            chunk_sum = rounded + swap(sent, "grp", bit).astype(f32)
+            pair = (sent, swap(sent, "grp", bit))
+            chunk_sum = rounded + pair[1].astype(f32)
             bit *= 2
         sums.append(chunk_sum)
-    held = [(chunk_sum, swap(chunk_sum, "grp", 1)) for chunk_sum in sums]
+        pairs.append(pair)
     where = core.reshape(1)
-    total = place(where, None, ((True, 0), (False, 0), (True, 1)), (*held[0], held[1][0]))
-    return place(where, total, ((False, 1),), (held[1][1],))
+    early = place(where, None, ((True, 0), (False, 0)), ((sums[0],), (swap(sums[0], "grp", 1),)))
+    last = pairs[1]
+    across = tuple(swap(array, "grp", 1) for array in last)
+    return place(where, early, ((True, 1), (False, 1)), (last, across))
 
 
 def solution(mesh):

time: 134 us -> 133 us (level)
  Pallas kernels: 36 us -> 45.2 us
  starting transfers between devices: 41.5 us -> 34 us
  waiting for transfers between devices: 46.5 us -> 43.1 us
    pallas_call x4, Pallas kernels: 19.2 us -> 25.1 us  [forward(): pl.pallas_call(functools.partial(forward_kernel, blocks, capacity), out_s...]
    ppermute x14 -> x15, starting transfers between devices: 26.8 us -> 21.8 us  [swap(): lax.ppermute(array, axis, [(i, i ^ bit) for i in range(lax.axis_size(axis...]
    pallas_call x4, Pallas kernels: 14.1 us -> 17.3 us  [backward(): pl.pallas_call(functools.partial(kernel, capacity, total // 2), out_shape...]
    ppermute x14 -> x15, waiting for transfers between devices: 23 us -> 20.2 us  [swap(): lax.ppermute(array, axis, [(i, i ^ bit) for i in range(lax.axis_size(axis...]
    ppermute x6, starting transfers between devices: 7.49 us -> 4.95 us  [shift(): lax.ppermute(array, axis, [(i, (i + 2 * steps) % size) for i in range(siz...]
  transfers between devices with their start and end apart: 21 -> 22, of which waited for: 9 -> 11; matrix products, arithmetic and copies ran while one was open for 2% -> 2% of each run, Pallas kernels for 21% -> 23%
where the time goes in v6:
time: 133 us
  Pallas kernels  45.2 us (34%)
  waiting for transfers between devices  43.1 us (32%)
  starting transfers between devices  34 us (26%)
  other arithmetic  5.76 us (4%)
  local copies, waits for them, and re-layouts  4.24 us (3%)
    pallas_call x4, Pallas kernels, forward(): pl.pallas_call(functools.partial(forward_kernel, blocks, capacity), out_s...  25.1 us
    ppermute x15, starting transfers between devices, swap(): lax.ppermute(array, axis, [(i, i ^ bit) for i in range(lax.axis_size(axis...  21.8 us
    ppermute x15, waiting for transfers between devices, swap(): lax.ppermute(array, axis, [(i, i ^ bit) for i in range(lax.axis_size(axis...  20.2 us
    ppermute x6, waiting for transfers between devices, shift(): lax.ppermute(array, axis, [(i, (i + 2 * steps) % size) for i in range(siz...  17.4 us
    pallas_call x4, Pallas kernels, backward(): pl.pallas_call(functools.partial(kernel, capacity, total // 2), out_shape...  17.3 us
    all_to_all x1, starting transfers between devices, body(): left = lax.all_to_all(send, 'rows', split_axis=0, concat_axis=0, tiled=True)  7.25 us
    all_to_all x1, waiting for transfers between devices, body(): left = lax.all_to_all(send, 'rows', split_axis=0, concat_axis=0, tiled=True)  5.44 us
    ppermute x6, starting transfers between devices, shift(): lax.ppermute(array, axis, [(i, (i + 2 * steps) % size) for i in range(siz...  4.95 us
  transfers between devices with their start and end apart: 22, of which 11 were waited for; matrix products, arithmetic and copies ran while one was open for 2% of the time, Pallas kernels for 23%

profile of v6, /device:TPU:0, one launch (start us, length us, event | category | flops | bytes accessed | tf_op | source)
XLA Modules:
  0.0 133.3 jit_solution(17089593618404188000)
XLA Ops:
  0.7 0.9 select_reduce_fusion
  1.5 0.7 compare_select_fusion.4
  2.2 0.2 convert_reduce_fusion
  2.4 0.1 select_reduce_fusion.1
  2.5 0.1 convert_element_type.62
  2.6 0.7 stack.118
  3.3 0.7 fusion.8
  4.0 0.1 stack.99
  4.0 0.7 fusion.2
  4.7 7.3 %all-to-all-start = ((bf16[8,8,1024]{2,1,0:T(8,128)(2,1)}), bf16[8,8,1024]{2,1,0:T(8,128)(2,1)S(1)}, u32[]{:S(2)}, u32[]{:S(2)}) async-start(bf16[8,8,1024]{2,1,0:T(8,128)(2,1)} %fusion.2), calls=%async_computation | async-start | bytes 262144 | tf_op jit(solution)/shard_map/all_to_all | solution.py:342
  12.0 0.8 broadcast_in_dim.90
  12.8 0.8 multiply_convert_fusion
  13.6 0.1 broadcast_select_fusion
  13.8 0.1 pad_add_fusion
  13.8 0.1 pad_maximum_fusion.right
  13.9 5.4 %all-to-all-done.left = bf16[8,8,1024]{2,1,0:T(8,128)(2,1)S(1)} async-done(((bf16[8,8,1024]{2,1,0:T(8,128)(2,1)}), bf16[8,8,1024]{2,1,0:T(8,128)(2,1)S(1)}, u32[]{:S(2)}, u32[]{:S(2)}) %all-to-all-start) | async-done | bytes 131104 | tf_op jit(solution)/shard_map/all_to_all | solution.py:342
  19.4 0.1 reshape.102.codes.refs_0_
  19.4 1.6 %copy-done = bf16[64,16384]{1,0:T(8,128)(2,1)S(1)} copy-done((bf16[64,16384]{1,0:T(8,128)(2,1)S(1)}, bf16[64,16384]{1,0:T(8,128)(2,1)}, u32[]{:S(2)}) %copy-start) | copy-done | bytes 2097176
  21.0 9.2 %forward.4 = (f32[64,1024]{1,0:T(8,128)S(1)}, f32[64,1024]{1,0:T(8,128)S(1)}, bf16[129,256,512]{2,1,0:T(8,128)(2,1)}) custom-call(s32[128]{0:T(128)S(1)} %reshape.102.codes.refs_0_, s32[2]{0:T(128)S(1)} %get-tuple-element.76.where, bf16[8,8,1024]{2,1,0:T(8,128)(2,1)S(1)} %all-to-all-done.left, bf16[32,8,1024]{2,1,0:T(8,128)(2,1)S(1)} %pad_maximum_fusion.right, ...), custom_call_target="tpu_custom_call" | custom-call | flops 32 | bytes 64 | tf_op jit(solution)/shard_map/forward/pallas_call | solution.py:152
  30.2 0.1 collective-permute-start
  30.4 1.6 %copy-done.1 = bf16[64,16384]{1,0:T(8,128)(2,1)S(1)} copy-done((bf16[64,16384]{1,0:T(8,128)(2,1)S(1)}, bf16[64,16384]{1,0:T(8,128)(2,1)}, u32[]{:S(2)}) %copy-start.1) | copy-done | bytes 2097176
  32.0 6.4 %forward.5 = (f32[64,1024]{1,0:T(8,128)S(1)}, f32[64,1024]{1,0:T(8,128)S(1)}, bf16[129,256,512]{2,1,0:T(8,128)(2,1)}) custom-call(s32[128]{0:T(128)S(1)} %reshape.102.codes.refs_0_, s32[2]{0:T(128)S(1)} %get-tuple-element.77.where, bf16[8,8,1024]{2,1,0:T(8,128)(2,1)S(1)} %all-to-all-done.left, ...), custom_call_target="tpu_custom_call", output_to_operand_aliasing={{2}: (5, {})} | custom-call | flops 32 | bytes 64 | tf_op jit(solution)/shard_map/forward/pallas_call | solution.py:152
  38.4 2.8 %collective-permute-start.1 = (f32[64,1024]{1,0:T(8,128)S(1)}, f32[64,1024]{1,0:T(8,128)S(1)}, u32[]{:S(2)}, u32[]{:S(2)}) collective-permute-start(f32[64,1024]{1,0:T(8,128)S(1)} %get-tuple-element.39), channel_id=1, source_target_pairs={{0,4},{4,0},{8,12},{12,8},{16,20},{20,16},{24,28},{28,24},{1,5},{5... | collective-permute-start | bytes 786440 | tf_op jit(solution)/shard_map/ppermute | solution.py:288
  41.2 0.1 collective-permute-start.2
  41.3 0.1 pad_add_fusion.2
  41.3 3.7 %forward.6 = (f32[64,1024]{1,0:T(8,128)S(1)}, f32[64,1024]{1,0:T(8,128)S(1)}, bf16[129,256,512]{2,1,0:T(8,128)(2,1)}) custom-call(s32[128]{0:T(128)S(1)} %reshape.102.codes.refs_0_, s32[2]{0:T(128)S(1)} %get-tuple-element.78.where, bf16[8,8,1024]{2,1,0:T(8,128)(2,1)S(1)} %all-to-all-done.left, ...), custom_call_target="tpu_custom_call", output_to_operand_aliasing={{2}: (5, {})} | custom-call | flops 32 | bytes 64 | tf_op jit(solution)/shard_map/forward/pallas_call | solution.py:152
  45.1 0.8 collective-permute-start.3
  45.8 0.4 collective-permute-done.1
  46.3 3.9 %collective-permute-done.2 = f32[64,1024]{1,0:T(8,128)S(1)} collective-permute-done((f32[64,1024]{1,0:T(8,128)S(1)}, f32[64,1024]{1,0:T(8,128)S(1)}, u32[]{:S(2)}, u32[]{:S(2)}) %collective-permute-start.2) | collective-permute-done | bytes 262176 | tf_op jit(solution)/shard_map/ppermute | solution.py:293
  50.2 5.8 %forward.7 = (f32[64,1024]{1,0:T(8,128)S(1)}, f32[64,1024]{1,0:T(8,128)S(1)}, bf16[129,256,512]{2,1,0:T(8,128)(2,1)}) custom-call(s32[128]{0:T(128)S(1)} %reshape.102.codes.refs_0_, s32[2]{0:T(128)S(1)} %get-tuple-element.79.where, bf16[8,8,1024]{2,1,0:T(8,128)(2,1)S(1)} %all-to-all-done.left, ...), custom_call_target="tpu_custom_call", output_to_operand_aliasing={{2}: (5, {})} | custom-call | flops 32 | bytes 64 | tf_op jit(solution)/shard_map/forward/pallas_call | solution.py:152
  56.0 2.0 %collective-permute-start.4 = (f32[64,1024]{1,0:T(8,128)S(1)}, f32[64,1024]{1,0:T(8,128)S(1)}, u32[]{:S(2)}, u32[]{:S(2)}) collective-permute-start(f32[64,1024]{1,0:T(8,128)S(1)} %get-tuple-element.50), channel_id=1, source_target_pairs={{0,4},{4,0},{8,12},{12,8},{16,20},{20,16},{24,28},{28,24},{1,5},{5... | collective-permute-start | bytes 786440 | tf_op jit(solution)/shard_map/ppermute | solution.py:288
  58.0 0.2 collective-permute-start.6
  58.3 4.7 %collective-permute-done.5 = f32[64,1024]{1,0:T(8,128)S(1)} collective-permute-done((f32[64,1024]{1,0:T(8,128)S(1)}, f32[64,1024]{1,0:T(8,128)S(1)}, u32[]{:S(2)}, u32[]{:S(2)}) %collective-permute-start.5) | collective-permute-done | bytes 262176 | tf_op jit(solution)/shard_map/ppermute | solution.py:293
  63.0 6.1 %collective-permute-done.6 = f32[64,1024]{1,0:T(8,128)S(1)} collective-permute-done((f32[64,1024]{1,0:T(8,128)S(1)}, f32[64,1024]{1,0:T(8,128)S(1)}, u32[]{:S(2)}, u32[]{:S(2)}) %collective-permute-start.6) | collective-permute-done | bytes 262176 | tf_op jit(solution)/shard_map/ppermute | solution.py:293
  69.1 0.1 add_convert_fusion.refs_0_
  69.1 4.0 %collective-permute-start.9 = (bf16[64,1024]{1,0:T(8,128)(2,1)S(1)}, bf16[64,1024]{1,0:T(8,128)(2,1)S(1)}, u32[]{:S(2)}, u32[]{:S(2)}) collective-permute-start(bf16[64,1024]{1,0:T(8,128)(2,1)S(1)} %add_convert_fusion.refs_0_), channel_id=1, source_target_pairs={{0,24},{4,28},{8,0},{12,4},{16,8},{20,12},{24,16},{28,20},{1,25},{... | collective-permute-start | bytes 393224 | tf_op jit(solution)/shard_map/ppermute | solution.py:293
  73.2 0.6 collective-permute-start.7
  73.8 0.1 pad_add_fusion.8
  73.9 2.0 %collective-permute-start.10 = (bf16[64,1024]{1,0:T(8,128)(2,1)S(1)}, bf16[64,1024]{1,0:T(8,128)(2,1)S(1)}, u32[]{:S(2)}, u32[]{:S(2)}) collective-permute-start(bf16[64,1024]{1,0:T(8,128)(2,1)S(1)} %add_convert_fusion.refs_0_), channel_id=1, source_target_pairs={{0,4},{4,0},{8,12},{12,8},{16,20},{20,16},{24,28},{28,24},{1,5},{5... | collective-permute-start | bytes 393224 | tf_op jit(solution)/shard_map/ppermute | solution.py:288
  75.9 1.8 %collective-permute-start.13 = (bf16[64,1024]{1,0:T(8,128)(2,1)S(1)}, bf16[64,1024]{1,0:T(8,128)(2,1)S(1)}, u32[]{:S(2)}, u32[]{:S(2)}) collective-permute-start(bf16[64,1024]{1,0:T(8,128)(2,1)S(1)} %collective-permute-done.9.refs_3_), channel_id=1, source_target_pairs={{0,4},{4,0},{8,12},{12,8},{16,20},{20,16},{24,28},{28,24},{1,5},{5... | collective-permute-start | bytes 393224 | tf_op jit(solution)/shard_map/ppermute | solution.py:288
  77.7 2.7 %collective-permute-done.8.refs_2_ = bf16[64,1024]{1,0:T(8,128)(2,1)S(1)} collective-permute-done((bf16[64,1024]{1,0:T(8,128)(2,1)S(1)}, bf16[64,1024]{1,0:T(8,128)(2,1)S(1)}, u32[]{:S(2)}, u32[]{:S(2)}) %collective-permute-start.8) | collective-permute-done | bytes 131104 | tf_op jit(solution)/shard_map/ppermute | solution.py:293
  80.4 2.0 %collective-permute-start.12 = (bf16[64,1024]{1,0:T(8,128)(2,1)S(1)}, bf16[64,1024]{1,0:T(8,128)(2,1)S(1)}, u32[]{:S(2)}, u32[]{:S(2)}) collective-permute-start(bf16[64,1024]{1,0:T(8,128)(2,1)S(1)} %collective-permute-done.8.refs_2_), channel_id=1, source_target_pairs={{0,4},{4,0},{8,12},{12,8},{16,20},{20,16},{24,28},{28,24},{1,5},{5... | collective-permute-start | bytes 393224 | tf_op jit(solution)/shard_map/ppermute | solution.py:288
  82.4 0.0 collective-permute-start.11
  82.5 0.1 pad_add_fusion.7
  82.6 2.8 %collective-permute-done.12.refs_6_ = bf16[64,1024]{1,0:T(8,128)(2,1)S(1)} collective-permute-done((bf16[64,1024]{1,0:T(8,128)(2,1)S(1)}, bf16[64,1024]{1,0:T(8,128)(2,1)S(1)}, u32[]{:S(2)}, u32[]{:S(2)}) %collective-permute-start.12) | collective-permute-done | bytes 131104 | tf_op jit(solution)/shard_map/ppermute | solution.py:288
  85.4 2.0 %collective-permute-done.11.refs_5_ = bf16[64,1024]{1,0:T(8,128)(2,1)S(1)} collective-permute-done((bf16[64,1024]{1,0:T(8,128)(2,1)S(1)}, bf16[64,1024]{1,0:T(8,128)(2,1)S(1)}, u32[]{:S(2)}, u32[]{:S(2)}) %collective-permute-start.11) | collective-permute-done | bytes 131104 | tf_op jit(solution)/shard_map/ppermute | solution.py:288
  87.4 4.0 %backward.4 = (f32[64,4096]{1,0:T(8,128)S(1)}, bf16[8,64,1024]{2,1,0:T(8,128)(2,1)S(1)}) custom-call(s32[128]{0:T(128)S(1)} %reshape.102.codes.refs_0_, s32[3]{0:T(128)S(1)} %get-tuple-element.72.where, bf16[129,256,512]{2,1,0:T(8,128)(2,1)} %get-tuple-element.48.jac.refs_2_, bf16[64,1024]{1,0:T(8,128)(2,1)S(1)} %add_convert_fusion.refs_0_, ...), custom_call_target="tpu_custom_call" | custom-call | flops 16 | bytes 64 | tf_op jit(solution)/shard_map/backward/pallas_call | solution.py:231
  91.4 0.1 collective-permute-start.14
  91.5 4.2 %backward.5 = f32[64,4096]{1,0:T(8,128)S(1)} custom-call(s32[128]{0:T(128)S(1)} %reshape.102.codes.refs_0_, s32[3]{0:T(128)S(1)} %get-tuple-element.73.refs_1_, bf16[129,256,512]{2,1,0:T(8,128)(2,1)} %get-tuple-element.48.jac.refs_2_, bf16[8,64,1024]{2,1,0:T(8,128)(2,1)S(1)} %get-tuple-element.57.refs_3_), custom_call_target="tpu_custom_call" | custom-call | flops 16 | bytes 64 | tf_op jit(solution)/shard_map/backward/pallas_call | solution.py:231
  95.7 0.1 fusion
  95.8 8.2 %collective-permute-start.16 = (bf16[64,4096]{1,0:T(8,128)(2,1)S(1)}, bf16[64,4096]{1,0:T(8,128)(2,1)S(1)}, u32[]{:S(2)}, u32[]{:S(2)}) collective-permute-start(bf16[64,4096]{1,0:T(8,128)(2,1)S(1)} %fusion), channel_id=1, source_target_pairs={{0,2},{1,3},{2,0},{3,1},{4,6},{5,7},{6,4},{7,5},{8,10},{9,11},{10,... | collective-permute-start | bytes 1572872 | tf_op jit(solution)/shard_map/ppermute | solution.py:288
  103.9 4.9 %backward.7 = f32[64,4096]{1,0:T(8,128)S(1)} custom-call(s32[128]{0:T(128)S(1)} %reshape.102.codes.refs_0_, s32[3]{0:T(128)S(1)} %get-tuple-element.63.refs_1_, bf16[129,256,512]{2,1,0:T(8,128)(2,1)} %get-tuple-element.48.jac.refs_2_, bf16[8,64,1024]{2,1,0:T(8,128)(2,1)S(1)} %get-tuple-element.57.refs_3_), custom_call_target="tpu_custom_call" | custom-call | flops 16 | bytes 64 | tf_op jit(solution)/shard_map/backward/pallas_call | solution.py:231
  108.9 0.1 collective-permute-start.15
  109.0 4.2 %backward.6 = f32[64,4096]{1,0:T(8,128)S(1)} custom-call(s32[128]{0:T(128)S(1)} %reshape.102.codes.refs_0_, s32[3]{0:T(128)S(1)} %get-tuple-element.71.refs_1_, bf16[129,256,512]{2,1,0:T(8,128)(2,1)} %get-tuple-element.48.jac.refs_2_, bf16[8,64,1024]{2,1,0:T(8,128)(2,1)S(1)} %get-tuple-element.57.refs_3_), custom_call_target="tpu_custom_call" | custom-call | flops 16 | bytes 64 | tf_op jit(solution)/shard_map/backward/pallas_call | solution.py:231
  113.1 2.1 %collective-permute-done.16 = bf16[64,4096]{1,0:T(8,128)(2,1)S(1)} collective-permute-done((bf16[64,4096]{1,0:T(8,128)(2,1)S(1)}, bf16[64,4096]{1,0:T(8,128)(2,1)S(1)}, u32[]{:S(2)}, u32[]{:S(2)}) %collective-permute-start.16) | collective-permute-done | bytes 524320 | tf_op jit(solution)/shard_map/ppermute | solution.py:288
  115.2 0.1 convert_add_fusion.refs_0_
  115.4 0.1 reduce-precision_convert_fusion.refs_1_
  115.5 0.1 collective-permute-start.17
  115.6 1.8 %collective-permute-start.18 = (bf16[64,4096]{1,0:T(8,128)(2,1)S(1)}, bf16[64,4096]{1,0:T(8,128)(2,1)S(1)}, u32[]{:S(2)}, u32[]{:S(2)}) collective-permute-start(bf16[64,4096]{1,0:T(8,128)(2,1)S(1)} %reduce-precision_convert_fusion.refs_1_), channel_id=1, source_target_pairs={{0,2},{1,3},{2,0},{3,1},{4,6},{5,7},{6,4},{7,5},{8,10},{9,11},{10,... | collective-permute-start | bytes 1572872 | tf_op jit(solution)/shard_map/ppermute | solution.py:288
  117.4 0.2 collective-permute-start.19
  117.6 12.4 %collective-permute-done.18.refs_2_ = bf16[64,4096]{1,0:T(8,128)(2,1)S(1)} collective-permute-done((bf16[64,4096]{1,0:T(8,128)(2,1)S(1)}, bf16[64,4096]{1,0:T(8,128)(2,1)S(1)}, u32[]{:S(2)}, u32[]{:S(2)}) %collective-permute-start.18) | collective-permute-done | bytes 524320 | tf_op jit(solution)/shard_map/ppermute | solution.py:288
  130.0 1.4 %place.2.refs_0_ = f32[64,16384]{1,0:T(8,128)} custom-call(s32[1]{0:T(128)} %bitcast.where, f32[64,4096]{1,0:T(8,128)S(1)} %convert_add_fusion.refs_0_, f32[64,4096]{1,0:T(8,128)S(1)} %collective-permute-done.17.refs_1_), custom_call_target="tpu_custom_call" | custom-call | tf_op jit(solution)/shard_map/place/pallas_call | solution.py:272
  131.4 0.5 collective-permute-done.20.refs_4_
  131.9 1.4 %place.3 = f32[64,16384]{1,0:T(8,128)} custom-call(s32[1]{0:T(128)} %bitcast.where, f32[64,16384]{1,0:T(8,128)} %place.2.refs_0_, bf16[64,4096]{1,0:T(8,128)(2,1)S(1)} %reduce-precision_convert_fusion.refs_1_, bf16[64,4096]{1,0:T(8,128)(2,1)S(1)} %collective-permute-done.18.refs_2_, ...), custom_call_target="tpu_custom_call", output_to_operand_aliasing={{}: (1, {})} | custom-call | tf_op jit(solution)/shard_map/place/pallas_call | solution.py:272
  (26 shorter events, 0.2 us)
Async XLA Ops:
  4.7 14.6 %all-to-all-start = ((bf16[8,8,1024]{2,1,0:T(8,128)(2,1)}), bf16[8,8,1024]{2,1,0:T(8,128)(2,1)S(1)}, u32[]{:S(2)}, u32[]{:S(2)}) async-start(bf16[8,8,1024]{2,1,0:T(8,128)(2,1)} %fusion.2), calls=%async_computation | async-start | bytes 262144 | tf_op jit(solution)/shard_map/all_to_all | solution.py:342
  19.4 1.6 %copy-start = (bf16[64,16384]{1,0:T(8,128)(2,1)S(1)}, bf16[64,16384]{1,0:T(8,128)(2,1)}, u32[]{:S(2)}) copy-start(bf16[64,16384]{1,0:T(8,128)(2,1)} %vectors.7) | copy-start | bytes 6291460
  30.2 10.9 %collective-permute-start = (f32[64,1024]{1,0:T(8,128)S(1)}, f32[64,1024]{1,0:T(8,128)S(1)}, u32[]{:S(2)}, u32[]{:S(2)}) collective-permute-start(f32[64,1024]{1,0:T(8,128)S(1)} %get-tuple-element.35), channel_id=1, source_target_pairs={{0,4},{4,0},{8,12},{12,8},{16,20},{20,16},{24,28},{28,24},{1,5},{5... | collective-permute-start | bytes 786440 | tf_op jit(solution)/shard_map/ppermute | solution.py:288
  30.4 1.6 %copy-start.1 = (bf16[64,16384]{1,0:T(8,128)(2,1)S(1)}, bf16[64,16384]{1,0:T(8,128)(2,1)}, u32[]{:S(2)}) copy-start(bf16[64,16384]{1,0:T(8,128)(2,1)} %vectors.7) | copy-start | bytes 6291460
  38.4 7.9 %collective-permute-start.1 = (f32[64,1024]{1,0:T(8,128)S(1)}, f32[64,1024]{1,0:T(8,128)S(1)}, u32[]{:S(2)}, u32[]{:S(2)}) collective-permute-start(f32[64,1024]{1,0:T(8,128)S(1)} %get-tuple-element.39), channel_id=1, source_target_pairs={{0,4},{4,0},{8,12},{12,8},{16,20},{20,16},{24,28},{28,24},{1,5},{5... | collective-permute-start | bytes 786440 | tf_op jit(solution)/shard_map/ppermute | solution.py:288
  41.2 9.0 %collective-permute-start.2 = (f32[64,1024]{1,0:T(8,128)S(1)}, f32[64,1024]{1,0:T(8,128)S(1)}, u32[]{:S(2)}, u32[]{:S(2)}) collective-permute-start(f32[64,1024]{1,0:T(8,128)S(1)} %add.124), channel_id=1, source_target_pairs={{0,24},{4,28},{8,0},{12,4},{16,8},{20,12},{24,16},{28,20},{1,25},{... | collective-permute-start | bytes 786440 | tf_op jit(solution)/shard_map/ppermute | solution.py:293
  45.1 12.9 %collective-permute-start.3 = (f32[64,1024]{1,0:T(8,128)S(1)}, f32[64,1024]{1,0:T(8,128)S(1)}, u32[]{:S(2)}, u32[]{:S(2)}) collective-permute-start(f32[64,1024]{1,0:T(8,128)S(1)} %get-tuple-element.44), channel_id=1, source_target_pairs={{0,4},{4,0},{8,12},{12,8},{16,20},{20,16},{24,28},{28,24},{1,5},{5... | collective-permute-start | bytes 786440 | tf_op jit(solution)/shard_map/ppermute | solution.py:288
  50.2 12.8 %collective-permute-start.5 = (f32[64,1024]{1,0:T(8,128)S(1)}, f32[64,1024]{1,0:T(8,128)S(1)}, u32[]{:S(2)}, u32[]{:S(2)}) collective-permute-start(f32[64,1024]{1,0:T(8,128)S(1)} %add.126), channel_id=1, source_target_pairs={{0,16},{4,20},{8,24},{12,28},{16,0},{20,4},{24,8},{28,12},{1,17},{... | collective-permute-start | bytes 786440 | tf_op jit(solution)/shard_map/ppermute | solution.py:293
  56.0 7.0 %collective-permute-start.4 = (f32[64,1024]{1,0:T(8,128)S(1)}, f32[64,1024]{1,0:T(8,128)S(1)}, u32[]{:S(2)}, u32[]{:S(2)}) collective-permute-start(f32[64,1024]{1,0:T(8,128)S(1)} %get-tuple-element.50), channel_id=1, source_target_pairs={{0,4},{4,0},{8,12},{12,8},{16,20},{20,16},{24,28},{28,24},{1,5},{5... | collective-permute-start | bytes 786440 | tf_op jit(solution)/shard_map/ppermute | solution.py:288
  58.0 11.0 %collective-permute-start.6 = (f32[64,1024]{1,0:T(8,128)S(1)}, f32[64,1024]{1,0:T(8,128)S(1)}, u32[]{:S(2)}, u32[]{:S(2)}) collective-permute-start(f32[64,1024]{1,0:T(8,128)S(1)} %add.128), channel_id=1, source_target_pairs={{0,8},{4,12},{8,16},{12,20},{16,24},{20,28},{24,0},{28,4},{1,9},{5... | collective-permute-start | bytes 786440 | tf_op jit(solution)/shard_map/ppermute | solution.py:293
  69.1 6.7 %collective-permute-start.9 = (bf16[64,1024]{1,0:T(8,128)(2,1)S(1)}, bf16[64,1024]{1,0:T(8,128)(2,1)S(1)}, u32[]{:S(2)}, u32[]{:S(2)}) collective-permute-start(bf16[64,1024]{1,0:T(8,128)(2,1)S(1)} %add_convert_fusion.refs_0_), channel_id=1, source_target_pairs={{0,24},{4,28},{8,0},{12,4},{16,8},{20,12},{24,16},{28,20},{1,25},{... | collective-permute-start | bytes 393224 | tf_op jit(solution)/shard_map/ppermute | solution.py:293
  73.2 7.3 %collective-permute-start.8 = (bf16[64,1024]{1,0:T(8,128)(2,1)S(1)}, bf16[64,1024]{1,0:T(8,128)(2,1)S(1)}, u32[]{:S(2)}, u32[]{:S(2)}) collective-permute-start(bf16[64,1024]{1,0:T(8,128)(2,1)S(1)} %add_convert_fusion.refs_0_), channel_id=1, source_target_pairs={{0,16},{4,20},{8,24},{12,28},{16,0},{20,4},{24,8},{28,12},{1,17},{... | collective-permute-start | bytes 393224 | tf_op jit(solution)/shard_map/ppermute | solution.py:293
  73.2 9.3 %collective-permute-start.7 = (bf16[64,1024]{1,0:T(8,128)(2,1)S(1)}, bf16[64,1024]{1,0:T(8,128)(2,1)S(1)}, u32[]{:S(2)}, u32[]{:S(2)}) collective-permute-start(bf16[64,1024]{1,0:T(8,128)(2,1)S(1)} %add_convert_fusion.refs_0_), channel_id=1, source_target_pairs={{0,8},{4,12},{8,16},{12,20},{16,24},{20,28},{24,0},{28,4},{1,9},{5... | collective-permute-start | bytes 393224 | tf_op jit(solution)/shard_map/ppermute | solution.py:293
  73.9 8.7 %collective-permute-start.10 = (bf16[64,1024]{1,0:T(8,128)(2,1)S(1)}, bf16[64,1024]{1,0:T(8,128)(2,1)S(1)}, u32[]{:S(2)}, u32[]{:S(2)}) collective-permute-start(bf16[64,1024]{1,0:T(8,128)(2,1)S(1)} %add_convert_fusion.refs_0_), channel_id=1, source_target_pairs={{0,4},{4,0},{8,12},{12,8},{16,20},{20,16},{24,28},{28,24},{1,5},{5... | collective-permute-start | bytes 393224 | tf_op jit(solution)/shard_map/ppermute | solution.py:288
  75.9 6.7 %collective-permute-start.13 = (bf16[64,1024]{1,0:T(8,128)(2,1)S(1)}, bf16[64,1024]{1,0:T(8,128)(2,1)S(1)}, u32[]{:S(2)}, u32[]{:S(2)}) collective-permute-start(bf16[64,1024]{1,0:T(8,128)(2,1)S(1)} %collective-permute-done.9.refs_3_), channel_id=1, source_target_pairs={{0,4},{4,0},{8,12},{12,8},{16,20},{20,16},{24,28},{28,24},{1,5},{5... | collective-permute-start | bytes 393224 | tf_op jit(solution)/shard_map/ppermute | solution.py:288
  80.4 5.0 %collective-permute-start.12 = (bf16[64,1024]{1,0:T(8,128)(2,1)S(1)}, bf16[64,1024]{1,0:T(8,128)(2,1)S(1)}, u32[]{:S(2)}, u32[]{:S(2)}) collective-permute-start(bf16[64,1024]{1,0:T(8,128)(2,1)S(1)} %collective-permute-done.8.refs_2_), channel_id=1, source_target_pairs={{0,4},{4,0},{8,12},{12,8},{16,20},{20,16},{24,28},{28,24},{1,5},{5... | collective-permute-start | bytes 393224 | tf_op jit(solution)/shard_map/ppermute | solution.py:288
  82.4 5.0 %collective-permute-start.11 = (bf16[64,1024]{1,0:T(8,128)(2,1)S(1)}, bf16[64,1024]{1,0:T(8,128)(2,1)S(1)}, u32[]{:S(2)}, u32[]{:S(2)}) collective-permute-start(bf16[64,1024]{1,0:T(8,128)(2,1)S(1)} %collective-permute-done.7.refs_1_), channel_id=1, source_target_pairs={{0,4},{4,0},{8,12},{12,8},{16,20},{20,16},{24,28},{28,24},{1,5},{5... | collective-permute-start | bytes 393224 | tf_op jit(solution)/shard_map/ppermute | solution.py:288
  91.4 4.3 %collective-permute-start.14 = (f32[64,4096]{1,0:T(8,128)S(1)}, f32[64,4096]{1,0:T(8,128)S(1)}, u32[]{:S(2)}, u32[]{:S(2)}) collective-permute-start(f32[64,4096]{1,0:T(8,128)S(1)} %get-tuple-element.58), channel_id=1, source_target_pairs={{0,1},{1,0},{2,3},{3,2},{4,5},{5,4},{6,7},{7,6},{8,9},{9,8},{10,11... | collective-permute-start | bytes 3145736 | tf_op jit(solution)/shard_map/ppermute | solution.py:288
  95.8 19.4 %collective-permute-start.16 = (bf16[64,4096]{1,0:T(8,128)(2,1)S(1)}, bf16[64,4096]{1,0:T(8,128)(2,1)S(1)}, u32[]{:S(2)}, u32[]{:S(2)}) collective-permute-start(bf16[64,4096]{1,0:T(8,128)(2,1)S(1)} %fusion), channel_id=1, source_target_pairs={{0,2},{1,3},{2,0},{3,1},{4,6},{5,7},{6,4},{7,5},{8,10},{9,11},{10,... | collective-permute-start | bytes 1572872 | tf_op jit(solution)/shard_map/ppermute | solution.py:288
  108.9 6.5 %collective-permute-start.15 = (f32[64,4096]{1,0:T(8,128)S(1)}, f32[64,4096]{1,0:T(8,128)S(1)}, u32[]{:S(2)}, u32[]{:S(2)}) collective-permute-start(f32[64,4096]{1,0:T(8,128)S(1)} %backward.7), channel_id=1, source_target_pairs={{0,1},{1,0},{2,3},{3,2},{4,5},{5,4},{6,7},{7,6},{8,9},{9,8},{10,11... | collective-permute-start | bytes 3145736 | tf_op jit(solution)/shard_map/ppermute | solution.py:288
  115.5 14.4 %collective-permute-start.17 = (f32[64,4096]{1,0:T(8,128)S(1)}, f32[64,4096]{1,0:T(8,128)S(1)}, u32[]{:S(2)}, u32[]{:S(2)}) collective-permute-start(f32[64,4096]{1,0:T(8,128)S(1)} %convert_add_fusion.refs_0_), channel_id=1, source_target_pairs={{0,1},{1,0},{2,3},{3,2},{4,5},{5,4},{6,7},{7,6},{8,9},{9,8},{10,11... | collective-permute-start | bytes 3145736 | tf_op jit(solution)/shard_map/ppermute | solution.py:288
  115.6 14.3 %collective-permute-start.18 = (bf16[64,4096]{1,0:T(8,128)(2,1)S(1)}, bf16[64,4096]{1,0:T(8,128)(2,1)S(1)}, u32[]{:S(2)}, u32[]{:S(2)}) collective-permute-start(bf16[64,4096]{1,0:T(8,128)(2,1)S(1)} %reduce-precision_convert_fusion.refs_1_), channel_id=1, source_target_pairs={{0,2},{1,3},{2,0},{3,1},{4,6},{5,7},{6,4},{7,5},{8,10},{9,11},{10,... | collective-permute-start | bytes 1572872 | tf_op jit(solution)/shard_map/ppermute | solution.py:288
  117.4 14.0 %collective-permute-start.19 = (bf16[64,4096]{1,0:T(8,128)(2,1)S(1)}, bf16[64,4096]{1,0:T(8,128)(2,1)S(1)}, u32[]{:S(2)}, u32[]{:S(2)}) collective-permute-start(bf16[64,4096]{1,0:T(8,128)(2,1)S(1)} %reduce-precision_convert_fusion.refs_1_), channel_id=1, source_target_pairs={{0,1},{1,0},{2,3},{3,2},{4,5},{5,4},{6,7},{7,6},{8,9},{9,8},{10,11... | collective-permute-start | bytes 1572872 | tf_op jit(solution)/shard_map/ppermute | solution.py:288
  130.0 1.9 %collective-permute-start.20 = (bf16[64,4096]{1,0:T(8,128)(2,1)S(1)}, bf16[64,4096]{1,0:T(8,128)(2,1)S(1)}, u32[]{:S(2)}, u32[]{:S(2)}) collective-permute-start(bf16[64,4096]{1,0:T(8,128)(2,1)S(1)} %collective-permute-done.18.refs_2_), channel_id=1, source_target_pairs={{0,1},{1,0},{2,3},{3,2},{4,5},{5,4},{6,7},{7,6},{8,9},{9,8},{10,11... | collective-permute-start | bytes 1572872 | tf_op jit(solution)/shard_map/ppermute | solution.py:288

commit v7 on v6

--- a/solution.py
+++ b/solution.py
@@ -368,6 +368,8 @@
         if k > 0:
             before, got = waiting[k - 1]
             pair = before + got
+            if k == ring - 1:
+                pair = pair.astype(bf16)
             older = arrived[: ring - 3]
             codes, pair, older = lax.optimization_barrier((codes, pair, older))
             arrived = older + arrived[ring - 3 :]
@@ -377,7 +379,7 @@
     arrived = early + arrived[-1:]
     outputs = near + got
     for pair in arrived:
-        outputs = outputs + pair
+        outputs = outputs + pair.astype(f32)
     outputs = outputs.astype(bf16)
 
     same = [outputs] + [shift(outputs, "rows", k) for k in range(1, ring)]

time: 133 us -> 128 us (0.962)
  starting transfers between devices: 34 us -> 28.5 us
    ppermute x15, starting transfers between devices: 21.8 us -> 14.4 us  [swap(): lax.ppermute(array, axis, [(i, i ^ bit) for i in range(lax.axis_size(axis...]
    ppermute x15, waiting for transfers between devices: 20.2 us -> 25.2 us  [swap(): lax.ppermute(array, axis, [(i, i ^ bit) for i in range(lax.axis_size(axis...]
    ppermute x6, waiting for transfers between devices: 17.4 us -> 12.8 us  [shift(): lax.ppermute(array, axis, [(i, (i + 2 * steps) % size) for i in range(siz...]
    ppermute x6, starting transfers between devices: 4.95 us -> 6.81 us  [shift(): lax.ppermute(array, axis, [(i, (i + 2 * steps) % size) for i in range(siz...]
  transfers between devices with their start and end apart: 22 -> 22, of which waited for: 11 -> 12; matrix products, arithmetic and copies ran while one was open for 2% -> 2% of each run, Pallas kernels for 23% -> 24%
where the time goes in v7:
time: 128 us; the launch traced here: 127 us
  Pallas kernels  44.2 us (35%)
  waiting for transfers between devices  43.4 us (34%)
  starting transfers between devices  28.5 us (22%)
  other arithmetic  5.76 us (4%)
  local copies, waits for them, and re-layouts  4.24 us (3%)
    ppermute x15, waiting for transfers between devices, swap(): lax.ppermute(array, axis, [(i, i ^ bit) for i in range(lax.axis_size(axis...  25.2 us
    pallas_call x4, Pallas kernels, forward(): pl.pallas_call(functools.partial(forward_kernel, blocks, capacity), out_s...  24.5 us
    pallas_call x4, Pallas kernels, backward(): pl.pallas_call(functools.partial(kernel, capacity, total // 2), out_shape...  16.9 us
    ppermute x15, starting transfers between devices, swap(): lax.ppermute(array, axis, [(i, i ^ bit) for i in range(lax.axis_size(axis...  14.4 us
    ppermute x6, waiting for transfers between devices, shift(): lax.ppermute(array, axis, [(i, (i + 2 * steps) % size) for i in range(siz...  12.8 us
    all_to_all x1, starting transfers between devices, body(): left = lax.all_to_all(send, 'rows', split_axis=0, concat_axis=0, tiled=True)  7.25 us
    ppermute x6, starting transfers between devices, shift(): lax.ppermute(array, axis, [(i, (i + 2 * steps) % size) for i in range(siz...  6.81 us
    all_to_all x1, waiting for transfers between devices, body(): left = lax.all_to_all(send, 'rows', split_axis=0, concat_axis=0, tiled=True)  5.44 us
  transfers between devices with their start and end apart: 22, of which 12 were waited for; matrix products, arithmetic and copies ran while one was open for 2% of the time, Pallas kernels for 24%

profile of v7, /device:TPU:0, one launch (start us, length us, event | category | flops | bytes accessed | tf_op | source)
XLA Modules:
  0.0 127.1 jit_solution(14217359355298618985)
XLA Ops:
  0.7 0.9 select_reduce_fusion
  1.5 0.7 compare_select_fusion.4
  2.2 0.2 convert_reduce_fusion
  2.4 0.1 select_reduce_fusion.1
  2.5 0.1 convert_element_type.70
  2.6 0.7 stack.118
  3.3 0.7 fusion.8
  4.0 0.1 stack.99
  4.0 0.7 fusion.2
  4.7 7.3 %all-to-all-start = ((bf16[8,8,1024]{2,1,0:T(8,128)(2,1)}), bf16[8,8,1024]{2,1,0:T(8,128)(2,1)S(1)}, u32[]{:S(2)}, u32[]{:S(2)}) async-start(bf16[8,8,1024]{2,1,0:T(8,128)(2,1)} %fusion.2), calls=%async_computation | async-start | bytes 262144 | tf_op jit(solution)/shard_map/all_to_all | solution.py:342
  12.0 0.8 broadcast_in_dim.90
  12.8 0.8 multiply_convert_fusion
  13.6 0.1 broadcast_select_fusion
  13.8 0.1 pad_add_fusion
  13.9 5.4 %all-to-all-done.left = bf16[8,8,1024]{2,1,0:T(8,128)(2,1)S(1)} async-done(((bf16[8,8,1024]{2,1,0:T(8,128)(2,1)}), bf16[8,8,1024]{2,1,0:T(8,128)(2,1)S(1)}, u32[]{:S(2)}, u32[]{:S(2)}) %all-to-all-start) | async-done | bytes 131104 | tf_op jit(solution)/shard_map/all_to_all | solution.py:342
  19.4 0.1 reshape.102.codes.refs_0_
  19.4 1.6 %copy-done = bf16[64,16384]{1,0:T(8,128)(2,1)S(1)} copy-done((bf16[64,16384]{1,0:T(8,128)(2,1)S(1)}, bf16[64,16384]{1,0:T(8,128)(2,1)}, u32[]{:S(2)}) %copy-start) | copy-done | bytes 2097176
  21.0 7.8 %forward.4 = (f32[64,1024]{1,0:T(8,128)S(1)}, f32[64,1024]{1,0:T(8,128)S(1)}, bf16[129,256,512]{2,1,0:T(8,128)(2,1)}) custom-call(s32[128]{0:T(128)S(1)} %reshape.102.codes.refs_0_, s32[2]{0:T(128)S(1)} %get-tuple-element.76.where, bf16[8,8,1024]{2,1,0:T(8,128)(2,1)S(1)} %all-to-all-done.left, bf16[32,8,1024]{2,1,0:T(8,128)(2,1)S(1)} %pad_maximum_fusion.right, ...), custom_call_target="tpu_custom_call" | custom-call | flops 32 | bytes 64 | tf_op jit(solution)/shard_map/forward/pallas_call | solution.py:152
  28.9 0.1 collective-permute-start
  29.0 1.6 %copy-done.1 = bf16[64,16384]{1,0:T(8,128)(2,1)S(1)} copy-done((bf16[64,16384]{1,0:T(8,128)(2,1)S(1)}, bf16[64,16384]{1,0:T(8,128)(2,1)}, u32[]{:S(2)}) %copy-start.1) | copy-done | bytes 2097176
  30.6 3.7 %forward.5 = (f32[64,1024]{1,0:T(8,128)S(1)}, f32[64,1024]{1,0:T(8,128)S(1)}, bf16[129,256,512]{2,1,0:T(8,128)(2,1)}) custom-call(s32[128]{0:T(128)S(1)} %reshape.102.codes.refs_0_, s32[2]{0:T(128)S(1)} %get-tuple-element.77.where, bf16[8,8,1024]{2,1,0:T(8,128)(2,1)S(1)} %all-to-all-done.left, ...), custom_call_target="tpu_custom_call", output_to_operand_aliasing={{2}: (5, {})} | custom-call | flops 32 | bytes 64 | tf_op jit(solution)/shard_map/forward/pallas_call | solution.py:152
  34.3 2.0 %collective-permute-start.1 = (f32[64,1024]{1,0:T(8,128)S(1)}, f32[64,1024]{1,0:T(8,128)S(1)}, u32[]{:S(2)}, u32[]{:S(2)}) collective-permute-start(f32[64,1024]{1,0:T(8,128)S(1)} %get-tuple-element.39), channel_id=1, source_target_pairs={{0,4},{4,0},{8,12},{12,8},{16,20},{20,16},{24,28},{28,24},{1,5},{5... | collective-permute-start | bytes 786440 | tf_op jit(solution)/shard_map/ppermute | solution.py:288
  36.4 1.3 %collective-permute-start.2 = (f32[64,1024]{1,0:T(8,128)S(1)}, f32[64,1024]{1,0:T(8,128)S(1)}, u32[]{:S(2)}, u32[]{:S(2)}) collective-permute-start(f32[64,1024]{1,0:T(8,128)S(1)} %add.124), channel_id=1, source_target_pairs={{0,24},{4,28},{8,0},{12,4},{16,8},{20,12},{24,16},{28,20},{1,25},{... | collective-permute-start | bytes 786440 | tf_op jit(solution)/shard_map/ppermute | solution.py:293
  37.7 0.1 pad_add_fusion.2
  37.7 5.1 %forward.6 = (f32[64,1024]{1,0:T(8,128)S(1)}, f32[64,1024]{1,0:T(8,128)S(1)}, bf16[129,256,512]{2,1,0:T(8,128)(2,1)}) custom-call(s32[128]{0:T(128)S(1)} %reshape.102.codes.refs_0_, s32[2]{0:T(128)S(1)} %get-tuple-element.78.where, bf16[8,8,1024]{2,1,0:T(8,128)(2,1)S(1)} %all-to-all-done.left, ...), custom_call_target="tpu_custom_call", output_to_operand_aliasing={{2}: (5, {})} | custom-call | flops 32 | bytes 64 | tf_op jit(solution)/shard_map/forward/pallas_call | solution.py:152
  42.9 2.1 %collective-permute-start.3 = (f32[64,1024]{1,0:T(8,128)S(1)}, f32[64,1024]{1,0:T(8,128)S(1)}, u32[]{:S(2)}, u32[]{:S(2)}) collective-permute-start(f32[64,1024]{1,0:T(8,128)S(1)} %get-tuple-element.44), channel_id=1, source_target_pairs={{0,4},{4,0},{8,12},{12,8},{16,20},{20,16},{24,28},{28,24},{1,5},{5... | collective-permute-start | bytes 786440 | tf_op jit(solution)/shard_map/ppermute | solution.py:288
  45.0 1.4 %collective-permute-done.2 = f32[64,1024]{1,0:T(8,128)S(1)} collective-permute-done((f32[64,1024]{1,0:T(8,128)S(1)}, f32[64,1024]{1,0:T(8,128)S(1)}, u32[]{:S(2)}, u32[]{:S(2)}) %collective-permute-start.2) | collective-permute-done | bytes 262176 | tf_op jit(solution)/shard_map/ppermute | solution.py:293
  46.4 2.9 %collective-permute-start.5 = (f32[64,1024]{1,0:T(8,128)S(1)}, f32[64,1024]{1,0:T(8,128)S(1)}, u32[]{:S(2)}, u32[]{:S(2)}) collective-permute-start(f32[64,1024]{1,0:T(8,128)S(1)} %add.126), channel_id=1, source_target_pairs={{0,16},{4,20},{8,24},{12,28},{16,0},{20,4},{24,8},{28,12},{1,17},{... | collective-permute-start | bytes 786440 | tf_op jit(solution)/shard_map/ppermute | solution.py:293
  49.3 7.8 %forward.7 = (f32[64,1024]{1,0:T(8,128)S(1)}, f32[64,1024]{1,0:T(8,128)S(1)}, bf16[129,256,512]{2,1,0:T(8,128)(2,1)}) custom-call(s32[128]{0:T(128)S(1)} %reshape.102.codes.refs_0_, s32[2]{0:T(128)S(1)} %get-tuple-element.79.where, bf16[8,8,1024]{2,1,0:T(8,128)(2,1)S(1)} %all-to-all-done.left, ...), custom_call_target="tpu_custom_call", output_to_operand_aliasing={{2}: (5, {})} | custom-call | flops 32 | bytes 64 | tf_op jit(solution)/shard_map/forward/pallas_call | solution.py:152
  57.2 0.7 collective-permute-start.4
  57.9 2.5 %collective-permute-done.5 = f32[64,1024]{1,0:T(8,128)S(1)} collective-permute-done((f32[64,1024]{1,0:T(8,128)S(1)}, f32[64,1024]{1,0:T(8,128)S(1)}, u32[]{:S(2)}, u32[]{:S(2)}) %collective-permute-start.5) | collective-permute-done | bytes 262176 | tf_op jit(solution)/shard_map/ppermute | solution.py:293
  60.5 3.1 %collective-permute-done.4 = f32[64,1024]{1,0:T(8,128)S(1)} collective-permute-done((f32[64,1024]{1,0:T(8,128)S(1)}, f32[64,1024]{1,0:T(8,128)S(1)}, u32[]{:S(2)}, u32[]{:S(2)}) %collective-permute-start.4) | collective-permute-done | bytes 262176 | tf_op jit(solution)/shard_map/ppermute | solution.py:288
  63.6 1.1 collective-permute-done.6
  64.7 0.1 add_convert_fusion.refs_0_
  64.8 1.1 collective-permute-start.9
  65.9 1.3 %collective-permute-start.8 = (bf16[64,1024]{1,0:T(8,128)(2,1)S(1)}, bf16[64,1024]{1,0:T(8,128)(2,1)S(1)}, u32[]{:S(2)}, u32[]{:S(2)}) collective-permute-start(bf16[64,1024]{1,0:T(8,128)(2,1)S(1)} %add_convert_fusion.refs_0_), channel_id=1, source_target_pairs={{0,16},{4,20},{8,24},{12,28},{16,0},{20,4},{24,8},{28,12},{1,17},{... | collective-permute-start | bytes 393224 | tf_op jit(solution)/shard_map/ppermute | solution.py:293
  67.3 0.1 collective-permute-start.7
  67.4 0.1 pad_add_fusion.8
  67.4 1.7 %collective-permute-start.10 = (bf16[64,1024]{1,0:T(8,128)(2,1)S(1)}, bf16[64,1024]{1,0:T(8,128)(2,1)S(1)}, u32[]{:S(2)}, u32[]{:S(2)}) collective-permute-start(bf16[64,1024]{1,0:T(8,128)(2,1)S(1)} %add_convert_fusion.refs_0_), channel_id=1, source_target_pairs={{0,4},{4,0},{8,12},{12,8},{16,20},{20,16},{24,28},{28,24},{1,5},{5... | collective-permute-start | bytes 393224 | tf_op jit(solution)/shard_map/ppermute | solution.py:288
  69.1 0.9 collective-permute-done.9.refs_3_
  70.0 1.7 %collective-permute-start.13 = (bf16[64,1024]{1,0:T(8,128)(2,1)S(1)}, bf16[64,1024]{1,0:T(8,128)(2,1)S(1)}, u32[]{:S(2)}, u32[]{:S(2)}) collective-permute-start(bf16[64,1024]{1,0:T(8,128)(2,1)S(1)} %collective-permute-done.9.refs_3_), channel_id=1, source_target_pairs={{0,4},{4,0},{8,12},{12,8},{16,20},{20,16},{24,28},{28,24},{1,5},{5... | collective-permute-start | bytes 393224 | tf_op jit(solution)/shard_map/ppermute | solution.py:288
  71.7 6.9 %collective-permute-done.8.refs_2_ = bf16[64,1024]{1,0:T(8,128)(2,1)S(1)} collective-permute-done((bf16[64,1024]{1,0:T(8,128)(2,1)S(1)}, bf16[64,1024]{1,0:T(8,128)(2,1)S(1)}, u32[]{:S(2)}, u32[]{:S(2)}) %collective-permute-start.8) | collective-permute-done | bytes 131104 | tf_op jit(solution)/shard_map/ppermute | solution.py:293
  78.6 0.8 collective-permute-start.12
  79.5 1.2 collective-permute-start.11
  80.7 0.1 pad_add_fusion.7
  80.7 3.8 %collective-permute-done.12.refs_6_ = bf16[64,1024]{1,0:T(8,128)(2,1)S(1)} collective-permute-done((bf16[64,1024]{1,0:T(8,128)(2,1)S(1)}, bf16[64,1024]{1,0:T(8,128)(2,1)S(1)}, u32[]{:S(2)}, u32[]{:S(2)}) %collective-permute-start.12) | collective-permute-done | bytes 131104 | tf_op jit(solution)/shard_map/ppermute | solution.py:288
  84.5 1.4 %collective-permute-done.11.refs_5_ = bf16[64,1024]{1,0:T(8,128)(2,1)S(1)} collective-permute-done((bf16[64,1024]{1,0:T(8,128)(2,1)S(1)}, bf16[64,1024]{1,0:T(8,128)(2,1)S(1)}, u32[]{:S(2)}, u32[]{:S(2)}) %collective-permute-start.11) | collective-permute-done | bytes 131104 | tf_op jit(solution)/shard_map/ppermute | solution.py:288
  85.9 4.7 %backward.4 = (f32[64,4096]{1,0:T(8,128)S(1)}, bf16[8,64,1024]{2,1,0:T(8,128)(2,1)S(1)}) custom-call(s32[128]{0:T(128)S(1)} %reshape.102.codes.refs_0_, s32[3]{0:T(128)S(1)} %get-tuple-element.72.where, bf16[129,256,512]{2,1,0:T(8,128)(2,1)} %get-tuple-element.48.jac.refs_2_, bf16[64,1024]{1,0:T(8,128)(2,1)S(1)} %add_convert_fusion.refs_0_, ...), custom_call_target="tpu_custom_call" | custom-call | flops 16 | bytes 64 | tf_op jit(solution)/shard_map/backward/pallas_call | solution.py:231
  90.7 0.1 collective-permute-start.14
  90.8 3.6 %backward.5 = f32[64,4096]{1,0:T(8,128)S(1)} custom-call(s32[128]{0:T(128)S(1)} %reshape.102.codes.refs_0_, s32[3]{0:T(128)S(1)} %get-tuple-element.73.refs_1_, bf16[129,256,512]{2,1,0:T(8,128)(2,1)} %get-tuple-element.48.jac.refs_2_, bf16[8,64,1024]{2,1,0:T(8,128)(2,1)S(1)} %get-tuple-element.57.refs_3_), custom_call_target="tpu_custom_call" | custom-call | flops 16 | bytes 64 | tf_op jit(solution)/shard_map/backward/pallas_call | solution.py:231
  94.4 0.1 fusion
  94.5 0.1 collective-permute-start.16
  94.6 4.5 %backward.7 = f32[64,4096]{1,0:T(8,128)S(1)} custom-call(s32[128]{0:T(128)S(1)} %reshape.102.codes.refs_0_, s32[3]{0:T(128)S(1)} %get-tuple-element.63.refs_1_, bf16[129,256,512]{2,1,0:T(8,128)(2,1)} %get-tuple-element.48.jac.refs_2_, bf16[8,64,1024]{2,1,0:T(8,128)(2,1)S(1)} %get-tuple-element.57.refs_3_), custom_call_target="tpu_custom_call" | custom-call | flops 16 | bytes 64 | tf_op jit(solution)/shard_map/backward/pallas_call | solution.py:231
  99.1 3.3 %collective-permute-start.15 = (f32[64,4096]{1,0:T(8,128)S(1)}, f32[64,4096]{1,0:T(8,128)S(1)}, u32[]{:S(2)}, u32[]{:S(2)}) collective-permute-start(f32[64,4096]{1,0:T(8,128)S(1)} %backward.7), channel_id=1, source_target_pairs={{0,1},{1,0},{2,3},{3,2},{4,5},{5,4},{6,7},{7,6},{8,9},{9,8},{10,11... | collective-permute-start | bytes 3145736 | tf_op jit(solution)/shard_map/ppermute | solution.py:288
  102.5 4.0 %backward.6 = f32[64,4096]{1,0:T(8,128)S(1)} custom-call(s32[128]{0:T(128)S(1)} %reshape.102.codes.refs_0_, s32[3]{0:T(128)S(1)} %get-tuple-element.71.refs_1_, bf16[129,256,512]{2,1,0:T(8,128)(2,1)} %get-tuple-element.48.jac.refs_2_, bf16[8,64,1024]{2,1,0:T(8,128)(2,1)S(1)} %get-tuple-element.57.refs_3_), custom_call_target="tpu_custom_call" | custom-call | flops 16 | bytes 64 | tf_op jit(solution)/shard_map/backward/pallas_call | solution.py:231
  106.5 2.5 %collective-permute-done.16 = bf16[64,4096]{1,0:T(8,128)(2,1)S(1)} collective-permute-done((bf16[64,4096]{1,0:T(8,128)(2,1)S(1)}, bf16[64,4096]{1,0:T(8,128)(2,1)S(1)}, u32[]{:S(2)}, u32[]{:S(2)}) %collective-permute-start.16) | collective-permute-done | bytes 524320 | tf_op jit(solution)/shard_map/ppermute | solution.py:288
  109.0 0.1 convert_add_fusion.refs_0_
  109.2 0.1 reduce-precision_convert_fusion.refs_1_
  109.3 0.3 collective-permute-start.17
  109.6 0.3 collective-permute-start.19
  109.9 13.8 %collective-permute-done.18.refs_2_ = bf16[64,4096]{1,0:T(8,128)(2,1)S(1)} collective-permute-done((bf16[64,4096]{1,0:T(8,128)(2,1)S(1)}, bf16[64,4096]{1,0:T(8,128)(2,1)S(1)}, u32[]{:S(2)}, u32[]{:S(2)}) %collective-permute-start.18) | collective-permute-done | bytes 524320 | tf_op jit(solution)/shard_map/ppermute | solution.py:288
  123.7 1.4 %place.2.refs_0_ = f32[64,16384]{1,0:T(8,128)} custom-call(s32[1]{0:T(128)} %bitcast.where, f32[64,4096]{1,0:T(8,128)S(1)} %convert_add_fusion.refs_0_, f32[64,4096]{1,0:T(8,128)S(1)} %collective-permute-done.17.refs_1_), custom_call_target="tpu_custom_call" | custom-call | tf_op jit(solution)/shard_map/place/pallas_call | solution.py:272
  125.1 0.5 collective-permute-done.20.refs_4_
  125.6 1.4 %place.3 = f32[64,16384]{1,0:T(8,128)} custom-call(s32[1]{0:T(128)} %bitcast.where, f32[64,16384]{1,0:T(8,128)} %place.2.refs_0_, bf16[64,4096]{1,0:T(8,128)(2,1)S(1)} %reduce-precision_convert_fusion.refs_1_, bf16[64,4096]{1,0:T(8,128)(2,1)S(1)} %collective-permute-done.18.refs_2_, ...), custom_call_target="tpu_custom_call", output_to_operand_aliasing={{}: (1, {})} | custom-call | tf_op jit(solution)/shard_map/place/pallas_call | solution.py:272
  (26 shorter events, 0.4 us)
Async XLA Ops:
  4.7 14.6 %all-to-all-start = ((bf16[8,8,1024]{2,1,0:T(8,128)(2,1)}), bf16[8,8,1024]{2,1,0:T(8,128)(2,1)S(1)}, u32[]{:S(2)}, u32[]{:S(2)}) async-start(bf16[8,8,1024]{2,1,0:T(8,128)(2,1)} %fusion.2), calls=%async_computation | async-start | bytes 262144 | tf_op jit(solution)/shard_map/all_to_all | solution.py:342
  19.4 1.6 %copy-start = (bf16[64,16384]{1,0:T(8,128)(2,1)S(1)}, bf16[64,16384]{1,0:T(8,128)(2,1)}, u32[]{:S(2)}) copy-start(bf16[64,16384]{1,0:T(8,128)(2,1)} %vectors.7) | copy-start | bytes 6291460
  28.9 7.5 %collective-permute-start = (f32[64,1024]{1,0:T(8,128)S(1)}, f32[64,1024]{1,0:T(8,128)S(1)}, u32[]{:S(2)}, u32[]{:S(2)}) collective-permute-start(f32[64,1024]{1,0:T(8,128)S(1)} %get-tuple-element.35), channel_id=1, source_target_pairs={{0,4},{4,0},{8,12},{12,8},{16,20},{20,16},{24,28},{28,24},{1,5},{5... | collective-permute-start | bytes 786440 | tf_op jit(solution)/shard_map/ppermute | solution.py:288
  29.0 1.6 %copy-start.1 = (bf16[64,16384]{1,0:T(8,128)(2,1)S(1)}, bf16[64,16384]{1,0:T(8,128)(2,1)}, u32[]{:S(2)}) copy-start(bf16[64,16384]{1,0:T(8,128)(2,1)} %vectors.7) | copy-start | bytes 6291460
  34.3 10.7 %collective-permute-start.1 = (f32[64,1024]{1,0:T(8,128)S(1)}, f32[64,1024]{1,0:T(8,128)S(1)}, u32[]{:S(2)}, u32[]{:S(2)}) collective-permute-start(f32[64,1024]{1,0:T(8,128)S(1)} %get-tuple-element.39), channel_id=1, source_target_pairs={{0,4},{4,0},{8,12},{12,8},{16,20},{20,16},{24,28},{28,24},{1,5},{5... | collective-permute-start | bytes 786440 | tf_op jit(solution)/shard_map/ppermute | solution.py:288
  36.4 10.1 %collective-permute-start.2 = (f32[64,1024]{1,0:T(8,128)S(1)}, f32[64,1024]{1,0:T(8,128)S(1)}, u32[]{:S(2)}, u32[]{:S(2)}) collective-permute-start(f32[64,1024]{1,0:T(8,128)S(1)} %add.124), channel_id=1, source_target_pairs={{0,24},{4,28},{8,0},{12,4},{16,8},{20,12},{24,16},{28,20},{1,25},{... | collective-permute-start | bytes 786440 | tf_op jit(solution)/shard_map/ppermute | solution.py:293
  42.9 15.0 %collective-permute-start.3 = (f32[64,1024]{1,0:T(8,128)S(1)}, f32[64,1024]{1,0:T(8,128)S(1)}, u32[]{:S(2)}, u32[]{:S(2)}) collective-permute-start(f32[64,1024]{1,0:T(8,128)S(1)} %get-tuple-element.44), channel_id=1, source_target_pairs={{0,4},{4,0},{8,12},{12,8},{16,20},{20,16},{24,28},{28,24},{1,5},{5... | collective-permute-start | bytes 786440 | tf_op jit(solution)/shard_map/ppermute | solution.py:288
  46.4 14.0 %collective-permute-start.5 = (f32[64,1024]{1,0:T(8,128)S(1)}, f32[64,1024]{1,0:T(8,128)S(1)}, u32[]{:S(2)}, u32[]{:S(2)}) collective-permute-start(f32[64,1024]{1,0:T(8,128)S(1)} %add.126), channel_id=1, source_target_pairs={{0,16},{4,20},{8,24},{12,28},{16,0},{20,4},{24,8},{28,12},{1,17},{... | collective-permute-start | bytes 786440 | tf_op jit(solution)/shard_map/ppermute | solution.py:293
  57.2 6.4 %collective-permute-start.4 = (f32[64,1024]{1,0:T(8,128)S(1)}, f32[64,1024]{1,0:T(8,128)S(1)}, u32[]{:S(2)}, u32[]{:S(2)}) collective-permute-start(f32[64,1024]{1,0:T(8,128)S(1)} %get-tuple-element.50), channel_id=1, source_target_pairs={{0,4},{4,0},{8,12},{12,8},{16,20},{20,16},{24,28},{28,24},{1,5},{5... | collective-permute-start | bytes 786440 | tf_op jit(solution)/shard_map/ppermute | solution.py:288
  57.9 6.8 %collective-permute-start.6 = (bf16[64,1024]{1,0:T(8,128)(2,1)S(1)}, bf16[64,1024]{1,0:T(8,128)(2,1)S(1)}, u32[]{:S(2)}, u32[]{:S(2)}) collective-permute-start(bf16[64,1024]{1,0:T(8,128)(2,1)S(1)} %add_convert_fusion.1), channel_id=1, source_target_pairs={{0,8},{4,12},{8,16},{12,20},{16,24},{20,28},{24,0},{28,4},{1,9},{5... | collective-permute-start | bytes 393224 | tf_op jit(solution)/shard_map/ppermute | solution.py:293
  64.8 5.3 %collective-permute-start.9 = (bf16[64,1024]{1,0:T(8,128)(2,1)S(1)}, bf16[64,1024]{1,0:T(8,128)(2,1)S(1)}, u32[]{:S(2)}, u32[]{:S(2)}) collective-permute-start(bf16[64,1024]{1,0:T(8,128)(2,1)S(1)} %add_convert_fusion.refs_0_), channel_id=1, source_target_pairs={{0,24},{4,28},{8,0},{12,4},{16,8},{20,12},{24,16},{28,20},{1,25},{... | collective-permute-start | bytes 393224 | tf_op jit(solution)/shard_map/ppermute | solution.py:293
  65.9 12.7 %collective-permute-start.8 = (bf16[64,1024]{1,0:T(8,128)(2,1)S(1)}, bf16[64,1024]{1,0:T(8,128)(2,1)S(1)}, u32[]{:S(2)}, u32[]{:S(2)}) collective-permute-start(bf16[64,1024]{1,0:T(8,128)(2,1)S(1)} %add_convert_fusion.refs_0_), channel_id=1, source_target_pairs={{0,16},{4,20},{8,24},{12,28},{16,0},{20,4},{24,8},{28,12},{1,17},{... | collective-permute-start | bytes 393224 | tf_op jit(solution)/shard_map/ppermute | solution.py:293
  67.3 12.2 %collective-permute-start.7 = (bf16[64,1024]{1,0:T(8,128)(2,1)S(1)}, bf16[64,1024]{1,0:T(8,128)(2,1)S(1)}, u32[]{:S(2)}, u32[]{:S(2)}) collective-permute-start(bf16[64,1024]{1,0:T(8,128)(2,1)S(1)} %add_convert_fusion.refs_0_), channel_id=1, source_target_pairs={{0,8},{4,12},{8,16},{12,20},{16,24},{20,28},{24,0},{28,4},{1,9},{5... | collective-permute-start | bytes 393224 | tf_op jit(solution)/shard_map/ppermute | solution.py:293
  67.4 13.3 %collective-permute-start.10 = (bf16[64,1024]{1,0:T(8,128)(2,1)S(1)}, bf16[64,1024]{1,0:T(8,128)(2,1)S(1)}, u32[]{:S(2)}, u32[]{:S(2)}) collective-permute-start(bf16[64,1024]{1,0:T(8,128)(2,1)S(1)} %add_convert_fusion.refs_0_), channel_id=1, source_target_pairs={{0,4},{4,0},{8,12},{12,8},{16,20},{20,16},{24,28},{28,24},{1,5},{5... | collective-permute-start | bytes 393224 | tf_op jit(solution)/shard_map/ppermute | solution.py:288
  70.0 10.7 %collective-permute-start.13 = (bf16[64,1024]{1,0:T(8,128)(2,1)S(1)}, bf16[64,1024]{1,0:T(8,128)(2,1)S(1)}, u32[]{:S(2)}, u32[]{:S(2)}) collective-permute-start(bf16[64,1024]{1,0:T(8,128)(2,1)S(1)} %collective-permute-done.9.refs_3_), channel_id=1, source_target_pairs={{0,4},{4,0},{8,12},{12,8},{16,20},{20,16},{24,28},{28,24},{1,5},{5... | collective-permute-start | bytes 393224 | tf_op jit(solution)/shard_map/ppermute | solution.py:288
  78.6 5.9 %collective-permute-start.12 = (bf16[64,1024]{1,0:T(8,128)(2,1)S(1)}, bf16[64,1024]{1,0:T(8,128)(2,1)S(1)}, u32[]{:S(2)}, u32[]{:S(2)}) collective-permute-start(bf16[64,1024]{1,0:T(8,128)(2,1)S(1)} %collective-permute-done.8.refs_2_), channel_id=1, source_target_pairs={{0,4},{4,0},{8,12},{12,8},{16,20},{20,16},{24,28},{28,24},{1,5},{5... | collective-permute-start | bytes 393224 | tf_op jit(solution)/shard_map/ppermute | solution.py:288
  79.5 6.5 %collective-permute-start.11 = (bf16[64,1024]{1,0:T(8,128)(2,1)S(1)}, bf16[64,1024]{1,0:T(8,128)(2,1)S(1)}, u32[]{:S(2)}, u32[]{:S(2)}) collective-permute-start(bf16[64,1024]{1,0:T(8,128)(2,1)S(1)} %collective-permute-done.7.refs_1_), channel_id=1, source_target_pairs={{0,4},{4,0},{8,12},{12,8},{16,20},{20,16},{24,28},{28,24},{1,5},{5... | collective-permute-start | bytes 393224 | tf_op jit(solution)/shard_map/ppermute | solution.py:288
  90.7 3.7 %collective-permute-start.14 = (f32[64,4096]{1,0:T(8,128)S(1)}, f32[64,4096]{1,0:T(8,128)S(1)}, u32[]{:S(2)}, u32[]{:S(2)}) collective-permute-start(f32[64,4096]{1,0:T(8,128)S(1)} %get-tuple-element.58), channel_id=1, source_target_pairs={{0,1},{1,0},{2,3},{3,2},{4,5},{5,4},{6,7},{7,6},{8,9},{9,8},{10,11... | collective-permute-start | bytes 3145736 | tf_op jit(solution)/shard_map/ppermute | solution.py:288
  94.5 14.5 %collective-permute-start.16 = (bf16[64,4096]{1,0:T(8,128)(2,1)S(1)}, bf16[64,4096]{1,0:T(8,128)(2,1)S(1)}, u32[]{:S(2)}, u32[]{:S(2)}) collective-permute-start(bf16[64,4096]{1,0:T(8,128)(2,1)S(1)} %fusion), channel_id=1, source_target_pairs={{0,2},{1,3},{2,0},{3,1},{4,6},{5,7},{6,4},{7,5},{8,10},{9,11},{10,... | collective-permute-start | bytes 1572872 | tf_op jit(solution)/shard_map/ppermute | solution.py:288
  99.1 10.0 %collective-permute-start.15 = (f32[64,4096]{1,0:T(8,128)S(1)}, f32[64,4096]{1,0:T(8,128)S(1)}, u32[]{:S(2)}, u32[]{:S(2)}) collective-permute-start(f32[64,4096]{1,0:T(8,128)S(1)} %backward.7), channel_id=1, source_target_pairs={{0,1},{1,0},{2,3},{3,2},{4,5},{5,4},{6,7},{7,6},{8,9},{9,8},{10,11... | collective-permute-start | bytes 3145736 | tf_op jit(solution)/shard_map/ppermute | solution.py:288
  109.3 14.4 %collective-permute-start.17 = (f32[64,4096]{1,0:T(8,128)S(1)}, f32[64,4096]{1,0:T(8,128)S(1)}, u32[]{:S(2)}, u32[]{:S(2)}) collective-permute-start(f32[64,4096]{1,0:T(8,128)S(1)} %convert_add_fusion.refs_0_), channel_id=1, source_target_pairs={{0,1},{1,0},{2,3},{3,2},{4,5},{5,4},{6,7},{7,6},{8,9},{9,8},{10,11... | collective-permute-start | bytes 3145736 | tf_op jit(solution)/shard_map/ppermute | solution.py:288
  109.6 14.1 %collective-permute-start.18 = (bf16[64,4096]{1,0:T(8,128)(2,1)S(1)}, bf16[64,4096]{1,0:T(8,128)(2,1)S(1)}, u32[]{:S(2)}, u32[]{:S(2)}) collective-permute-start(bf16[64,4096]{1,0:T(8,128)(2,1)S(1)} %reduce-precision_convert_fusion.refs_1_), channel_id=1, source_target_pairs={{0,2},{1,3},{2,0},{3,1},{4,6},{5,7},{6,4},{7,5},{8,10},{9,11},{10,... | collective-permute-start | bytes 1572872 | tf_op jit(solution)/shard_map/ppermute | solution.py:288
  109.6 15.6 %collective-permute-start.19 = (bf16[64,4096]{1,0:T(8,128)(2,1)S(1)}, bf16[64,4096]{1,0:T(8,128)(2,1)S(1)}, u32[]{:S(2)}, u32[]{:S(2)}) collective-permute-start(bf16[64,4096]{1,0:T(8,128)(2,1)S(1)} %reduce-precision_convert_fusion.refs_1_), channel_id=1, source_target_pairs={{0,1},{1,0},{2,3},{3,2},{4,5},{5,4},{6,7},{7,6},{8,9},{9,8},{10,11... | collective-permute-start | bytes 1572872 | tf_op jit(solution)/shard_map/ppermute | solution.py:288
  123.7 1.9 %collective-permute-start.20 = (bf16[64,4096]{1,0:T(8,128)(2,1)S(1)}, bf16[64,4096]{1,0:T(8,128)(2,1)S(1)}, u32[]{:S(2)}, u32[]{:S(2)}) collective-permute-start(bf16[64,4096]{1,0:T(8,128)(2,1)S(1)} %collective-permute-done.18.refs_2_), channel_id=1, source_target_pairs={{0,1},{1,0},{2,3},{3,2},{4,5},{5,4},{6,7},{7,6},{8,9},{9,8},{10,11... | collective-permute-start | bytes 1572872 | tf_op jit(solution)/shard_map/ppermute | solution.py:288

commit v8 on v7

--- a/solution.py
+++ b/solution.py
@@ -95,11 +95,11 @@
         block, row, _, away = decode(place)
         chosen = vectors[:, pl.ds(pl.multiple_of(block * BLK_P, BLK_P), BLK_P)]
         term = lax.dot_general(
-            buffer[...], chosen, (((1,), (1,)), ((), ())), preferred_element_type=f32
+            chosen, buffer[...], (((1,), (1,)), ((), ())), preferred_element_type=f32
         )
         if keep is not None:
             term = jnp.where(keep, term, 0.0)
-        part[away, :, pl.ds(pl.multiple_of(row * BLK_R, BLK_R), BLK_R)] += term.T
+        part[away, :, pl.ds(pl.multiple_of(row * BLK_R, BLK_R), BLK_R)] += term
 
     def save(buffer, parity, which, place):
         return pltpu.make_async_copy(buffer.at[parity], jac.at[place], sems.at[parity, which])

time: 128 us -> 135 us (1.055)
  waiting for transfers between devices: 43.4 us -> 31.9 us
  starting transfers between devices: 28.5 us -> 38.3 us
  Pallas kernels: 44.2 us -> 53.6 us
    ppermute x15, starting transfers between devices: 14.4 us -> 24.6 us  [swap(): lax.ppermute(array, axis, [(i, i ^ bit) for i in range(lax.axis_size(axis...]
    ppermute x6, waiting for transfers between devices: 12.8 us -> 3.58 us  [shift(): lax.ppermute(array, axis, [(i, (i + 2 * steps) % size) for i in range(siz...]
    pallas_call x4, Pallas kernels: 24.5 us -> 30.9 us  [forward(): pl.pallas_call(functools.partial(forward_kernel, blocks, capacity), out_s...]
    pallas_call x4, Pallas kernels: 16.9 us -> 19.9 us  [backward(): pl.pallas_call(functools.partial(kernel, capacity, total // 2), out_shape...]
    ppermute x15, waiting for transfers between devices: 25.2 us -> 22.9 us  [swap(): lax.ppermute(array, axis, [(i, i ^ bit) for i in range(lax.axis_size(axis...]
  transfers between devices with their start and end apart: 22 -> 22, of which waited for: 12 -> 8; matrix products, arithmetic and copies ran while one was open for 2% -> 2% of each run, Pallas kernels for 24% -> 29%
where the time goes in v8:
time: 135 us
  Pallas kernels  53.6 us (40%)
  starting transfers between devices  38.3 us (28%)
  waiting for transfers between devices  31.9 us (24%)
  other arithmetic  5.77 us (4%)
  local copies, waits for them, and re-layouts  4.25 us (3%)
    pallas_call x4, Pallas kernels, forward(): pl.pallas_call(functools.partial(forward_kernel, blocks, capacity), out_s...  30.9 us
    ppermute x15, starting transfers between devices, swap(): lax.ppermute(array, axis, [(i, i ^ bit) for i in range(lax.axis_size(axis...  24.6 us
    ppermute x15, waiting for transfers between devices, swap(): lax.ppermute(array, axis, [(i, i ^ bit) for i in range(lax.axis_size(axis...  22.9 us
    pallas_call x4, Pallas kernels, backward(): pl.pallas_call(functools.partial(kernel, capacity, total // 2), out_shape...  19.9 us
    all_to_all x1, starting transfers between devices, body(): left = lax.all_to_all(send, 'rows', split_axis=0, concat_axis=0, tiled=True)  7.25 us
    ppermute x6, starting transfers between devices, shift(): lax.ppermute(array, axis, [(i, (i + 2 * steps) % size) for i in range(siz...  6.51 us
    all_to_all x1, waiting for transfers between devices, body(): left = lax.all_to_all(send, 'rows', split_axis=0, concat_axis=0, tiled=True)  5.44 us
    ppermute x6, waiting for transfers between devices, shift(): lax.ppermute(array, axis, [(i, (i + 2 * steps) % size) for i in range(siz...  3.58 us
  transfers between devices with their start and end apart: 22, of which 8 were waited for; matrix products, arithmetic and copies ran while one was open for 2% of the time, Pallas kernels for 29%

profile of v8, /device:TPU:0, one launch (start us, length us, event | category | flops | bytes accessed | tf_op | source)
XLA Modules:
  0.0 134.8 jit_solution(3300459816411599673)
XLA Ops:
  0.7 0.9 select_reduce_fusion
  1.5 0.7 compare_select_fusion.4
  2.2 0.2 convert_reduce_fusion
  2.4 0.1 select_reduce_fusion.1
  2.5 0.1 convert_element_type.70
  2.6 0.7 stack.118
  3.3 0.7 fusion.8
  4.0 0.1 stack.99
  4.0 0.7 fusion.2
  4.7 7.3 %all-to-all-start = ((bf16[8,8,1024]{2,1,0:T(8,128)(2,1)}), bf16[8,8,1024]{2,1,0:T(8,128)(2,1)S(1)}, u32[]{:S(2)}, u32[]{:S(2)}) async-start(bf16[8,8,1024]{2,1,0:T(8,128)(2,1)} %fusion.2), calls=%async_computation | async-start | bytes 262144 | tf_op jit(solution)/shard_map/all_to_all | solution.py:342
  12.0 0.8 broadcast_in_dim.90
  12.8 0.8 multiply_convert_fusion
  13.6 0.1 broadcast_select_fusion
  13.8 0.1 pad_add_fusion
  13.8 0.1 pad_maximum_fusion.right
  13.9 5.4 %all-to-all-done.left = bf16[8,8,1024]{2,1,0:T(8,128)(2,1)S(1)} async-done(((bf16[8,8,1024]{2,1,0:T(8,128)(2,1)}), bf16[8,8,1024]{2,1,0:T(8,128)(2,1)S(1)}, u32[]{:S(2)}, u32[]{:S(2)}) %all-to-all-start) | async-done | bytes 131104 | tf_op jit(solution)/shard_map/all_to_all | solution.py:342
  19.4 0.1 reshape.102.codes.refs_0_
  19.4 1.6 %copy-done = bf16[64,16384]{1,0:T(8,128)(2,1)S(1)} copy-done((bf16[64,16384]{1,0:T(8,128)(2,1)S(1)}, bf16[64,16384]{1,0:T(8,128)(2,1)}, u32[]{:S(2)}) %copy-start) | copy-done | bytes 2097176
  21.0 9.8 %forward.4 = (f32[64,1024]{1,0:T(8,128)S(1)}, f32[64,1024]{1,0:T(8,128)S(1)}, bf16[129,256,512]{2,1,0:T(8,128)(2,1)}) custom-call(s32[128]{0:T(128)S(1)} %reshape.102.codes.refs_0_, s32[2]{0:T(128)S(1)} %get-tuple-element.76.where, bf16[8,8,1024]{2,1,0:T(8,128)(2,1)S(1)} %all-to-all-done.left, bf16[32,8,1024]{2,1,0:T(8,128)(2,1)S(1)} %pad_maximum_fusion.right, ...), custom_call_target="tpu_custom_call" | custom-call | flops 32 | bytes 64 | tf_op jit(solution)/shard_map/forward/pallas_call | solution.py:152
  30.8 1.7 %collective-permute-start = (f32[64,1024]{1,0:T(8,128)S(1)}, f32[64,1024]{1,0:T(8,128)S(1)}, u32[]{:S(2)}, u32[]{:S(2)}) collective-permute-start(f32[64,1024]{1,0:T(8,128)S(1)} %get-tuple-element.35), channel_id=1, source_target_pairs={{0,4},{4,0},{8,12},{12,8},{16,20},{20,16},{24,28},{28,24},{1,5},{5... | collective-permute-start | bytes 786440 | tf_op jit(solution)/shard_map/ppermute | solution.py:288
  32.6 1.6 %copy-done.1 = bf16[64,16384]{1,0:T(8,128)(2,1)S(1)} copy-done((bf16[64,16384]{1,0:T(8,128)(2,1)S(1)}, bf16[64,16384]{1,0:T(8,128)(2,1)}, u32[]{:S(2)}) %copy-start.1) | copy-done | bytes 2097176
  34.1 9.0 %forward.5 = (f32[64,1024]{1,0:T(8,128)S(1)}, f32[64,1024]{1,0:T(8,128)S(1)}, bf16[129,256,512]{2,1,0:T(8,128)(2,1)}) custom-call(s32[128]{0:T(128)S(1)} %reshape.102.codes.refs_0_, s32[2]{0:T(128)S(1)} %get-tuple-element.77.where, bf16[8,8,1024]{2,1,0:T(8,128)(2,1)S(1)} %all-to-all-done.left, ...), custom_call_target="tpu_custom_call", output_to_operand_aliasing={{2}: (5, {})} | custom-call | flops 32 | bytes 64 | tf_op jit(solution)/shard_map/forward/pallas_call | solution.py:152
  43.1 0.1 collective-permute-start.1
  43.3 0.1 collective-permute-start.2
  43.3 0.1 pad_add_fusion.2
  43.4 6.8 %forward.6 = (f32[64,1024]{1,0:T(8,128)S(1)}, f32[64,1024]{1,0:T(8,128)S(1)}, bf16[129,256,512]{2,1,0:T(8,128)(2,1)}) custom-call(s32[128]{0:T(128)S(1)} %reshape.102.codes.refs_0_, s32[2]{0:T(128)S(1)} %get-tuple-element.78.where, bf16[8,8,1024]{2,1,0:T(8,128)(2,1)S(1)} %all-to-all-done.left, ...), custom_call_target="tpu_custom_call", output_to_operand_aliasing={{2}: (5, {})} | custom-call | flops 32 | bytes 64 | tf_op jit(solution)/shard_map/forward/pallas_call | solution.py:152
  50.2 3.5 %collective-permute-start.3 = (f32[64,1024]{1,0:T(8,128)S(1)}, f32[64,1024]{1,0:T(8,128)S(1)}, u32[]{:S(2)}, u32[]{:S(2)}) collective-permute-start(f32[64,1024]{1,0:T(8,128)S(1)} %get-tuple-element.44), channel_id=1, source_target_pairs={{0,4},{4,0},{8,12},{12,8},{16,20},{20,16},{24,28},{28,24},{1,5},{5... | collective-permute-start | bytes 786440 | tf_op jit(solution)/shard_map/ppermute | solution.py:288
  53.7 0.0 collective-permute-done.1
  53.8 0.0 collective-permute-done.2
  53.8 2.6 %collective-permute-start.5 = (f32[64,1024]{1,0:T(8,128)S(1)}, f32[64,1024]{1,0:T(8,128)S(1)}, u32[]{:S(2)}, u32[]{:S(2)}) collective-permute-start(f32[64,1024]{1,0:T(8,128)S(1)} %add.126), channel_id=1, source_target_pairs={{0,16},{4,20},{8,24},{12,28},{16,0},{20,4},{24,8},{28,12},{1,17},{... | collective-permute-start | bytes 786440 | tf_op jit(solution)/shard_map/ppermute | solution.py:293
  56.4 5.3 %forward.7 = (f32[64,1024]{1,0:T(8,128)S(1)}, f32[64,1024]{1,0:T(8,128)S(1)}, bf16[129,256,512]{2,1,0:T(8,128)(2,1)}) custom-call(s32[128]{0:T(128)S(1)} %reshape.102.codes.refs_0_, s32[2]{0:T(128)S(1)} %get-tuple-element.79.where, bf16[8,8,1024]{2,1,0:T(8,128)(2,1)S(1)} %all-to-all-done.left, ...), custom_call_target="tpu_custom_call", output_to_operand_aliasing={{2}: (5, {})} | custom-call | flops 32 | bytes 64 | tf_op jit(solution)/shard_map/forward/pallas_call | solution.py:152
  61.8 3.7 %collective-permute-start.4 = (f32[64,1024]{1,0:T(8,128)S(1)}, f32[64,1024]{1,0:T(8,128)S(1)}, u32[]{:S(2)}, u32[]{:S(2)}) collective-permute-start(f32[64,1024]{1,0:T(8,128)S(1)} %get-tuple-element.50), channel_id=1, source_target_pairs={{0,4},{4,0},{8,12},{12,8},{16,20},{20,16},{24,28},{28,24},{1,5},{5... | collective-permute-start | bytes 786440 | tf_op jit(solution)/shard_map/ppermute | solution.py:288
  65.6 0.1 collective-permute-start.6
  65.6 4.2 %collective-permute-done.4 = f32[64,1024]{1,0:T(8,128)S(1)} collective-permute-done((f32[64,1024]{1,0:T(8,128)S(1)}, f32[64,1024]{1,0:T(8,128)S(1)}, u32[]{:S(2)}, u32[]{:S(2)}) %collective-permute-start.4) | collective-permute-done | bytes 262176 | tf_op jit(solution)/shard_map/ppermute | solution.py:288
  69.9 2.6 %collective-permute-done.6 = bf16[64,1024]{1,0:T(8,128)(2,1)S(1)} collective-permute-done((bf16[64,1024]{1,0:T(8,128)(2,1)S(1)}, bf16[64,1024]{1,0:T(8,128)(2,1)S(1)}, u32[]{:S(2)}, u32[]{:S(2)}) %collective-permute-start.6) | collective-permute-done | bytes 131104 | tf_op jit(solution)/shard_map/ppermute | solution.py:293
  72.5 0.1 add_convert_fusion.refs_0_
  72.6 3.1 %collective-permute-start.9 = (bf16[64,1024]{1,0:T(8,128)(2,1)S(1)}, bf16[64,1024]{1,0:T(8,128)(2,1)S(1)}, u32[]{:S(2)}, u32[]{:S(2)}) collective-permute-start(bf16[64,1024]{1,0:T(8,128)(2,1)S(1)} %add_convert_fusion.refs_0_), channel_id=1, source_target_pairs={{0,24},{4,28},{8,0},{12,4},{16,8},{20,12},{24,16},{28,20},{1,25},{... | collective-permute-start | bytes 393224 | tf_op jit(solution)/shard_map/ppermute | solution.py:293
  75.7 0.6 collective-permute-start.7
  76.3 0.1 pad_add_fusion.8
  76.4 3.8 %collective-permute-start.10 = (bf16[64,1024]{1,0:T(8,128)(2,1)S(1)}, bf16[64,1024]{1,0:T(8,128)(2,1)S(1)}, u32[]{:S(2)}, u32[]{:S(2)}) collective-permute-start(bf16[64,1024]{1,0:T(8,128)(2,1)S(1)} %add_convert_fusion.refs_0_), channel_id=1, source_target_pairs={{0,4},{4,0},{8,12},{12,8},{16,20},{20,16},{24,28},{28,24},{1,5},{5... | collective-permute-start | bytes 393224 | tf_op jit(solution)/shard_map/ppermute | solution.py:288
  80.2 1.8 %collective-permute-start.13 = (bf16[64,1024]{1,0:T(8,128)(2,1)S(1)}, bf16[64,1024]{1,0:T(8,128)(2,1)S(1)}, u32[]{:S(2)}, u32[]{:S(2)}) collective-permute-start(bf16[64,1024]{1,0:T(8,128)(2,1)S(1)} %collective-permute-done.9.refs_3_), channel_id=1, source_target_pairs={{0,4},{4,0},{8,12},{12,8},{16,20},{20,16},{24,28},{28,24},{1,5},{5... | collective-permute-start | bytes 393224 | tf_op jit(solution)/shard_map/ppermute | solution.py:288
  82.0 1.0 collective-permute-done.8.refs_2_
  83.0 3.8 %collective-permute-start.12 = (bf16[64,1024]{1,0:T(8,128)(2,1)S(1)}, bf16[64,1024]{1,0:T(8,128)(2,1)S(1)}, u32[]{:S(2)}, u32[]{:S(2)}) collective-permute-start(bf16[64,1024]{1,0:T(8,128)(2,1)S(1)} %collective-permute-done.8.refs_2_), channel_id=1, source_target_pairs={{0,4},{4,0},{8,12},{12,8},{16,20},{20,16},{24,28},{28,24},{1,5},{5... | collective-permute-start | bytes 393224 | tf_op jit(solution)/shard_map/ppermute | solution.py:288
  86.8 0.0 collective-permute-start.11
  86.8 0.1 pad_add_fusion.7
  86.9 2.8 %collective-permute-done.12.refs_6_ = bf16[64,1024]{1,0:T(8,128)(2,1)S(1)} collective-permute-done((bf16[64,1024]{1,0:T(8,128)(2,1)S(1)}, bf16[64,1024]{1,0:T(8,128)(2,1)S(1)}, u32[]{:S(2)}, u32[]{:S(2)}) %collective-permute-start.12) | collective-permute-done | bytes 131104 | tf_op jit(solution)/shard_map/ppermute | solution.py:288
  89.7 2.0 %collective-permute-done.11.refs_5_ = bf16[64,1024]{1,0:T(8,128)(2,1)S(1)} collective-permute-done((bf16[64,1024]{1,0:T(8,128)(2,1)S(1)}, bf16[64,1024]{1,0:T(8,128)(2,1)S(1)}, u32[]{:S(2)}, u32[]{:S(2)}) %collective-permute-start.11) | collective-permute-done | bytes 131104 | tf_op jit(solution)/shard_map/ppermute | solution.py:288
  91.7 3.6 %backward.4 = (f32[64,4096]{1,0:T(8,128)S(1)}, bf16[8,64,1024]{2,1,0:T(8,128)(2,1)S(1)}) custom-call(s32[128]{0:T(128)S(1)} %reshape.102.codes.refs_0_, s32[3]{0:T(128)S(1)} %get-tuple-element.72.where, bf16[129,256,512]{2,1,0:T(8,128)(2,1)} %get-tuple-element.48.jac.refs_2_, bf16[64,1024]{1,0:T(8,128)(2,1)S(1)} %add_convert_fusion.refs_0_, ...), custom_call_target="tpu_custom_call" | custom-call | flops 16 | bytes 64 | tf_op jit(solution)/shard_map/backward/pallas_call | solution.py:231
  95.4 0.1 collective-permute-start.14
  95.4 4.9 %backward.5 = f32[64,4096]{1,0:T(8,128)S(1)} custom-call(s32[128]{0:T(128)S(1)} %reshape.102.codes.refs_0_, s32[3]{0:T(128)S(1)} %get-tuple-element.73.refs_1_, bf16[129,256,512]{2,1,0:T(8,128)(2,1)} %get-tuple-element.48.jac.refs_2_, bf16[8,64,1024]{2,1,0:T(8,128)(2,1)S(1)} %get-tuple-element.57.refs_3_), custom_call_target="tpu_custom_call" | custom-call | flops 16 | bytes 64 | tf_op jit(solution)/shard_map/backward/pallas_call | solution.py:231
  100.4 0.1 fusion
  100.5 4.8 %collective-permute-start.16 = (bf16[64,4096]{1,0:T(8,128)(2,1)S(1)}, bf16[64,4096]{1,0:T(8,128)(2,1)S(1)}, u32[]{:S(2)}, u32[]{:S(2)}) collective-permute-start(bf16[64,4096]{1,0:T(8,128)(2,1)S(1)} %fusion), channel_id=1, source_target_pairs={{0,2},{1,3},{2,0},{3,1},{4,6},{5,7},{6,4},{7,5},{8,10},{9,11},{10,... | collective-permute-start | bytes 1572872 | tf_op jit(solution)/shard_map/ppermute | solution.py:288
  105.3 6.0 %backward.7 = f32[64,4096]{1,0:T(8,128)S(1)} custom-call(s32[128]{0:T(128)S(1)} %reshape.102.codes.refs_0_, s32[3]{0:T(128)S(1)} %get-tuple-element.63.refs_1_, bf16[129,256,512]{2,1,0:T(8,128)(2,1)} %get-tuple-element.48.jac.refs_2_, bf16[8,64,1024]{2,1,0:T(8,128)(2,1)S(1)} %get-tuple-element.57.refs_3_), custom_call_target="tpu_custom_call" | custom-call | flops 16 | bytes 64 | tf_op jit(solution)/shard_map/backward/pallas_call | solution.py:231
  111.3 0.1 collective-permute-start.15
  111.4 5.3 %backward.6 = f32[64,4096]{1,0:T(8,128)S(1)} custom-call(s32[128]{0:T(128)S(1)} %reshape.102.codes.refs_0_, s32[3]{0:T(128)S(1)} %get-tuple-element.71.refs_1_, bf16[129,256,512]{2,1,0:T(8,128)(2,1)} %get-tuple-element.48.jac.refs_2_, bf16[8,64,1024]{2,1,0:T(8,128)(2,1)S(1)} %get-tuple-element.57.refs_3_), custom_call_target="tpu_custom_call" | custom-call | flops 16 | bytes 64 | tf_op jit(solution)/shard_map/backward/pallas_call | solution.py:231
  116.7 0.1 convert_add_fusion.refs_0_
  116.9 0.1 reduce-precision_convert_fusion.refs_1_
  117.0 0.6 collective-permute-start.17
  117.6 0.5 collective-permute-start.18
  118.0 0.2 collective-permute-start.19
  118.2 13.3 %collective-permute-done.18.refs_2_ = bf16[64,4096]{1,0:T(8,128)(2,1)S(1)} collective-permute-done((bf16[64,4096]{1,0:T(8,128)(2,1)S(1)}, bf16[64,4096]{1,0:T(8,128)(2,1)S(1)}, u32[]{:S(2)}, u32[]{:S(2)}) %collective-permute-start.18) | collective-permute-done | bytes 524320 | tf_op jit(solution)/shard_map/ppermute | solution.py:288
  131.5 1.4 %place.2.refs_0_ = f32[64,16384]{1,0:T(8,128)} custom-call(s32[1]{0:T(128)} %bitcast.where, f32[64,4096]{1,0:T(8,128)S(1)} %convert_add_fusion.refs_0_, f32[64,4096]{1,0:T(8,128)S(1)} %collective-permute-done.17.refs_1_), custom_call_target="tpu_custom_call" | custom-call | tf_op jit(solution)/shard_map/place/pallas_call | solution.py:272
  132.9 0.5 collective-permute-done.20.refs_4_
  133.4 1.4 %place.3 = f32[64,16384]{1,0:T(8,128)} custom-call(s32[1]{0:T(128)} %bitcast.where, f32[64,16384]{1,0:T(8,128)} %place.2.refs_0_, bf16[64,4096]{1,0:T(8,128)(2,1)S(1)} %reduce-precision_convert_fusion.refs_1_, bf16[64,4096]{1,0:T(8,128)(2,1)S(1)} %collective-permute-done.18.refs_2_, ...), custom_call_target="tpu_custom_call", output_to_operand_aliasing={{}: (1, {})} | custom-call | tf_op jit(solution)/shard_map/place/pallas_call | solution.py:272
  (26 shorter events, 0.2 us)
Async XLA Ops:
  4.7 14.6 %all-to-all-start = ((bf16[8,8,1024]{2,1,0:T(8,128)(2,1)}), bf16[8,8,1024]{2,1,0:T(8,128)(2,1)S(1)}, u32[]{:S(2)}, u32[]{:S(2)}) async-start(bf16[8,8,1024]{2,1,0:T(8,128)(2,1)} %fusion.2), calls=%async_computation | async-start | bytes 262144 | tf_op jit(solution)/shard_map/all_to_all | solution.py:342
  19.4 1.6 %copy-start = (bf16[64,16384]{1,0:T(8,128)(2,1)S(1)}, bf16[64,16384]{1,0:T(8,128)(2,1)}, u32[]{:S(2)}) copy-start(bf16[64,16384]{1,0:T(8,128)(2,1)} %vectors.7) | copy-start | bytes 6291460
  30.8 12.4 %collective-permute-start = (f32[64,1024]{1,0:T(8,128)S(1)}, f32[64,1024]{1,0:T(8,128)S(1)}, u32[]{:S(2)}, u32[]{:S(2)}) collective-permute-start(f32[64,1024]{1,0:T(8,128)S(1)} %get-tuple-element.35), channel_id=1, source_target_pairs={{0,4},{4,0},{8,12},{12,8},{16,20},{20,16},{24,28},{28,24},{1,5},{5... | collective-permute-start | bytes 786440 | tf_op jit(solution)/shard_map/ppermute | solution.py:288
  32.6 1.6 %copy-start.1 = (bf16[64,16384]{1,0:T(8,128)(2,1)S(1)}, bf16[64,16384]{1,0:T(8,128)(2,1)}, u32[]{:S(2)}) copy-start(bf16[64,16384]{1,0:T(8,128)(2,1)} %vectors.7) | copy-start | bytes 6291460
  43.1 10.6 %collective-permute-start.1 = (f32[64,1024]{1,0:T(8,128)S(1)}, f32[64,1024]{1,0:T(8,128)S(1)}, u32[]{:S(2)}, u32[]{:S(2)}) collective-permute-start(f32[64,1024]{1,0:T(8,128)S(1)} %get-tuple-element.39), channel_id=1, source_target_pairs={{0,4},{4,0},{8,12},{12,8},{16,20},{20,16},{24,28},{28,24},{1,5},{5... | collective-permute-start | bytes 786440 | tf_op jit(solution)/shard_map/ppermute | solution.py:288
  43.3 10.5 %collective-permute-start.2 = (f32[64,1024]{1,0:T(8,128)S(1)}, f32[64,1024]{1,0:T(8,128)S(1)}, u32[]{:S(2)}, u32[]{:S(2)}) collective-permute-start(f32[64,1024]{1,0:T(8,128)S(1)} %add.124), channel_id=1, source_target_pairs={{0,24},{4,28},{8,0},{12,4},{16,8},{20,12},{24,16},{28,20},{1,25},{... | collective-permute-start | bytes 786440 | tf_op jit(solution)/shard_map/ppermute | solution.py:293
  50.2 15.3 %collective-permute-start.3 = (f32[64,1024]{1,0:T(8,128)S(1)}, f32[64,1024]{1,0:T(8,128)S(1)}, u32[]{:S(2)}, u32[]{:S(2)}) collective-permute-start(f32[64,1024]{1,0:T(8,128)S(1)} %get-tuple-element.44), channel_id=1, source_target_pairs={{0,4},{4,0},{8,12},{12,8},{16,20},{20,16},{24,28},{28,24},{1,5},{5... | collective-permute-start | bytes 786440 | tf_op jit(solution)/shard_map/ppermute | solution.py:288
  53.8 11.8 %collective-permute-start.5 = (f32[64,1024]{1,0:T(8,128)S(1)}, f32[64,1024]{1,0:T(8,128)S(1)}, u32[]{:S(2)}, u32[]{:S(2)}) collective-permute-start(f32[64,1024]{1,0:T(8,128)S(1)} %add.126), channel_id=1, source_target_pairs={{0,16},{4,20},{8,24},{12,28},{16,0},{20,4},{24,8},{28,12},{1,17},{... | collective-permute-start | bytes 786440 | tf_op jit(solution)/shard_map/ppermute | solution.py:293
  61.8 8.1 %collective-permute-start.4 = (f32[64,1024]{1,0:T(8,128)S(1)}, f32[64,1024]{1,0:T(8,128)S(1)}, u32[]{:S(2)}, u32[]{:S(2)}) collective-permute-start(f32[64,1024]{1,0:T(8,128)S(1)} %get-tuple-element.50), channel_id=1, source_target_pairs={{0,4},{4,0},{8,12},{12,8},{16,20},{20,16},{24,28},{28,24},{1,5},{5... | collective-permute-start | bytes 786440 | tf_op jit(solution)/shard_map/ppermute | solution.py:288
  65.6 6.9 %collective-permute-start.6 = (bf16[64,1024]{1,0:T(8,128)(2,1)S(1)}, bf16[64,1024]{1,0:T(8,128)(2,1)S(1)}, u32[]{:S(2)}, u32[]{:S(2)}) collective-permute-start(bf16[64,1024]{1,0:T(8,128)(2,1)S(1)} %add_convert_fusion.1), channel_id=1, source_target_pairs={{0,8},{4,12},{8,16},{12,20},{16,24},{20,28},{24,0},{28,4},{1,9},{5... | collective-permute-start | bytes 393224 | tf_op jit(solution)/shard_map/ppermute | solution.py:293
  72.6 7.6 %collective-permute-start.9 = (bf16[64,1024]{1,0:T(8,128)(2,1)S(1)}, bf16[64,1024]{1,0:T(8,128)(2,1)S(1)}, u32[]{:S(2)}, u32[]{:S(2)}) collective-permute-start(bf16[64,1024]{1,0:T(8,128)(2,1)S(1)} %add_convert_fusion.refs_0_), channel_id=1, source_target_pairs={{0,24},{4,28},{8,0},{12,4},{16,8},{20,12},{24,16},{28,20},{1,25},{... | collective-permute-start | bytes 393224 | tf_op jit(solution)/shard_map/ppermute | solution.py:293
  75.7 7.3 %collective-permute-start.8 = (bf16[64,1024]{1,0:T(8,128)(2,1)S(1)}, bf16[64,1024]{1,0:T(8,128)(2,1)S(1)}, u32[]{:S(2)}, u32[]{:S(2)}) collective-permute-start(bf16[64,1024]{1,0:T(8,128)(2,1)S(1)} %add_convert_fusion.refs_0_), channel_id=1, source_target_pairs={{0,16},{4,20},{8,24},{12,28},{16,0},{20,4},{24,8},{28,12},{1,17},{... | collective-permute-start | bytes 393224 | tf_op jit(solution)/shard_map/ppermute | solution.py:293
  75.7 11.0 %collective-permute-start.7 = (bf16[64,1024]{1,0:T(8,128)(2,1)S(1)}, bf16[64,1024]{1,0:T(8,128)(2,1)S(1)}, u32[]{:S(2)}, u32[]{:S(2)}) collective-permute-start(bf16[64,1024]{1,0:T(8,128)(2,1)S(1)} %add_convert_fusion.refs_0_), channel_id=1, source_target_pairs={{0,8},{4,12},{8,16},{12,20},{16,24},{20,28},{24,0},{28,4},{1,9},{5... | collective-permute-start | bytes 393224 | tf_op jit(solution)/shard_map/ppermute | solution.py:293
  76.4 10.4 %collective-permute-start.10 = (bf16[64,1024]{1,0:T(8,128)(2,1)S(1)}, bf16[64,1024]{1,0:T(8,128)(2,1)S(1)}, u32[]{:S(2)}, u32[]{:S(2)}) collective-permute-start(bf16[64,1024]{1,0:T(8,128)(2,1)S(1)} %add_convert_fusion.refs_0_), channel_id=1, source_target_pairs={{0,4},{4,0},{8,12},{12,8},{16,20},{20,16},{24,28},{28,24},{1,5},{5... | collective-permute-start | bytes 393224 | tf_op jit(solution)/shard_map/ppermute | solution.py:288
  80.2 6.7 %collective-permute-start.13 = (bf16[64,1024]{1,0:T(8,128)(2,1)S(1)}, bf16[64,1024]{1,0:T(8,128)(2,1)S(1)}, u32[]{:S(2)}, u32[]{:S(2)}) collective-permute-start(bf16[64,1024]{1,0:T(8,128)(2,1)S(1)} %collective-permute-done.9.refs_3_), channel_id=1, source_target_pairs={{0,4},{4,0},{8,12},{12,8},{16,20},{20,16},{24,28},{28,24},{1,5},{5... | collective-permute-start | bytes 393224 | tf_op jit(solution)/shard_map/ppermute | solution.py:288
  83.0 6.7 %collective-permute-start.12 = (bf16[64,1024]{1,0:T(8,128)(2,1)S(1)}, bf16[64,1024]{1,0:T(8,128)(2,1)S(1)}, u32[]{:S(2)}, u32[]{:S(2)}) collective-permute-start(bf16[64,1024]{1,0:T(8,128)(2,1)S(1)} %collective-permute-done.8.refs_2_), channel_id=1, source_target_pairs={{0,4},{4,0},{8,12},{12,8},{16,20},{20,16},{24,28},{28,24},{1,5},{5... | collective-permute-start | bytes 393224 | tf_op jit(solution)/shard_map/ppermute | solution.py:288
  86.8 5.0 %collective-permute-start.11 = (bf16[64,1024]{1,0:T(8,128)(2,1)S(1)}, bf16[64,1024]{1,0:T(8,128)(2,1)S(1)}, u32[]{:S(2)}, u32[]{:S(2)}) collective-permute-start(bf16[64,1024]{1,0:T(8,128)(2,1)S(1)} %collective-permute-done.7.refs_1_), channel_id=1, source_target_pairs={{0,4},{4,0},{8,12},{12,8},{16,20},{20,16},{24,28},{28,24},{1,5},{5... | collective-permute-start | bytes 393224 | tf_op jit(solution)/shard_map/ppermute | solution.py:288
  95.4 5.0 %collective-permute-start.14 = (f32[64,4096]{1,0:T(8,128)S(1)}, f32[64,4096]{1,0:T(8,128)S(1)}, u32[]{:S(2)}, u32[]{:S(2)}) collective-permute-start(f32[64,4096]{1,0:T(8,128)S(1)} %get-tuple-element.58), channel_id=1, source_target_pairs={{0,1},{1,0},{2,3},{3,2},{4,5},{5,4},{6,7},{7,6},{8,9},{9,8},{10,11... | collective-permute-start | bytes 3145736 | tf_op jit(solution)/shard_map/ppermute | solution.py:288
  100.5 16.2 %collective-permute-start.16 = (bf16[64,4096]{1,0:T(8,128)(2,1)S(1)}, bf16[64,4096]{1,0:T(8,128)(2,1)S(1)}, u32[]{:S(2)}, u32[]{:S(2)}) collective-permute-start(bf16[64,4096]{1,0:T(8,128)(2,1)S(1)} %fusion), channel_id=1, source_target_pairs={{0,2},{1,3},{2,0},{3,1},{4,6},{5,7},{6,4},{7,5},{8,10},{9,11},{10,... | collective-permute-start | bytes 1572872 | tf_op jit(solution)/shard_map/ppermute | solution.py:288
  111.3 5.5 %collective-permute-start.15 = (f32[64,4096]{1,0:T(8,128)S(1)}, f32[64,4096]{1,0:T(8,128)S(1)}, u32[]{:S(2)}, u32[]{:S(2)}) collective-permute-start(f32[64,4096]{1,0:T(8,128)S(1)} %backward.7), channel_id=1, source_target_pairs={{0,1},{1,0},{2,3},{3,2},{4,5},{5,4},{6,7},{7,6},{8,9},{9,8},{10,11... | collective-permute-start | bytes 3145736 | tf_op jit(solution)/shard_map/ppermute | solution.py:288
  117.0 14.5 %collective-permute-start.17 = (f32[64,4096]{1,0:T(8,128)S(1)}, f32[64,4096]{1,0:T(8,128)S(1)}, u32[]{:S(2)}, u32[]{:S(2)}) collective-permute-start(f32[64,4096]{1,0:T(8,128)S(1)} %convert_add_fusion.refs_0_), channel_id=1, source_target_pairs={{0,1},{1,0},{2,3},{3,2},{4,5},{5,4},{6,7},{7,6},{8,9},{9,8},{10,11... | collective-permute-start | bytes 3145736 | tf_op jit(solution)/shard_map/ppermute | solution.py:288
  117.6 13.9 %collective-permute-start.18 = (bf16[64,4096]{1,0:T(8,128)(2,1)S(1)}, bf16[64,4096]{1,0:T(8,128)(2,1)S(1)}, u32[]{:S(2)}, u32[]{:S(2)}) collective-permute-start(bf16[64,4096]{1,0:T(8,128)(2,1)S(1)} %reduce-precision_convert_fusion.refs_1_), channel_id=1, source_target_pairs={{0,2},{1,3},{2,0},{3,1},{4,6},{5,7},{6,4},{7,5},{8,10},{9,11},{10,... | collective-permute-start | bytes 1572872 | tf_op jit(solution)/shard_map/ppermute | solution.py:288
  118.0 14.9 %collective-permute-start.19 = (bf16[64,4096]{1,0:T(8,128)(2,1)S(1)}, bf16[64,4096]{1,0:T(8,128)(2,1)S(1)}, u32[]{:S(2)}, u32[]{:S(2)}) collective-permute-start(bf16[64,4096]{1,0:T(8,128)(2,1)S(1)} %reduce-precision_convert_fusion.refs_1_), channel_id=1, source_target_pairs={{0,1},{1,0},{2,3},{3,2},{4,5},{5,4},{6,7},{7,6},{8,9},{9,8},{10,11... | collective-permute-start | bytes 1572872 | tf_op jit(solution)/shard_map/ppermute | solution.py:288
  131.5 1.9 %collective-permute-start.20 = (bf16[64,4096]{1,0:T(8,128)(2,1)S(1)}, bf16[64,4096]{1,0:T(8,128)(2,1)S(1)}, u32[]{:S(2)}, u32[]{:S(2)}) collective-permute-start(bf16[64,4096]{1,0:T(8,128)(2,1)S(1)} %collective-permute-done.18.refs_2_), channel_id=1, source_target_pairs={{0,1},{1,0},{2,3},{3,2},{4,5},{5,4},{6,7},{7,6},{8,9},{9,8},{10,11... | collective-permute-start | bytes 1572872 | tf_op jit(solution)/shard_map/ppermute | solution.py:288

commit v9 on v8

--- a/solution.py
+++ b/solution.py
@@ -115,12 +115,12 @@
             save(even, parity, 0, 0).wait()
             save(odd, parity, 1, 0).wait()
 
-        apply(odd.at[1 - parity], before, turn > 0)
         make(even.at[parity], first)
         save(even, parity, 0, first).start()
-        apply(even.at[parity], first, None)
+        apply(odd.at[1 - parity], before, turn > 0)
         make(odd.at[parity], second)
         save(odd, parity, 1, jnp.where(paired, second, spare)).start()
+        apply(even.at[parity], first, None)
         return second
 
     last = lax.fori_loop(0, steps, step, todo[0])

time: 135 us -> 135 us (level)
  Pallas kernels: 53.6 us -> 48.5 us
  starting transfers between devices: 38.3 us -> 40.4 us
  waiting for transfers between devices: 31.9 us -> 33.7 us
    pallas_call x4, Pallas kernels: 30.9 us -> 27.1 us  [forward(): pl.pallas_call(functools.partial(forward_kernel, blocks, capacity), out_s...]
    ppermute x15, starting transfers between devices: 24.6 us -> 26.8 us  [swap(): lax.ppermute(array, axis, [(i, i ^ bit) for i in range(lax.axis_size(axis...]
  transfers between devices with their start and end apart: 22 -> 22, of which waited for: 8 -> 12; matrix products, arithmetic and copies ran while one was open for 2% -> 2% of each run, Pallas kernels for 29% -> 25%
where the time goes in v9:
time: 135 us; the launch traced here: 134 us
  Pallas kernels  48.5 us (36%)
  starting transfers between devices  40.4 us (30%)
  waiting for transfers between devices  33.7 us (25%)
  other arithmetic  5.77 us (4%)
  local copies, waits for them, and re-layouts  4.25 us (3%)
    pallas_call x4, Pallas kernels, forward(): pl.pallas_call(functools.partial(forward_kernel, blocks, capacity), out_s...  27.1 us
    ppermute x15, starting transfers between devices, swap(): lax.ppermute(array, axis, [(i, i ^ bit) for i in range(lax.axis_size(axis...  26.8 us
    ppermute x15, waiting for transfers between devices, swap(): lax.ppermute(array, axis, [(i, i ^ bit) for i in range(lax.axis_size(axis...  23.5 us
    pallas_call x4, Pallas kernels, backward(): pl.pallas_call(functools.partial(kernel, capacity, total // 2), out_shape...  18.6 us
    all_to_all x1, starting transfers between devices, body(): left = lax.all_to_all(send, 'rows', split_axis=0, concat_axis=0, tiled=True)  7.25 us
    ppermute x6, starting transfers between devices, shift(): lax.ppermute(array, axis, [(i, (i + 2 * steps) % size) for i in range(siz...  6.33 us
    all_to_all x1, waiting for transfers between devices, body(): left = lax.all_to_all(send, 'rows', split_axis=0, concat_axis=0, tiled=True)  5.44 us
    ppermute x6, waiting for transfers between devices, shift(): lax.ppermute(array, axis, [(i, (i + 2 * steps) % size) for i in range(siz...  4.68 us
  transfers between devices with their start and end apart: 22, of which 12 were waited for; matrix products, arithmetic and copies ran while one was open for 2% of the time, Pallas kernels for 25%

profile of v9, /device:TPU:0, one launch (start us, length us, event | category | flops | bytes accessed | tf_op | source)
XLA Modules:
  0.0 133.5 jit_solution(8999248088318525114)
XLA Ops:
  0.7 0.9 select_reduce_fusion
  1.5 0.7 compare_select_fusion.4
  2.2 0.2 convert_reduce_fusion
  2.4 0.1 select_reduce_fusion.1
  2.5 0.1 convert_element_type.70
  2.6 0.7 stack.118
  3.3 0.7 fusion.8
  4.0 0.1 stack.99
  4.0 0.7 fusion.2
  4.7 7.3 %all-to-all-start = ((bf16[8,8,1024]{2,1,0:T(8,128)(2,1)}), bf16[8,8,1024]{2,1,0:T(8,128)(2,1)S(1)}, u32[]{:S(2)}, u32[]{:S(2)}) async-start(bf16[8,8,1024]{2,1,0:T(8,128)(2,1)} %fusion.2), calls=%async_computation | async-start | bytes 262144 | tf_op jit(solution)/shard_map/all_to_all | solution.py:342
  12.0 0.8 broadcast_in_dim.90
  12.8 0.8 multiply_convert_fusion
  13.6 0.1 broadcast_select_fusion
  13.8 0.1 pad_add_fusion
  13.9 5.4 %all-to-all-done.left = bf16[8,8,1024]{2,1,0:T(8,128)(2,1)S(1)} async-done(((bf16[8,8,1024]{2,1,0:T(8,128)(2,1)}), bf16[8,8,1024]{2,1,0:T(8,128)(2,1)S(1)}, u32[]{:S(2)}, u32[]{:S(2)}) %all-to-all-start) | async-done | bytes 131104 | tf_op jit(solution)/shard_map/all_to_all | solution.py:342
  19.4 0.1 reshape.102.codes.refs_0_
  19.4 1.6 %copy-done = bf16[64,16384]{1,0:T(8,128)(2,1)S(1)} copy-done((bf16[64,16384]{1,0:T(8,128)(2,1)S(1)}, bf16[64,16384]{1,0:T(8,128)(2,1)}, u32[]{:S(2)}) %copy-start) | copy-done | bytes 2097176
  21.0 7.8 %forward.4 = (f32[64,1024]{1,0:T(8,128)S(1)}, f32[64,1024]{1,0:T(8,128)S(1)}, bf16[129,256,512]{2,1,0:T(8,128)(2,1)}) custom-call(s32[128]{0:T(128)S(1)} %reshape.102.codes.refs_0_, s32[2]{0:T(128)S(1)} %get-tuple-element.76.where, bf16[8,8,1024]{2,1,0:T(8,128)(2,1)S(1)} %all-to-all-done.left, bf16[32,8,1024]{2,1,0:T(8,128)(2,1)S(1)} %pad_maximum_fusion.right, ...), custom_call_target="tpu_custom_call" | custom-call | flops 32 | bytes 64 | tf_op jit(solution)/shard_map/forward/pallas_call | solution.py:152
  28.9 0.9 collective-permute-start
  29.8 1.6 %copy-done.1 = bf16[64,16384]{1,0:T(8,128)(2,1)S(1)} copy-done((bf16[64,16384]{1,0:T(8,128)(2,1)S(1)}, bf16[64,16384]{1,0:T(8,128)(2,1)}, u32[]{:S(2)}) %copy-start.1) | copy-done | bytes 2097176
  31.4 7.1 %forward.5 = (f32[64,1024]{1,0:T(8,128)S(1)}, f32[64,1024]{1,0:T(8,128)S(1)}, bf16[129,256,512]{2,1,0:T(8,128)(2,1)}) custom-call(s32[128]{0:T(128)S(1)} %reshape.102.codes.refs_0_, s32[2]{0:T(128)S(1)} %get-tuple-element.77.where, bf16[8,8,1024]{2,1,0:T(8,128)(2,1)S(1)} %all-to-all-done.left, ...), custom_call_target="tpu_custom_call", output_to_operand_aliasing={{2}: (5, {})} | custom-call | flops 32 | bytes 64 | tf_op jit(solution)/shard_map/forward/pallas_call | solution.py:152
  38.5 1.2 collective-permute-start.1
  39.8 0.1 collective-permute-start.2
  39.8 0.1 pad_add_fusion.2
  39.9 7.8 %forward.6 = (f32[64,1024]{1,0:T(8,128)S(1)}, f32[64,1024]{1,0:T(8,128)S(1)}, bf16[129,256,512]{2,1,0:T(8,128)(2,1)}) custom-call(s32[128]{0:T(128)S(1)} %reshape.102.codes.refs_0_, s32[2]{0:T(128)S(1)} %get-tuple-element.78.where, bf16[8,8,1024]{2,1,0:T(8,128)(2,1)S(1)} %all-to-all-done.left, ...), custom_call_target="tpu_custom_call", output_to_operand_aliasing={{2}: (5, {})} | custom-call | flops 32 | bytes 64 | tf_op jit(solution)/shard_map/forward/pallas_call | solution.py:152
  47.7 0.1 collective-permute-start.3
  47.9 1.4 %collective-permute-start.5 = (f32[64,1024]{1,0:T(8,128)S(1)}, f32[64,1024]{1,0:T(8,128)S(1)}, u32[]{:S(2)}, u32[]{:S(2)}) collective-permute-start(f32[64,1024]{1,0:T(8,128)S(1)} %add.126), channel_id=1, source_target_pairs={{0,16},{4,20},{8,24},{12,28},{16,0},{20,4},{24,8},{28,12},{1,17},{... | collective-permute-start | bytes 786440 | tf_op jit(solution)/shard_map/ppermute | solution.py:293
  49.3 4.4 %forward.7 = (f32[64,1024]{1,0:T(8,128)S(1)}, f32[64,1024]{1,0:T(8,128)S(1)}, bf16[129,256,512]{2,1,0:T(8,128)(2,1)}) custom-call(s32[128]{0:T(128)S(1)} %reshape.102.codes.refs_0_, s32[2]{0:T(128)S(1)} %get-tuple-element.79.where, bf16[8,8,1024]{2,1,0:T(8,128)(2,1)S(1)} %all-to-all-done.left, ...), custom_call_target="tpu_custom_call", output_to_operand_aliasing={{2}: (5, {})} | custom-call | flops 32 | bytes 64 | tf_op jit(solution)/shard_map/forward/pallas_call | solution.py:152
  53.7 4.1 %collective-permute-start.4 = (f32[64,1024]{1,0:T(8,128)S(1)}, f32[64,1024]{1,0:T(8,128)S(1)}, u32[]{:S(2)}, u32[]{:S(2)}) collective-permute-start(f32[64,1024]{1,0:T(8,128)S(1)} %get-tuple-element.50), channel_id=1, source_target_pairs={{0,4},{4,0},{8,12},{12,8},{16,20},{20,16},{24,28},{28,24},{1,5},{5... | collective-permute-start | bytes 786440 | tf_op jit(solution)/shard_map/ppermute | solution.py:288
  57.9 0.1 collective-permute-start.6
  58.0 1.1 collective-permute-done.5
  59.0 3.7 %collective-permute-done.4 = f32[64,1024]{1,0:T(8,128)S(1)} collective-permute-done((f32[64,1024]{1,0:T(8,128)S(1)}, f32[64,1024]{1,0:T(8,128)S(1)}, u32[]{:S(2)}, u32[]{:S(2)}) %collective-permute-start.4) | collective-permute-done | bytes 262176 | tf_op jit(solution)/shard_map/ppermute | solution.py:288
  62.7 2.8 %collective-permute-done.6 = bf16[64,1024]{1,0:T(8,128)(2,1)S(1)} collective-permute-done((bf16[64,1024]{1,0:T(8,128)(2,1)S(1)}, bf16[64,1024]{1,0:T(8,128)(2,1)S(1)}, u32[]{:S(2)}, u32[]{:S(2)}) %collective-permute-start.6) | collective-permute-done | bytes 131104 | tf_op jit(solution)/shard_map/ppermute | solution.py:293
  65.6 0.1 add_convert_fusion.refs_0_
  65.7 1.2 collective-permute-start.9
  66.9 1.6 %collective-permute-start.8 = (bf16[64,1024]{1,0:T(8,128)(2,1)S(1)}, bf16[64,1024]{1,0:T(8,128)(2,1)S(1)}, u32[]{:S(2)}, u32[]{:S(2)}) collective-permute-start(bf16[64,1024]{1,0:T(8,128)(2,1)S(1)} %add_convert_fusion.refs_0_), channel_id=1, source_target_pairs={{0,16},{4,20},{8,24},{12,28},{16,0},{20,4},{24,8},{28,12},{1,17},{... | collective-permute-start | bytes 393224 | tf_op jit(solution)/shard_map/ppermute | solution.py:293
  68.5 1.9 %collective-permute-start.7 = (bf16[64,1024]{1,0:T(8,128)(2,1)S(1)}, bf16[64,1024]{1,0:T(8,128)(2,1)S(1)}, u32[]{:S(2)}, u32[]{:S(2)}) collective-permute-start(bf16[64,1024]{1,0:T(8,128)(2,1)S(1)} %add_convert_fusion.refs_0_), channel_id=1, source_target_pairs={{0,8},{4,12},{8,16},{12,20},{16,24},{20,28},{24,0},{28,4},{1,9},{5... | collective-permute-start | bytes 393224 | tf_op jit(solution)/shard_map/ppermute | solution.py:293
  70.4 0.1 pad_add_fusion.8
  70.5 0.6 collective-permute-done.9.refs_3_
  71.1 1.5 %collective-permute-start.13 = (bf16[64,1024]{1,0:T(8,128)(2,1)S(1)}, bf16[64,1024]{1,0:T(8,128)(2,1)S(1)}, u32[]{:S(2)}, u32[]{:S(2)}) collective-permute-start(bf16[64,1024]{1,0:T(8,128)(2,1)S(1)} %collective-permute-done.9.refs_3_), channel_id=1, source_target_pairs={{0,4},{4,0},{8,12},{12,8},{16,20},{20,16},{24,28},{28,24},{1,5},{5... | collective-permute-start | bytes 393224 | tf_op jit(solution)/shard_map/ppermute | solution.py:288
  72.5 0.2 collective-permute-done.8.refs_2_
  72.8 3.9 %collective-permute-start.12 = (bf16[64,1024]{1,0:T(8,128)(2,1)S(1)}, bf16[64,1024]{1,0:T(8,128)(2,1)S(1)}, u32[]{:S(2)}, u32[]{:S(2)}) collective-permute-start(bf16[64,1024]{1,0:T(8,128)(2,1)S(1)} %collective-permute-done.8.refs_2_), channel_id=1, source_target_pairs={{0,4},{4,0},{8,12},{12,8},{16,20},{20,16},{24,28},{28,24},{1,5},{5... | collective-permute-start | bytes 393224 | tf_op jit(solution)/shard_map/ppermute | solution.py:288
  76.7 0.1 pad_add_fusion.7
  76.7 1.0 collective-permute-done.13.refs_7_
  77.7 1.8 %collective-permute-done.12.refs_6_ = bf16[64,1024]{1,0:T(8,128)(2,1)S(1)} collective-permute-done((bf16[64,1024]{1,0:T(8,128)(2,1)S(1)}, bf16[64,1024]{1,0:T(8,128)(2,1)S(1)}, u32[]{:S(2)}, u32[]{:S(2)}) %collective-permute-start.12) | collective-permute-done | bytes 131104 | tf_op jit(solution)/shard_map/ppermute | solution.py:288
  79.6 2.0 %collective-permute-done.11.refs_5_ = bf16[64,1024]{1,0:T(8,128)(2,1)S(1)} collective-permute-done((bf16[64,1024]{1,0:T(8,128)(2,1)S(1)}, bf16[64,1024]{1,0:T(8,128)(2,1)S(1)}, u32[]{:S(2)}, u32[]{:S(2)}) %collective-permute-start.11) | collective-permute-done | bytes 131104 | tf_op jit(solution)/shard_map/ppermute | solution.py:288
  81.6 5.3 %backward.4 = (f32[64,4096]{1,0:T(8,128)S(1)}, bf16[8,64,1024]{2,1,0:T(8,128)(2,1)S(1)}) custom-call(s32[128]{0:T(128)S(1)} %reshape.102.codes.refs_0_, s32[3]{0:T(128)S(1)} %get-tuple-element.72.where, bf16[129,256,512]{2,1,0:T(8,128)(2,1)} %get-tuple-element.48.jac.refs_2_, bf16[64,1024]{1,0:T(8,128)(2,1)S(1)} %add_convert_fusion.refs_0_, ...), custom_call_target="tpu_custom_call" | custom-call | flops 16 | bytes 64 | tf_op jit(solution)/shard_map/backward/pallas_call | solution.py:231
  86.9 0.1 collective-permute-start.14
  87.0 4.4 %backward.5 = f32[64,4096]{1,0:T(8,128)S(1)} custom-call(s32[128]{0:T(128)S(1)} %reshape.102.codes.refs_0_, s32[3]{0:T(128)S(1)} %get-tuple-element.73.refs_1_, bf16[129,256,512]{2,1,0:T(8,128)(2,1)} %get-tuple-element.48.jac.refs_2_, bf16[8,64,1024]{2,1,0:T(8,128)(2,1)S(1)} %get-tuple-element.57.refs_3_), custom_call_target="tpu_custom_call" | custom-call | flops 16 | bytes 64 | tf_op jit(solution)/shard_map/backward/pallas_call | solution.py:231
  91.4 0.1 fusion
  91.5 12.9 %collective-permute-start.16 = (bf16[64,4096]{1,0:T(8,128)(2,1)S(1)}, bf16[64,4096]{1,0:T(8,128)(2,1)S(1)}, u32[]{:S(2)}, u32[]{:S(2)}) collective-permute-start(bf16[64,4096]{1,0:T(8,128)(2,1)S(1)} %fusion), channel_id=1, source_target_pairs={{0,2},{1,3},{2,0},{3,1},{4,6},{5,7},{6,4},{7,5},{8,10},{9,11},{10,... | collective-permute-start | bytes 1572872 | tf_op jit(solution)/shard_map/ppermute | solution.py:288
  104.4 4.9 %backward.7 = f32[64,4096]{1,0:T(8,128)S(1)} custom-call(s32[128]{0:T(128)S(1)} %reshape.102.codes.refs_0_, s32[3]{0:T(128)S(1)} %get-tuple-element.63.refs_1_, bf16[129,256,512]{2,1,0:T(8,128)(2,1)} %get-tuple-element.48.jac.refs_2_, bf16[8,64,1024]{2,1,0:T(8,128)(2,1)S(1)} %get-tuple-element.57.refs_3_), custom_call_target="tpu_custom_call" | custom-call | flops 16 | bytes 64 | tf_op jit(solution)/shard_map/backward/pallas_call | solution.py:231
  109.3 0.1 collective-permute-start.15
  109.4 4.0 %backward.6 = f32[64,4096]{1,0:T(8,128)S(1)} custom-call(s32[128]{0:T(128)S(1)} %reshape.102.codes.refs_0_, s32[3]{0:T(128)S(1)} %get-tuple-element.71.refs_1_, bf16[129,256,512]{2,1,0:T(8,128)(2,1)} %get-tuple-element.48.jac.refs_2_, bf16[8,64,1024]{2,1,0:T(8,128)(2,1)S(1)} %get-tuple-element.57.refs_3_), custom_call_target="tpu_custom_call" | custom-call | flops 16 | bytes 64 | tf_op jit(solution)/shard_map/backward/pallas_call | solution.py:231
  113.4 2.1 %collective-permute-done.16 = bf16[64,4096]{1,0:T(8,128)(2,1)S(1)} collective-permute-done((bf16[64,4096]{1,0:T(8,128)(2,1)S(1)}, bf16[64,4096]{1,0:T(8,128)(2,1)S(1)}, u32[]{:S(2)}, u32[]{:S(2)}) %collective-permute-start.16) | collective-permute-done | bytes 524320 | tf_op jit(solution)/shard_map/ppermute | solution.py:288
  115.5 0.1 convert_add_fusion.refs_0_
  115.6 0.1 reduce-precision_convert_fusion.refs_1_
  115.8 0.1 collective-permute-start.17
  115.8 1.8 %collective-permute-start.18 = (bf16[64,4096]{1,0:T(8,128)(2,1)S(1)}, bf16[64,4096]{1,0:T(8,128)(2,1)S(1)}, u32[]{:S(2)}, u32[]{:S(2)}) collective-permute-start(bf16[64,4096]{1,0:T(8,128)(2,1)S(1)} %reduce-precision_convert_fusion.refs_1_), channel_id=1, source_target_pairs={{0,2},{1,3},{2,0},{3,1},{4,6},{5,7},{6,4},{7,5},{8,10},{9,11},{10,... | collective-permute-start | bytes 1572872 | tf_op jit(solution)/shard_map/ppermute | solution.py:288
  117.6 0.2 collective-permute-start.19
  117.8 12.4 %collective-permute-done.18.refs_2_ = bf16[64,4096]{1,0:T(8,128)(2,1)S(1)} collective-permute-done((bf16[64,4096]{1,0:T(8,128)(2,1)S(1)}, bf16[64,4096]{1,0:T(8,128)(2,1)S(1)}, u32[]{:S(2)}, u32[]{:S(2)}) %collective-permute-start.18) | collective-permute-done | bytes 524320 | tf_op jit(solution)/shard_map/ppermute | solution.py:288
  130.2 1.4 %place.2.refs_0_ = f32[64,16384]{1,0:T(8,128)} custom-call(s32[1]{0:T(128)} %bitcast.where, f32[64,4096]{1,0:T(8,128)S(1)} %convert_add_fusion.refs_0_, f32[64,4096]{1,0:T(8,128)S(1)} %collective-permute-done.17.refs_1_), custom_call_target="tpu_custom_call" | custom-call | tf_op jit(solution)/shard_map/place/pallas_call | solution.py:272
  131.6 0.5 collective-permute-done.20.refs_4_
  132.1 1.4 %place.3 = f32[64,16384]{1,0:T(8,128)} custom-call(s32[1]{0:T(128)} %bitcast.where, f32[64,16384]{1,0:T(8,128)} %place.2.refs_0_, bf16[64,4096]{1,0:T(8,128)(2,1)S(1)} %reduce-precision_convert_fusion.refs_1_, bf16[64,4096]{1,0:T(8,128)(2,1)S(1)} %collective-permute-done.18.refs_2_, ...), custom_call_target="tpu_custom_call", output_to_operand_aliasing={{}: (1, {})} | custom-call | tf_op jit(solution)/shard_map/place/pallas_call | solution.py:272
  (26 shorter events, 0.3 us)
Async XLA Ops:
  4.7 14.6 %all-to-all-start = ((bf16[8,8,1024]{2,1,0:T(8,128)(2,1)}), bf16[8,8,1024]{2,1,0:T(8,128)(2,1)S(1)}, u32[]{:S(2)}, u32[]{:S(2)}) async-start(bf16[8,8,1024]{2,1,0:T(8,128)(2,1)} %fusion.2), calls=%async_computation | async-start | bytes 262144 | tf_op jit(solution)/shard_map/all_to_all | solution.py:342
  19.4 1.6 %copy-start = (bf16[64,16384]{1,0:T(8,128)(2,1)S(1)}, bf16[64,16384]{1,0:T(8,128)(2,1)}, u32[]{:S(2)}) copy-start(bf16[64,16384]{1,0:T(8,128)(2,1)} %vectors.7) | copy-start | bytes 6291460
  28.9 10.9 %collective-permute-start = (f32[64,1024]{1,0:T(8,128)S(1)}, f32[64,1024]{1,0:T(8,128)S(1)}, u32[]{:S(2)}, u32[]{:S(2)}) collective-permute-start(f32[64,1024]{1,0:T(8,128)S(1)} %get-tuple-element.35), channel_id=1, source_target_pairs={{0,4},{4,0},{8,12},{12,8},{16,20},{20,16},{24,28},{28,24},{1,5},{5... | collective-permute-start | bytes 786440 | tf_op jit(solution)/shard_map/ppermute | solution.py:288
  29.8 1.6 %copy-start.1 = (bf16[64,16384]{1,0:T(8,128)(2,1)S(1)}, bf16[64,16384]{1,0:T(8,128)(2,1)}, u32[]{:S(2)}) copy-start(bf16[64,16384]{1,0:T(8,128)(2,1)} %vectors.7) | copy-start | bytes 6291460
  38.5 9.3 %collective-permute-start.1 = (f32[64,1024]{1,0:T(8,128)S(1)}, f32[64,1024]{1,0:T(8,128)S(1)}, u32[]{:S(2)}, u32[]{:S(2)}) collective-permute-start(f32[64,1024]{1,0:T(8,128)S(1)} %get-tuple-element.39), channel_id=1, source_target_pairs={{0,4},{4,0},{8,12},{12,8},{16,20},{20,16},{24,28},{28,24},{1,5},{5... | collective-permute-start | bytes 786440 | tf_op jit(solution)/shard_map/ppermute | solution.py:288
  39.8 8.1 %collective-permute-start.2 = (f32[64,1024]{1,0:T(8,128)S(1)}, f32[64,1024]{1,0:T(8,128)S(1)}, u32[]{:S(2)}, u32[]{:S(2)}) collective-permute-start(f32[64,1024]{1,0:T(8,128)S(1)} %add.124), channel_id=1, source_target_pairs={{0,24},{4,28},{8,0},{12,4},{16,8},{20,12},{24,16},{28,20},{1,25},{... | collective-permute-start | bytes 786440 | tf_op jit(solution)/shard_map/ppermute | solution.py:293
  47.7 10.1 %collective-permute-start.3 = (f32[64,1024]{1,0:T(8,128)S(1)}, f32[64,1024]{1,0:T(8,128)S(1)}, u32[]{:S(2)}, u32[]{:S(2)}) collective-permute-start(f32[64,1024]{1,0:T(8,128)S(1)} %get-tuple-element.44), channel_id=1, source_target_pairs={{0,4},{4,0},{8,12},{12,8},{16,20},{20,16},{24,28},{28,24},{1,5},{5... | collective-permute-start | bytes 786440 | tf_op jit(solution)/shard_map/ppermute | solution.py:288
  47.9 11.2 %collective-permute-start.5 = (f32[64,1024]{1,0:T(8,128)S(1)}, f32[64,1024]{1,0:T(8,128)S(1)}, u32[]{:S(2)}, u32[]{:S(2)}) collective-permute-start(f32[64,1024]{1,0:T(8,128)S(1)} %add.126), channel_id=1, source_target_pairs={{0,16},{4,20},{8,24},{12,28},{16,0},{20,4},{24,8},{28,12},{1,17},{... | collective-permute-start | bytes 786440 | tf_op jit(solution)/shard_map/ppermute | solution.py:293
  53.7 9.0 %collective-permute-start.4 = (f32[64,1024]{1,0:T(8,128)S(1)}, f32[64,1024]{1,0:T(8,128)S(1)}, u32[]{:S(2)}, u32[]{:S(2)}) collective-permute-start(f32[64,1024]{1,0:T(8,128)S(1)} %get-tuple-element.50), channel_id=1, source_target_pairs={{0,4},{4,0},{8,12},{12,8},{16,20},{20,16},{24,28},{28,24},{1,5},{5... | collective-permute-start | bytes 786440 | tf_op jit(solution)/shard_map/ppermute | solution.py:288
  57.9 7.7 %collective-permute-start.6 = (bf16[64,1024]{1,0:T(8,128)(2,1)S(1)}, bf16[64,1024]{1,0:T(8,128)(2,1)S(1)}, u32[]{:S(2)}, u32[]{:S(2)}) collective-permute-start(bf16[64,1024]{1,0:T(8,128)(2,1)S(1)} %add_convert_fusion.1), channel_id=1, source_target_pairs={{0,8},{4,12},{8,16},{12,20},{16,24},{20,28},{24,0},{28,4},{1,9},{5... | collective-permute-start | bytes 393224 | tf_op jit(solution)/shard_map/ppermute | solution.py:293
  65.7 5.4 %collective-permute-start.9 = (bf16[64,1024]{1,0:T(8,128)(2,1)S(1)}, bf16[64,1024]{1,0:T(8,128)(2,1)S(1)}, u32[]{:S(2)}, u32[]{:S(2)}) collective-permute-start(bf16[64,1024]{1,0:T(8,128)(2,1)S(1)} %add_convert_fusion.refs_0_), channel_id=1, source_target_pairs={{0,24},{4,28},{8,0},{12,4},{16,8},{20,12},{24,16},{28,20},{1,25},{... | collective-permute-start | bytes 393224 | tf_op jit(solution)/shard_map/ppermute | solution.py:293
  66.9 5.9 %collective-permute-start.8 = (bf16[64,1024]{1,0:T(8,128)(2,1)S(1)}, bf16[64,1024]{1,0:T(8,128)(2,1)S(1)}, u32[]{:S(2)}, u32[]{:S(2)}) collective-permute-start(bf16[64,1024]{1,0:T(8,128)(2,1)S(1)} %add_convert_fusion.refs_0_), channel_id=1, source_target_pairs={{0,16},{4,20},{8,24},{12,28},{16,0},{20,4},{24,8},{28,12},{1,17},{... | collective-permute-start | bytes 393224 | tf_op jit(solution)/shard_map/ppermute | solution.py:293
  68.5 8.1 %collective-permute-start.7 = (bf16[64,1024]{1,0:T(8,128)(2,1)S(1)}, bf16[64,1024]{1,0:T(8,128)(2,1)S(1)}, u32[]{:S(2)}, u32[]{:S(2)}) collective-permute-start(bf16[64,1024]{1,0:T(8,128)(2,1)S(1)} %add_convert_fusion.refs_0_), channel_id=1, source_target_pairs={{0,8},{4,12},{8,16},{12,20},{16,24},{20,28},{24,0},{28,4},{1,9},{5... | collective-permute-start | bytes 393224 | tf_op jit(solution)/shard_map/ppermute | solution.py:293
  70.5 6.2 %collective-permute-start.10 = (bf16[64,1024]{1,0:T(8,128)(2,1)S(1)}, bf16[64,1024]{1,0:T(8,128)(2,1)S(1)}, u32[]{:S(2)}, u32[]{:S(2)}) collective-permute-start(bf16[64,1024]{1,0:T(8,128)(2,1)S(1)} %add_convert_fusion.refs_0_), channel_id=1, source_target_pairs={{0,4},{4,0},{8,12},{12,8},{16,20},{20,16},{24,28},{28,24},{1,5},{5... | collective-permute-start | bytes 393224 | tf_op jit(solution)/shard_map/ppermute | solution.py:288
  71.1 6.7 %collective-permute-start.13 = (bf16[64,1024]{1,0:T(8,128)(2,1)S(1)}, bf16[64,1024]{1,0:T(8,128)(2,1)S(1)}, u32[]{:S(2)}, u32[]{:S(2)}) collective-permute-start(bf16[64,1024]{1,0:T(8,128)(2,1)S(1)} %collective-permute-done.9.refs_3_), channel_id=1, source_target_pairs={{0,4},{4,0},{8,12},{12,8},{16,20},{20,16},{24,28},{28,24},{1,5},{5... | collective-permute-start | bytes 393224 | tf_op jit(solution)/shard_map/ppermute | solution.py:288
  72.8 6.8 %collective-permute-start.12 = (bf16[64,1024]{1,0:T(8,128)(2,1)S(1)}, bf16[64,1024]{1,0:T(8,128)(2,1)S(1)}, u32[]{:S(2)}, u32[]{:S(2)}) collective-permute-start(bf16[64,1024]{1,0:T(8,128)(2,1)S(1)} %collective-permute-done.8.refs_2_), channel_id=1, source_target_pairs={{0,4},{4,0},{8,12},{12,8},{16,20},{20,16},{24,28},{28,24},{1,5},{5... | collective-permute-start | bytes 393224 | tf_op jit(solution)/shard_map/ppermute | solution.py:288
  76.6 5.0 %collective-permute-start.11 = (bf16[64,1024]{1,0:T(8,128)(2,1)S(1)}, bf16[64,1024]{1,0:T(8,128)(2,1)S(1)}, u32[]{:S(2)}, u32[]{:S(2)}) collective-permute-start(bf16[64,1024]{1,0:T(8,128)(2,1)S(1)} %collective-permute-done.7.refs_1_), channel_id=1, source_target_pairs={{0,4},{4,0},{8,12},{12,8},{16,20},{20,16},{24,28},{28,24},{1,5},{5... | collective-permute-start | bytes 393224 | tf_op jit(solution)/shard_map/ppermute | solution.py:288
  86.9 4.4 %collective-permute-start.14 = (f32[64,4096]{1,0:T(8,128)S(1)}, f32[64,4096]{1,0:T(8,128)S(1)}, u32[]{:S(2)}, u32[]{:S(2)}) collective-permute-start(f32[64,4096]{1,0:T(8,128)S(1)} %get-tuple-element.58), channel_id=1, source_target_pairs={{0,1},{1,0},{2,3},{3,2},{4,5},{5,4},{6,7},{7,6},{8,9},{9,8},{10,11... | collective-permute-start | bytes 3145736 | tf_op jit(solution)/shard_map/ppermute | solution.py:288
  91.5 24.0 %collective-permute-start.16 = (bf16[64,4096]{1,0:T(8,128)(2,1)S(1)}, bf16[64,4096]{1,0:T(8,128)(2,1)S(1)}, u32[]{:S(2)}, u32[]{:S(2)}) collective-permute-start(bf16[64,4096]{1,0:T(8,128)(2,1)S(1)} %fusion), channel_id=1, source_target_pairs={{0,2},{1,3},{2,0},{3,1},{4,6},{5,7},{6,4},{7,5},{8,10},{9,11},{10,... | collective-permute-start | bytes 1572872 | tf_op jit(solution)/shard_map/ppermute | solution.py:288
  109.3 6.3 %collective-permute-start.15 = (f32[64,4096]{1,0:T(8,128)S(1)}, f32[64,4096]{1,0:T(8,128)S(1)}, u32[]{:S(2)}, u32[]{:S(2)}) collective-permute-start(f32[64,4096]{1,0:T(8,128)S(1)} %backward.7), channel_id=1, source_target_pairs={{0,1},{1,0},{2,3},{3,2},{4,5},{5,4},{6,7},{7,6},{8,9},{9,8},{10,11... | collective-permute-start | bytes 3145736 | tf_op jit(solution)/shard_map/ppermute | solution.py:288
  115.8 14.4 %collective-permute-start.17 = (f32[64,4096]{1,0:T(8,128)S(1)}, f32[64,4096]{1,0:T(8,128)S(1)}, u32[]{:S(2)}, u32[]{:S(2)}) collective-permute-start(f32[64,4096]{1,0:T(8,128)S(1)} %convert_add_fusion.refs_0_), channel_id=1, source_target_pairs={{0,1},{1,0},{2,3},{3,2},{4,5},{5,4},{6,7},{7,6},{8,9},{9,8},{10,11... | collective-permute-start | bytes 3145736 | tf_op jit(solution)/shard_map/ppermute | solution.py:288
  115.8 14.3 %collective-permute-start.18 = (bf16[64,4096]{1,0:T(8,128)(2,1)S(1)}, bf16[64,4096]{1,0:T(8,128)(2,1)S(1)}, u32[]{:S(2)}, u32[]{:S(2)}) collective-permute-start(bf16[64,4096]{1,0:T(8,128)(2,1)S(1)} %reduce-precision_convert_fusion.refs_1_), channel_id=1, source_target_pairs={{0,2},{1,3},{2,0},{3,1},{4,6},{5,7},{6,4},{7,5},{8,10},{9,11},{10,... | collective-permute-start | bytes 1572872 | tf_op jit(solution)/shard_map/ppermute | solution.py:288
  117.6 14.0 %collective-permute-start.19 = (bf16[64,4096]{1,0:T(8,128)(2,1)S(1)}, bf16[64,4096]{1,0:T(8,128)(2,1)S(1)}, u32[]{:S(2)}, u32[]{:S(2)}) collective-permute-start(bf16[64,4096]{1,0:T(8,128)(2,1)S(1)} %reduce-precision_convert_fusion.refs_1_), channel_id=1, source_target_pairs={{0,1},{1,0},{2,3},{3,2},{4,5},{5,4},{6,7},{7,6},{8,9},{9,8},{10,11... | collective-permute-start | bytes 1572872 | tf_op jit(solution)/shard_map/ppermute | solution.py:288
  130.2 1.9 %collective-permute-start.20 = (bf16[64,4096]{1,0:T(8,128)(2,1)S(1)}, bf16[64,4096]{1,0:T(8,128)(2,1)S(1)}, u32[]{:S(2)}, u32[]{:S(2)}) collective-permute-start(bf16[64,4096]{1,0:T(8,128)(2,1)S(1)} %collective-permute-done.18.refs_2_), channel_id=1, source_target_pairs={{0,1},{1,0},{2,3},{3,2},{4,5},{5,4},{6,7},{7,6},{8,9},{9,8},{10,11... | collective-permute-start | bytes 1572872 | tf_op jit(solution)/shard_map/ppermute | solution.py:288
